TPU v7x, 512 devices: a whole 4x8x8 slice. The times are simulated.
512 devices in a mesh: fil: 128 (over x, y_hi, z), row: 4 (over y_lo, core).
Axes of the slice: x: 4, y: 8 (y_hi: 4, y_lo: 2; y = y_hi * 2 + y_lo), z: 8, core: 2. Of those that a mesh axis runs over, the one named last changes fastest.
Arguments:
- images: bfloat16 [1024, 2, 256, 128], P('fil', None, 'row'), may hold values from -6 to 6
- defocus: float32 [1024], P('fil'), may hold values from 0.5 to 2
- references: bfloat16 [128, 2, 256, 128], P('fil', None, 'row'), may hold values from -0.0234375 to 0.0234375
- offsets: int32 [1024, 32, 2], P('fil'), may hold values from -8 to 8
- posterior: int32 [1024, 32], P('fil'), may hold values from 0 to 255
- class_ids: int32 [1024], P('fil'), may hold values from 0 to 15
- seg_count: int32 [128], P('fil'), may hold values from 1 to 8, as said below
Outputs:
- scores: float32 [1024, 32, 128], P('fil', 'row')
- averages: float32 [16, 65536], P(None, ('row', 'fil'))
Inputs may be any that keep to these rules, and one draw needn't show every extreme that they name: `seg_count`: each filament has its segments in the first slots of its 8; some filament has exactly 8.
All inputs are finite; a program needn't handle non-finite values.
Results may differ from a plain program's by a relative error of at most 0.0029.
Values may be sent and summed in bfloat16 or wider, within the bound.
No kernel may reach another device: no remote copies, remote signals or barrier semaphores. Data moves between devices by JAX's collectives and lax.ppermute only.
A program may use at most 128 MiB of HBM per device.

v0:
```python
import math

import jax
import jax.numpy as jnp
from jax import lax
from jax.sharding import PartitionSpec as P

FROWS = 256
SHIFTS = 32
CLASSES = 16
SEG_FIL = 8


def wave_tables(shift_rows, shift_cols, row_freq, col_freq, box):
    row_angle = (shift_rows[..., None] * row_freq % box).astype(jnp.float32) * (
        -2.0 * math.pi / box
    )
    col_angle = (shift_cols[..., None] * col_freq % box).astype(jnp.float32) * (
        -2.0 * math.pi / box
    )
    row_cos = jnp.cos(row_angle)[..., :, None]
    row_sin = jnp.sin(row_angle)[..., :, None]
    col_cos = jnp.cos(col_angle)[..., None, :]
    col_sin = jnp.sin(col_angle)[..., None, :]
    phase_re = row_cos * col_cos - row_sin * col_sin
    phase_im = row_cos * col_sin + row_sin * col_cos
    return (phase_re, phase_im)


def contrast(defocus_vals, row_freq, col_freq, box):
    radius = (row_freq[:, None] * row_freq[:, None] + col_freq[None, :] * col_freq[None, :]).astype(
        jnp.float32
    ) / float(box * box)
    return -jnp.sin(200.0 * defocus_vals[:, None, None] * radius[None] + 0.1)


def aligned_rows(block_images, gain, block_offsets, row_freq, col_freq, box):
    phase_re, phase_im = wave_tables(
        block_offsets[..., 0], block_offsets[..., 1], row_freq, col_freq, box
    )
    scaled = gain[:, None]
    real_part = block_images[:, 0].astype(jnp.float32)[:, None]
    imag_part = block_images[:, 1].astype(jnp.float32)[:, None]
    aligned_re = scaled * (real_part * phase_re - imag_part * phase_im)
    aligned_im = scaled * (real_part * phase_im + imag_part * phase_re)
    stacked = jnp.stack([aligned_re, aligned_im], axis=3).astype(jnp.bfloat16)
    return stacked.reshape(stacked.shape[0] * stacked.shape[1], -1)


def correlate(aligned, panel):
    return lax.dot_general(
        aligned, panel, (((1,), (1,)), ((), ())), preferred_element_type=jnp.float32
    )


def per_device(images, defocus, references, offsets, posterior, class_ids, seg_count):
    seg_dev = images.shape[0]
    rows = images.shape[2]
    cols = images.shape[3]
    box = FROWS
    row_first = lax.axis_index("row") * rows
    row_freq = (row_first + jnp.arange(rows, dtype=jnp.int32) + box // 2) % box - box // 2
    col_freq = jnp.arange(cols, dtype=jnp.int32)
    live = (
        (jnp.arange(SEG_FIL, dtype=jnp.int32)[None, :] < seg_count[:, None])
        .reshape(-1)
        .astype(jnp.float32)
    )
    weight = live[:, None] * posterior.astype(jnp.float32) / 256.0
    local_panel = jnp.transpose(references, (0, 2, 1, 3)).reshape(references.shape[0], -1)
    classes = jnp.arange(CLASSES, dtype=jnp.int32)
    blocks = seg_dev // 8
    panel = lax.all_gather(local_panel, "fil", axis=0, tiled=True)

    def step(carry, inputs):
        numer, denom = carry
        block_images, block_defocus, block_offsets, block_weight, block_live, block_ids = inputs
        ctf = contrast(block_defocus, row_freq, col_freq, box)
        aligned = aligned_rows(
            block_images, ctf * block_live[:, None, None], block_offsets, row_freq, col_freq, box
        )
        block_scores = correlate(aligned, panel)
        member = (block_ids[None, :] == classes[:, None]).astype(jnp.float32)
        spread = (member[:, :, None] * block_weight[None]).astype(jnp.bfloat16).reshape(CLASSES, -1)
        numer = numer + jnp.dot(spread, aligned, preferred_element_type=jnp.float32)
        totals = member * jnp.sum(block_weight, axis=1)[None, :]
        denom = denom + jnp.dot(
            totals,
            (ctf * ctf).reshape(ctf.shape[0], -1),
            precision=lax.Precision.HIGHEST,
            preferred_element_type=jnp.float32,
        )
        return ((numer, denom), block_scores.reshape(8, SHIFTS, -1))

    inputs = (
        images.reshape(blocks, 8, 2, rows, cols),
        defocus.reshape(blocks, 8),
        offsets.reshape(blocks, 8, SHIFTS, 2),
        weight.reshape(blocks, 8, SHIFTS),
        live.reshape(blocks, 8),
        class_ids.reshape(blocks, 8),
    )
    start = (
        jnp.zeros((CLASSES, rows * 2 * cols), jnp.float32),
        jnp.zeros((CLASSES, rows * cols), jnp.float32),
    )
    (numer, denom), partial_scores = lax.scan(step, start, inputs)
    scores = lax.psum_scatter(
        partial_scores.reshape(seg_dev, SHIFTS, -1), "row", scatter_dimension=1, tiled=True
    )
    share = rows * 2 * cols // lax.axis_size("fil")
    total_numer, total_denom = lax.psum((numer, denom), "fil")
    wide = jnp.broadcast_to(
        total_denom.reshape(CLASSES, rows, 1, cols), (CLASSES, rows, 2, cols)
    ).reshape(CLASSES, -1)
    whole_avg = total_numer * lax.rsqrt(wide + 1.0)
    averages = lax.dynamic_slice_in_dim(whole_avg, lax.axis_index("fil") * share, share, 1)
    return (scores, averages)


def solution(mesh):
    placed = (
        P("fil", None, "row", None),
        P("fil"),
        P("fil", None, "row", None),
        P("fil", None, None),
        P("fil", None),
        P("fil"),
        P("fil"),
    )
    return jax.shard_map(
        per_device,
        mesh=mesh,
        in_specs=placed,
        out_specs=(P("fil", "row", None), P(None, ("row", "fil"))),
        check_vma=False,
    )
```

profile of v0, /device:TPU:1, one launch (start us, length us, event | category | flops | bytes accessed | tf_op | source)
XLA Modules:
  0.0 1596.1 jit_solution(9929572981778291256)
XLA Ops:
  7.2 0.0 all-gather.3.cloned.1.call-start
  7.2 0.8 copy.14
  8.0 0.6 reshape.286
  8.6 0.0 all-gather.3.cloned.1.call-update
  8.7 0.0 all-reduce.3.cloned.1.call-start
  9.4 0.7 broadcast_multiply_fusion
  10.1 0.8 fusion.37
  10.9 0.1 convert_multiply_fusion
  10.9 0.6 fusion.21
  11.5 0.6 fusion.23
  12.1 0.9 negate_multiply_fusion
  13.1 1.0 bitcast_convert_fusion.1
  14.1 6.8 subtract_multiply_fusion
  20.9 6.3 maximum_convert_fusion
  27.3 16.3 %copy.13 = bf16[8,32,64,2,128]{4,3,2,1,0:T(2,128)(2,1)} copy(bf16[8,32,64,2,128]{4,2,3,1,0:T(8,128)(2,1)} %maximum_convert_fusion) | data formatting | bytes 16777216 | tf_op jit(solution)/shard_map/while/body/eval_jaxpr/convert_element_type | solution.py:46
  43.6 0.0 copy-start
  43.6 0.0 copy-start.1
  43.6 14.5 convert_element_type.99
  58.1 0.0 copy-done
  58.1 0.2 fusion.36
  58.3 0.0 copy-done.1
  58.3 0.1 multiply_convert_fusion
  58.4 0.1 convert_element_type.98
  58.5 0.1 add.184
  58.6 2.3 fusion.3
  60.9 5.7 fusion.38
  66.5 0.0 all-reduce.3.cloned.1.call-update
  66.6 0.2 reduce-scatter.2.cloned.1.call-start
  66.8 14.6 convert_element_type.94
  81.4 90.7 %all-gather.3.cloned.1.call-done = bf16[128,1,16384]{2,1,0:T(2,128)(2,1)} async-done(((bf16[1,1,16384]{2,1,0:T(2,128)(2,1)}), bf16[128,1,16384]{2,1,0:T(2,128)(2,1)}) %all-gather.3.cloned.1.call-update) | async-done | bytes 4194320 | tf_op jit(solution)/shard_map/all_gather | solution.py:73
  172.0 12.0 fusion
  184.0 0.0 reduce-scatter.2.cloned.1.call-update
  184.0 1316.9 %all-reduce.3.cloned.1.call-done = (f32[16,8192]{1,0:T(8,128)}, f32[16,16384]{1,0:T(8,128)}) async-done(((f32[16,8192]{1,0:T(8,128)}, f32[16,16384]{1,0:T(8,128)}), (f32[16,8192]{1,0:T(8,128)}, f32[16,16384]{1,0:T(8,128)})) %all-reduce.3.cloned.1.call-update) | async-done | bytes 1572880 | tf_op jit(solution)/shard_map/psum | solution.py:112
  1501.0 1.1 rsqrt_bitcast_fusion
  1502.1 0.1 copy.17
  1502.2 0.4 broadcast_in_dim.21
  1502.6 0.8 rsqrt.12
  1503.4 1.3 dynamic-slice_multiply_fusion
  1504.7 84.8 %reduce-scatter.2.cloned.1.call-done = f32[8,8,128]{2,1,0:T(8,128)} async-done(((f32[8,32,128]{2,1,0:T(8,128)}), f32[8,8,128]{2,1,0:T(8,128)}) %reduce-scatter.2.cloned.1.call-update) | async-done | bytes 32784 | tf_op jit(solution)/shard_map/reduce_scatter | solution.py:108
  (5 shorter events, 0.0 us)
Async XLA Ops:
  7.2 164.9 %all-gather.3.cloned.1.call-start = ((), (), s32[]{:S(2)}) async-start(), calls=%async_computation.2 | async-start | bytes 8454144 | tf_op jit(solution)/shard_map/all_gather | solution.py:73
  8.7 1492.3 %all-reduce.3.cloned.1.call-start = ((), (), s32[]{:S(2)}) async-start(), calls=%async_computation.3 | async-start | bytes 3145728 | tf_op jit(solution)/shard_map/psum | solution.py:112
  43.6 14.5 copy-start
  43.6 14.7 copy-start.1
  66.6 1523.0 %reduce-scatter.2.cloned.1.call-start = ((), (), s32[]{:S(2)}) async-start(), calls=%async_computation.1 | async-start | bytes 163840 | tf_op jit(solution)/shard_map/reduce_scatter | solution.py:108
Sparse Core Ops, SparseCore 0:
  12.5 159.4 all-gather.2
  175.0 1325.9 all-reduce.2
  1504.5 84.9 reduce-scatter.1
where the time goes:
time: 1600 us
  waiting for transfers between devices  1490 us (93%)
  local copies, waits for them, and re-layouts  49.1 us (3%)
  matrix products  19.9 us (1%)
  other arithmetic  19.8 us (1%)
    psum x1, waiting for transfers between devices, per_device(): total_numer, total_denom = lax.psum((numer, denom), 'fil')  1320 us
    all_gather x1, waiting for transfers between devices, per_device(): panel = lax.all_gather(local_panel, 'fil', axis=0, tiled=True)  90.7 us
    reduce_scatter x1, waiting for transfers between devices, per_device(): lax.psum_scatter(partial_scores.reshape(seg_dev, SHIFTS, -1), 'row', scat...  84.8 us
    convert_element_type x3, local copies, waits for them, and re-layouts, aligned_rows(): stacked = jnp.stack([aligned_re, aligned_im], axis=3).astype(jnp.bfloat16)  45.4 us
  transfers between devices with their start and end apart: 3, of which 3 were waited for; matrix products, arithmetic and copies ran while one was open for 5% of the time, Pallas kernels for 0%

commit v1 on v0

v1 whole, which is shorter than its diff:
```python
import math

import jax
import jax.numpy as jnp
from jax import lax
from jax.experimental import pallas as pl
from jax.experimental.pallas import tpu as pltpu
from jax.sharding import Mesh
from jax.sharding import PartitionSpec as P

BOX = 256
SHIFTS = 32
CLASSES = 16
SEG = 8
NX = 4
NYZ = 32
KY = 16
COLS = 128
META = 16
FIL = ("x", "yh", "z")
ROW = ("yl", "core")
bf16 = jnp.bfloat16
f32 = jnp.float32


def small_sincos(theta):
    t2 = theta * theta
    sin = theta * (1.0 + t2 * (-1.0 / 6 + t2 * (1.0 / 120 + t2 * (-1.0 / 5040 + t2 * (1.0 / 362880)))))
    cos = 1.0 + t2 * (-0.5 + t2 * (1.0 / 24 + t2 * (-1.0 / 720 + t2 * (1.0 / 40320 + t2 * (-1.0 / 3628800)))))
    return sin, cos


def turn(m):
    n = jnp.floor(m * (1.0 / 64) + 0.5)
    sin, cos = small_sincos((m - 64.0 * n) * (math.pi / 128))
    quad = n - 4.0 * jnp.floor(n * 0.25)
    odd = (quad == 1.0) | (quad == 3.0)
    c = jnp.where(odd, sin, cos)
    s = jnp.where(odd, cos, sin)
    c = jnp.where((quad == 1.0) | (quad == 2.0), -c, c)
    s = jnp.where(quad >= 2.0, s, -s)
    return c, s


def align_kernel(kw_ref, img_ref, meta_ref, gain_ref, spread_ref, aligned_ref, numer_ref, x_ref):
    step = pl.program_id(0)
    kw0 = kw_ref[0].astype(f32)
    lane = lax.broadcasted_iota(jnp.int32, (SHIFTS, COLS), 1)
    sub = lax.broadcasted_iota(jnp.int32, (SHIFTS, COLS), 0)
    kx = lane.astype(f32)

    @pl.when(step == 0)
    def _():
        numer_ref[...] = jnp.zeros_like(numer_ref)

    def segment(i, carry):
        row = meta_ref[pl.ds(i, 1), :]
        wide = jnp.broadcast_to(row, (SHIFTS, COLS))
        sy = jnp.sum(jnp.where(lane == sub, wide, 0.0), axis=1, keepdims=True)
        sx = jnp.sum(jnp.where(lane == sub + SHIFTS, wide, 0.0), axis=1, keepdims=True)
        sy = jnp.broadcast_to(sy, (SHIFTS, COLS))
        pr, pi = turn(sy * kw0 + sx * kx)
        si, cr = small_sincos(sy * (-2.0 * math.pi / BOX))
        base = pl.multiple_of(i * 2 * KY, 2 * KY)
        img = img_ref[0, pl.ds(base, 2 * KY), :].astype(f32)
        gain = gain_ref[i]
        x_ref[0:KY, :] = img[0:KY] * gain
        x_ref[KY : 2 * KY, :] = img[KY : 2 * KY] * gain
        rows = pl.ds(pl.multiple_of(i * SHIFTS, SHIFTS), SHIFTS)
        for ky in range(KY):
            xr = x_ref[ky : ky + 1, :]
            xi = x_ref[KY + ky : KY + ky + 1, :]
            aligned_ref[rows, 2 * ky * COLS : (2 * ky + 1) * COLS] = (xr * pr - xi * pi).astype(bf16)
            aligned_ref[rows, (2 * ky + 1) * COLS : (2 * ky + 2) * COLS] = (xr * pi + xi * pr).astype(bf16)
            if ky < KY - 1:
                pr, pi = pr * cr - pi * si, pr * si + pi * cr
        return carry

    lax.fori_loop(0, SEG, segment, 0)
    part = jnp.dot(spread_ref[...], aligned_ref[...], preferred_element_type=f32)
    for d in range(2 * KY):
        numer_ref[d] += part[:, d * COLS : (d + 1) * COLS]


def align(kw0, recv, meta, gain, spread):
    segs = NX * SEG
    return pl.pallas_call(
        align_kernel,
        grid=(NX,),
        in_specs=[
            pl.BlockSpec(memory_space=pltpu.SMEM),
            pl.BlockSpec((1, SEG * 2 * KY, COLS), lambda j: (j, 0, 0)),
            pl.BlockSpec((SEG, COLS), lambda j: (j, 0)),
            pl.BlockSpec((SEG, KY, COLS), lambda j: (j, 0, 0)),
            pl.BlockSpec((CLASSES, SEG * SHIFTS), lambda j: (0, j)),
        ],
        out_specs=[
            pl.BlockSpec((SEG * SHIFTS, 2 * KY * COLS), lambda j: (j, 0)),
            pl.BlockSpec((2 * KY, CLASSES, COLS), lambda j: (0, 0, 0)),
        ],
        out_shape=[
            jax.ShapeDtypeStruct((segs * SHIFTS, 2 * KY * COLS), bf16),
            jax.ShapeDtypeStruct((2 * KY, CLASSES, COLS), f32),
        ],
        scratch_shapes=[pltpu.VMEM((2 * KY, COLS), f32)],
        compiler_params=pltpu.CompilerParams(vmem_limit_bytes=32 << 20),
        cost_estimate=pl.CostEstimate(flops=600_000_000, bytes_accessed=9_000_000, transcendentals=0),
        name="align",
    )(kw0, recv, meta, gain, spread)


def score_kernel(panel_ref, aligned_ref, out_ref, wide_ref, packed_ref):
    step = pl.program_id(0)
    rows = NX * 2 * KY

    @pl.when(step == 0)
    def _():
        def widen(j, carry):
            wide_ref[pl.ds(pl.multiple_of(j * rows, rows), rows), :] = panel_ref[j, 0:rows, :].astype(f32)
            return carry

        lax.fori_loop(0, NYZ, widen, 0)
        for d in range(2 * KY):
            parts = [wide_ref[pl.ds(x * 2 * KY + d, NYZ, stride=rows), :] for x in range(NX)]
            packed_ref[:, d * COLS : (d + 1) * COLS] = jnp.concatenate(parts, axis=0).astype(bf16)

    res = lax.dot_general(
        aligned_ref[...], packed_ref[...], (((1,), (1,)), ((), ())), preferred_element_type=f32
    )
    for i in range(SEG):
        for r in range(4):
            out_ref[0, r, i] = res[i * SHIFTS + r * 8 : i * SHIFTS + (r + 1) * 8, :]


def score(panel, aligned):
    refs = NX * NYZ
    return pl.pallas_call(
        score_kernel,
        grid=(NX,),
        in_specs=[
            pl.BlockSpec(panel.shape, lambda j: (0, 0, 0)),
            pl.BlockSpec((SEG * SHIFTS, 2 * KY * COLS), lambda j: (j, 0)),
        ],
        out_specs=pl.BlockSpec((1, 4, SEG, 8, refs), lambda j: (j, 0, 0, 0, 0)),
        out_shape=jax.ShapeDtypeStruct((NX, 4, SEG, 8, refs), f32),
        scratch_shapes=[
            pltpu.VMEM((NYZ * NX * 2 * KY, COLS), f32),
            pltpu.VMEM((refs, 2 * KY * COLS), bf16),
        ],
        compiler_params=pltpu.CompilerParams(vmem_limit_bytes=32 << 20),
        cost_estimate=pl.CostEstimate(flops=1_100_000_000, bytes_accessed=10_000_000, transcendentals=0),
        name="score",
    )(panel, aligned)


def three_parts(v):
    hi = lax.reduce_precision(v, 8, 7)
    rest = v - hi
    mid = lax.reduce_precision(rest, 8, 7)
    return hi, mid, rest - mid


def contrast(defocus, kw, kx):
    radius = (kw * kw + kx * kx).astype(f32) / float(BOX * BOX)
    return -jnp.sin(200.0 * defocus * radius + 0.1)


def per_device(images, defocus, references, offsets, posterior, class_ids, seg_count):
    row = lax.axis_index(ROW)
    my_x = lax.axis_index("x")
    fil = lax.axis_index(FIL)
    kx = jnp.arange(COLS, dtype=jnp.int32)

    live = (jnp.arange(SEG, dtype=jnp.int32) < seg_count[0]).astype(f32)
    weights = live[:, None] * posterior.astype(f32)
    scalars = jnp.stack([*three_parts(defocus), class_ids.astype(f32), live], axis=1)
    meta = jnp.concatenate(
        [offsets[:, :, 0].astype(f32), offsets[:, :, 1].astype(f32), weights, scalars], axis=1
    )
    meta = jnp.pad(meta, ((0, META - SEG), (0, COLS - meta.shape[1]))).astype(bf16)
    send = jnp.concatenate(
        [
            images.reshape(SEG, 2, NX, KY, COLS).transpose(2, 0, 1, 3, 4).reshape(NX, SEG * 2 * KY, COLS),
            references.reshape(2, NX, KY, COLS).transpose(1, 2, 0, 3).reshape(NX, 2 * KY, COLS),
            jnp.broadcast_to(meta[None], (NX, META, COLS)),
        ],
        axis=1,
    )
    recv = lax.all_to_all(send, "x", 0, 0, tiled=True)
    img_rows = SEG * 2 * KY
    own_refs = recv[:, img_rows : img_rows + 2 * KY]
    meta = recv[:, img_rows + 2 * KY : img_rows + 2 * KY + SEG].reshape(NX * SEG, COLS).astype(f32)
    weights = meta[:, 2 * SHIFTS : 3 * SHIFTS]
    own_defocus = meta[:, 96] + meta[:, 97] + meta[:, 98]
    own_class = meta[:, 99]
    own_live = meta[:, 100]

    ky_first = row * 64 + my_x * KY
    kw_first = (ky_first + BOX // 2) % BOX - BOX // 2
    kw = kw_first + jnp.arange(KY, dtype=jnp.int32)
    gain = contrast(own_defocus[:, None, None], kw[:, None], kx[None, :]) * own_live[:, None, None]
    classes = jnp.arange(CLASSES, dtype=f32)
    member = (own_class[None, :] == classes[:, None]).astype(f32)
    spread = (member[:, :, None] * (weights * (1.0 / 256))[None]).astype(bf16).reshape(CLASSES, -1)

    total = jnp.sum(weights, axis=1)
    total_hi = jnp.floor(total * (1.0 / 32))
    facts = jnp.stack(
        [meta[:, 96], meta[:, 97], meta[:, 98], total_hi, total - 32.0 * total_hi, own_class], axis=0
    )
    facts = jnp.pad(facts, ((0, META - 6), (0, COLS - NX * SEG))).astype(bf16)
    chunk = jnp.concatenate([own_refs.reshape(NX * 2 * KY, COLS), facts], axis=0)
    panel = lax.all_to_all(
        lax.optimization_barrier(jnp.broadcast_to(chunk[None], (NYZ, *chunk.shape))),
        ("yh", "z"), 0, 0, tiled=True,
    )

    aligned, numer = align(kw_first.reshape(1), recv, meta, gain, spread)
    partial = score(panel, aligned)
    partial = lax.all_to_all(partial.reshape(16, SEG * 8, COLS), ("x", *ROW), 0, 0, tiled=True)
    scores = jnp.sum(partial, axis=0).reshape(SEG, 8, COLS)

    numer = lax.all_to_all(numer, ("yh", "z"), 0, 0, tiled=True)
    numer = jnp.sum(numer, axis=0)

    facts = panel[:, NX * 2 * KY : NX * 2 * KY + 6, : NX * SEG].astype(f32)
    all_defocus = (facts[:, 0] + facts[:, 1] + facts[:, 2]).reshape(-1)
    all_total = ((facts[:, 3] * 32.0 + facts[:, 4]) * (1.0 / 256)).reshape(-1)
    all_class = facts[:, 5].reshape(-1)
    ky_mine = row * 64 + fil // 2
    kw_mine = (ky_mine + BOX // 2) % BOX - BOX // 2
    ctf = contrast(all_defocus[:, None], kw_mine, kx[None, :])
    totals = jnp.where(all_class[None, :] == classes[:, None], all_total[None, :], 0.0)
    denom = jnp.dot(totals, ctf * ctf, precision=lax.Precision.HIGHEST, preferred_element_type=f32)
    averages = numer * lax.rsqrt(denom + 1.0)
    return scores, averages


def solution(mesh):
    fine = Mesh(mesh.devices.reshape(4, 4, 8, 2, 2), (*FIL, *ROW))
    placed = (
        P(FIL, None, ROW, None),
        P(FIL),
        P(FIL, None, ROW, None),
        P(FIL, None, None),
        P(FIL, None),
        P(FIL),
        P(FIL),
    )
    return jax.shard_map(
        per_device,
        mesh=fine,
        in_specs=placed,
        out_specs=(P(FIL, ROW, None), P(None, (*ROW, *FIL))),
        check_vma=False,
    )
```

time: 1600 us -> 105 us (0.07)
  waiting for transfers between devices: 1490 us -> 27.8 us
  local copies, waits for them, and re-layouts: 49.1 us -> 11.7 us
  starting transfers between devices: 0.3 us -> 29.9 us
  matrix products: 19.9 us -> 2.83 us
    psum x1 -> x0, waiting for transfers between devices: 1320 us -> none  [per_device(): total_numer, total_denom = lax.psum((numer, denom), 'fil')]
    all_gather x1 -> x0, waiting for transfers between devices: 90.7 us -> none  [per_device(): panel = lax.all_gather(local_panel, 'fil', axis=0, tiled=True)]
    reduce_scatter x1 -> x0, waiting for transfers between devices: 84.8 us -> none  [per_device(): lax.psum_scatter(partial_scores.reshape(seg_dev, SHIFTS, -1), 'row', scat...]
    convert_element_type x4 -> x0, local copies, waits for them, and re-layouts: 45.5 us -> none  [the longest x3 45.4 us: aligned_rows(): stacked = jnp.stack([aligned_re, aligned_im], axis=3).astype(jnp.bfloat16)]
    all_to_all x0 -> x3, starting transfers between devices: none -> 29.9 us  [the longest x1 15.9 us: per_device(): lax.all_to_all(lax.optimization_barrier(jnp.broadcast_to(chunk[None], (NY...]
    all_to_all x0 -> x3, waiting for transfers between devices: none -> 27.8 us  [the longest x1 17.4 us: per_device(): lax.all_to_all(lax.optimization_barrier(jnp.broadcast_to(chunk[None], (NY...]
    dot_general x3 -> x1, matrix products: 19.9 us -> 2.83 us  [per_device(): jnp.dot(totals, ctf * ctf, precision=lax.Precision.HIGHEST, preferred_ele...]
  transfers between devices with their start and end apart: 3 -> 3, of which waited for: 3 -> 3; matrix products, arithmetic and copies ran while one was open for 5% -> 5% of each run, Pallas kernels for 0% -> 15%
where the time goes in v1:
time: 105 us; the launch traced here: 104 us
  starting transfers between devices  29.9 us (28%)
  waiting for transfers between devices  27.8 us (26%)
  Pallas kernels  15.3 us (15%)
  local copies, waits for them, and re-layouts  11.7 us (11%)
  blocking collectives  10.4 us (10%)
  other arithmetic  4.56 us (4%)
  matrix products  2.83 us (3%)
  between operations  1.45 us (1%)
    all_to_all x1, waiting for transfers between devices, per_device(): lax.all_to_all(lax.optimization_barrier(jnp.broadcast_to(chunk[None], (NY...  17.4 us
    all_to_all x1, starting transfers between devices, per_device(): lax.all_to_all(lax.optimization_barrier(jnp.broadcast_to(chunk[None], (NY...  15.9 us
    all_to_all x1, blocking collectives, per_device(): recv = lax.all_to_all(send, 'x', 0, 0, tiled=True)  10.4 us
    pallas_call x1, Pallas kernels, align(): pl.pallas_call(align_kernel, grid=(NX,), in_specs=[pl.BlockSpec(memory_sp...  9.88 us
    all_to_all x1, starting transfers between devices, per_device(): numer = lax.all_to_all(numer, ('yh', 'z'), 0, 0, tiled=True)  8.15 us
    unnamed x4, local copies, waits for them, and re-layouts  6.6 us
    all_to_all x1, waiting for transfers between devices, per_device(): lax.all_to_all(partial.reshape(16, SEG * 8, COLS), ('x', *ROW), 0, 0, til...  6.57 us
    all_to_all x1, starting transfers between devices, per_device(): lax.all_to_all(partial.reshape(16, SEG * 8, COLS), ('x', *ROW), 0, 0, til...  5.86 us
  transfers between devices with their start and end apart: 3, of which 3 were waited for; matrix products, arithmetic and copies ran while one was open for 5% of the time, Pallas kernels for 15%

profile of v1, /device:TPU:1, one launch (start us, length us, event | category | flops | bytes accessed | tf_op | source)
XLA Modules:
  0.0 104.0 jit_solution(3365969907614724538)
XLA Ops:
  0.6 0.8 fusion.36
  2.1 0.7 fusion.30
  2.7 0.1 copy.21
  2.8 0.1 copy.22
  2.9 0.1 copy.23
  3.0 0.7 convert_bitcast_fusion
  3.7 0.1 copy.24
  3.8 0.8 copy.18
  4.6 1.0 copy.17
  5.6 0.8 multiply_convert_fusion.1
  6.3 0.1 concatenate.10
  6.5 10.4 %all_to_all.20.img_ref = bf16[4,304,128]{2,1,0:T(8,128)(2,1)S(1)} all-to-all(bf16[4,304,128]{2,1,0:T(8,128)(2,1)S(1)} %pad_maximum_fusion), channel_id=1, replica_groups=mesh['x'=4,'yh'=4,'z'=8,'yl'=2,'core'=2] {'x'}, dimensions={0} | all-to-all | bytes 622592 | tf_op jit(solution)/shard_map/all_to_all | solution.py:189
  16.9 0.2 fusion.22
  17.1 0.2 slice_multiply_fusion.1
  17.4 1.3 %broadcast_in_dim.13 = bf16[32,144,128]{2,1,0:T(8,128)(2,1)} broadcast(bf16[144,128]{1,0:T(8,128)(2,1)S(1)} %fusion.11), dimensions={1,2} | broadcast | bytes 1216512 | tf_op jit(solution)/shard_map/broadcast_in_dim | solution.py:214
  18.6 15.9 %all-to-all-start.1 = ((bf16[32,144,128]{2,1,0:T(8,128)(2,1)}), bf16[32,144,128]{2,1,0:T(8,128)(2,1)S(1)}, u32[]{:S(2)}, u32[]{:S(2)}) async-start(bf16[32,144,128]{2,1,0:T(8,128)(2,1)} %broadcast_in_dim.13), calls=%async_computation.1 | async-start | bytes 2359296 | tf_op jit(solution)/shard_map/all_to_all | solution.py:213
  34.6 0.1 convert_multiply_fusion
  34.7 0.2 slice_reduce_fusion.2
  34.9 0.1 mul.211
  35.0 0.1 mul.212
  35.2 0.1 mul.214
  35.3 1.0 negate_multiply_fusion.gain_ref
  36.3 9.9 %align.1 = (bf16[1024,4096]{1,0:T(8,128)(2,1)S(1)}, f32[32,16,128]{2,1,0:T(8,128)}) custom-call(s32[1]{0:T(128)} %bitcast.17.kw_ref, bf16[4,304,128]{2,1,0:T(8,128)(2,1)S(1)} %all_to_all.20.img_ref, f32[32,128]{1,0:T(8,128)S(1)} %fusion.23.meta_ref, f32[32,16,128]{2,1,0:T(8,128)S(1)} %negate_multiply_fusion.gain_ref, ...), custom_call_target="tpu_custom_call" | custom-call | flops 600000000 | bytes 9000000 | tf_op jit(solution)/shard_map/align/pallas_call | solution.py:87
  46.2 0.0 copy-start
  46.2 3.2 %copy-done = bf16[1024,4096]{1,0:T(8,128)(2,1)} copy-done((bf16[1024,4096]{1,0:T(8,128)(2,1)}, bf16[1024,4096]{1,0:T(8,128)(2,1)S(1)}, u32[]{:S(2)}) %copy-start) | copy-done | bytes 8388632
  49.4 17.4 %all-to-all-done.1.panel_ref = bf16[32,144,128]{2,1,0:T(8,128)(2,1)S(1)} async-done(((bf16[32,144,128]{2,1,0:T(8,128)(2,1)}), bf16[32,144,128]{2,1,0:T(8,128)(2,1)S(1)}, u32[]{:S(2)}, u32[]{:S(2)}) %all-to-all-start.1) | async-done | bytes 1179680 | tf_op jit(solution)/shard_map/all_to_all | solution.py:213
  66.8 8.2 %all-to-all-start.3 = ((f32[32,16,128]{2,1,0:T(8,128)}), f32[32,16,128]{2,1,0:T(8,128)S(1)}, u32[]{:S(2)}, u32[]{:S(2)}) async-start(f32[32,16,128]{2,1,0:T(8,128)} %get-tuple-element.5), calls=%async_computation.3 | async-start | bytes 524288 | tf_op jit(solution)/shard_map/all_to_all | solution.py:223
  74.9 0.0 copy-start.1
  74.9 3.4 %copy-done.1 = bf16[1024,4096]{1,0:T(8,128)(2,1)S(1)} copy-done((bf16[1024,4096]{1,0:T(8,128)(2,1)S(1)}, bf16[1024,4096]{1,0:T(8,128)(2,1)}, u32[]{:S(2)}) %copy-start.1) | copy-done | bytes 8388632
  78.3 5.4 %score.1 = f32[4,4,8,8,128]{4,3,2,1,0:T(8,128)} custom-call(bf16[32,144,128]{2,1,0:T(8,128)(2,1)S(1)} %all-to-all-done.1.panel_ref, bf16[1024,4096]{1,0:T(8,128)(2,1)S(1)} %copy-done.1), custom_call_target="tpu_custom_call" | custom-call | flops 1100000000 | bytes 10000000 | tf_op jit(solution)/shard_map/score/pallas_call | solution.py:137
  83.7 3.9 %all-to-all-done.3 = f32[32,16,128]{2,1,0:T(8,128)S(1)} async-done(((f32[32,16,128]{2,1,0:T(8,128)}), f32[32,16,128]{2,1,0:T(8,128)S(1)}, u32[]{:S(2)}, u32[]{:S(2)}) %all-to-all-start.3) | async-done | bytes 262176 | tf_op jit(solution)/shard_map/all_to_all | solution.py:223
  87.6 5.9 %all-to-all-start.2 = ((f32[16,64,128]{2,1,0:T(8,128)}), f32[16,64,128]{2,1,0:T(8,128)S(1)}, u32[]{:S(2)}, u32[]{:S(2)}) async-start(f32[16,64,128]{2,1,0:T(8,128)} %bitcast.18), calls=%async_computation.2 | async-start | bytes 1048576 | tf_op jit(solution)/shard_map/all_to_all | solution.py:220
  93.5 0.2 slice_reduce_fusion
  93.7 0.1 mul.223
  93.8 0.1 mul.220
  93.9 0.1 eq.41
  93.9 2.8 %fusion.1 = f32[16,128]{1,0:T(8,128)} fusion(f32[16,128]{1,0:T(8,128)S(1)} %reduce_sum.32, f32[128]{0:T(128)S(1)} %convert_multiply_fusion.1, f32[1024]{0:T(1024)S(1)} %mul.223, f32[1024]{0:T(1024)S(1)} %mul.220, f32[1024]{0:T(1024)S(1)} %eq.41), kind=kOutput, calls=%fused_computation.2 | convolution fusion | flops 25595904 | bytes 29184 | tf_op jit(solution)/shard_map/dot_general | solution.py:234
  96.8 6.6 %all-to-all-done.2 = f32[16,64,128]{2,1,0:T(8,128)S(1)} async-done(((f32[16,64,128]{2,1,0:T(8,128)}), f32[16,64,128]{2,1,0:T(8,128)S(1)}, u32[]{:S(2)}, u32[]{:S(2)}) %all-to-all-start.2) | async-done | bytes 524320 | tf_op jit(solution)/shard_map/all_to_all | solution.py:220
  103.3 0.6 reduce_sum.31
  (18 shorter events, 0.2 us)
Async XLA Ops:
  18.6 48.1 %all-to-all-start.1 = ((bf16[32,144,128]{2,1,0:T(8,128)(2,1)}), bf16[32,144,128]{2,1,0:T(8,128)(2,1)S(1)}, u32[]{:S(2)}, u32[]{:S(2)}) async-start(bf16[32,144,128]{2,1,0:T(8,128)(2,1)} %broadcast_in_dim.13), calls=%async_computation.1 | async-start | bytes 2359296 | tf_op jit(solution)/shard_map/all_to_all | solution.py:213
  46.2 3.2 %copy-start = (bf16[1024,4096]{1,0:T(8,128)(2,1)}, bf16[1024,4096]{1,0:T(8,128)(2,1)S(1)}, u32[]{:S(2)}) copy-start(bf16[1024,4096]{1,0:T(8,128)(2,1)S(1)} %get-tuple-element.4.aligned_ref) | copy-start | bytes 25165828
  66.8 20.8 %all-to-all-start.3 = ((f32[32,16,128]{2,1,0:T(8,128)}), f32[32,16,128]{2,1,0:T(8,128)S(1)}, u32[]{:S(2)}, u32[]{:S(2)}) async-start(f32[32,16,128]{2,1,0:T(8,128)} %get-tuple-element.5), calls=%async_computation.3 | async-start | bytes 524288 | tf_op jit(solution)/shard_map/all_to_all | solution.py:223
  74.9 3.4 %copy-start.1 = (bf16[1024,4096]{1,0:T(8,128)(2,1)S(1)}, bf16[1024,4096]{1,0:T(8,128)(2,1)}, u32[]{:S(2)}) copy-start(bf16[1024,4096]{1,0:T(8,128)(2,1)} %copy-done) | copy-start | bytes 25165828
  87.6 15.7 %all-to-all-start.2 = ((f32[16,64,128]{2,1,0:T(8,128)}), f32[16,64,128]{2,1,0:T(8,128)S(1)}, u32[]{:S(2)}, u32[]{:S(2)}) async-start(f32[16,64,128]{2,1,0:T(8,128)} %bitcast.18), calls=%async_computation.2 | async-start | bytes 1048576 | tf_op jit(solution)/shard_map/all_to_all | solution.py:220

commit v2 on v1

v2 whole, which is shorter than its diff:
```python
import math

import jax
import jax.numpy as jnp
from jax import lax
from jax.experimental import pallas as pl
from jax.experimental.pallas import tpu as pltpu
from jax.sharding import Mesh
from jax.sharding import PartitionSpec as P

BOX = 256
SHIFTS = 32
CLASSES = 16
SEG = 8
NA = 8
NB = 16
NROW = 4
KY = 8
D = 2 * KY
COLS = 128
META = 16
FIL = ("x", "yh", "zh", "zl")
ROW = ("yl", "core")
bf16 = jnp.bfloat16
f32 = jnp.float32
PARTIAL = f32


def small_sincos(theta):
    t2 = theta * theta
    sin = theta * (1.0 + t2 * (-1.0 / 6 + t2 * (1.0 / 120 + t2 * (-1.0 / 5040 + t2 * (1.0 / 362880)))))
    cos = 1.0 + t2 * (-0.5 + t2 * (1.0 / 24 + t2 * (-1.0 / 720 + t2 * (1.0 / 40320 + t2 * (-1.0 / 3628800)))))
    return sin, cos


def turn(m):
    n = jnp.floor(m * (1.0 / 64) + 0.5)
    sin, cos = small_sincos((m - 64.0 * n) * (math.pi / 128))
    quad = n - 4.0 * jnp.floor(n * 0.25)
    odd = (quad == 1.0) | (quad == 3.0)
    c = jnp.where(odd, sin, cos)
    s = jnp.where(odd, cos, sin)
    c = jnp.where((quad == 1.0) | (quad == 2.0), -c, c)
    s = jnp.where(quad >= 2.0, s, -s)
    return c, s


def parts_of(v):
    hi = v.astype(bf16).astype(f32)
    rest = v - hi
    mid = rest.astype(bf16).astype(f32)
    return hi, mid, rest - mid


def pack_kernel(defocus_ref, class_ref, count_ref, img_ref, ref_ref, off_ref, post_ref, out_ref, meta_ref):
    sub = lax.broadcasted_iota(jnp.int32, (META, COLS), 0)
    lane = lax.broadcasted_iota(jnp.int32, (META, COLS), 1)
    live = (sub < count_ref[0]).astype(f32)
    defocus = jnp.zeros((META, COLS), f32)
    ids = jnp.zeros((META, COLS), f32)
    for i in range(SEG):
        defocus = jnp.where(sub == i, defocus_ref[i], defocus)
        ids = jnp.where(sub == i, class_ref[i].astype(f32), ids)
    hi, mid, low = parts_of(defocus)
    facts = jnp.where(lane == 96, hi, jnp.where(lane == 97, mid, jnp.where(lane == 98, low, 0.0)))
    facts = jnp.where(lane == 99, ids, jnp.where(lane == 100, live, facts))
    meta_ref[...] = facts
    for i in range(SEG):
        both = off_ref[i].astype(f32)
        meta_ref[i : i + 1, 0:SHIFTS] = both[0:1]
        meta_ref[i : i + 1, SHIFTS : 2 * SHIFTS] = both[1:2]
    meta_ref[0:SEG, 2 * SHIFTS : 3 * SHIFTS] = post_ref[...].astype(f32) * live[0:SEG, 0:SHIFTS]
    meta = meta_ref[...].astype(bf16)
    for j in range(NA):
        for p in range(2):
            for i in range(SEG):
                out_ref[j, i * D + p * KY : i * D + (p + 1) * KY] = img_ref[i, p, j * KY : (j + 1) * KY]
            base = SEG * D + p * KY
            out_ref[j, base : base + KY] = ref_ref[0, p, j * KY : (j + 1) * KY]
        out_ref[j, SEG * D + D : SEG * D + D + META] = meta


def pack(images, defocus, references, offsets, posterior, class_ids, seg_count):
    smem = pl.BlockSpec(memory_space=pltpu.SMEM)
    vmem = pl.BlockSpec(memory_space=pltpu.VMEM)
    return pl.pallas_call(
        pack_kernel,
        in_specs=[smem, smem, smem, vmem, vmem, vmem, vmem],
        out_specs=vmem,
        out_shape=jax.ShapeDtypeStruct((NA, SEG * D + D + META, COLS), bf16),
        scratch_shapes=[pltpu.VMEM((META, COLS), f32)],
        compiler_params=pltpu.CompilerParams(vmem_limit_bytes=4 << 20),
        cost_estimate=pl.CostEstimate(flops=100_000, bytes_accessed=700_000, transcendentals=0),
        name="pack",
    )(defocus, class_ids, seg_count, images, references, offsets.transpose(0, 2, 1), posterior)


def chunk_kernel(recv_ref, out_ref, meta_out_ref, wide_ref):
    first = SEG * D + D
    wide_ref[...] = jnp.zeros_like(wide_ref)
    for a in range(NA):
        meta = recv_ref[a, first : first + META, :].astype(f32)[0:SEG]
        wide_ref[a * SEG : (a + 1) * SEG] = meta
        meta_out_ref[a * SEG : (a + 1) * SEG] = meta
    flat = wide_ref[...].T
    total = jnp.sum(flat[2 * SHIFTS : 3 * SHIFTS], axis=0, keepdims=True)
    total_hi = jnp.floor(total * (1.0 / 32))
    sub = lax.broadcasted_iota(jnp.int32, (META, COLS), 0)
    facts = jnp.where(sub == 5, total_hi, jnp.where(sub == 6, total - 32.0 * total_hi, flat[96 : 96 + META]))
    facts = facts.astype(bf16)
    for q in range(NB):
        for a in range(NA):
            out_ref[q, a * D : (a + 1) * D] = recv_ref[a, SEG * D : SEG * D + D]
        out_ref[q, NA * D : NA * D + META] = facts


def chunk(recv):
    vmem = pl.BlockSpec(memory_space=pltpu.VMEM)
    return pl.pallas_call(
        chunk_kernel,
        in_specs=[vmem],
        out_specs=[vmem, vmem],
        out_shape=[
            jax.ShapeDtypeStruct((NB, NA * D + META, COLS), bf16),
            jax.ShapeDtypeStruct((NA * SEG, COLS), f32),
        ],
        scratch_shapes=[pltpu.VMEM((COLS, COLS), f32)],
        compiler_params=pltpu.CompilerParams(vmem_limit_bytes=4 << 20),
        cost_estimate=pl.CostEstimate(flops=100_000, bytes_accessed=1_000_000, transcendentals=0),
        name="chunk",
    )(recv)


def align_kernel(kw_ref, img_ref, meta_ref, gain_ref, spread_ref, aligned_ref, numer_ref, x_ref):
    step = pl.program_id(0)
    kw0 = kw_ref[0].astype(f32)
    lane = lax.broadcasted_iota(jnp.int32, (SHIFTS, COLS), 1)
    sub = lax.broadcasted_iota(jnp.int32, (SHIFTS, COLS), 0)
    kx = lane.astype(f32)

    @pl.when(step == 0)
    def _():
        numer_ref[...] = jnp.zeros_like(numer_ref)

    def segment(i, carry):
        row = meta_ref[pl.ds(i, 1), :]
        wide = jnp.broadcast_to(row, (SHIFTS, COLS))
        sy = jnp.sum(jnp.where(lane == sub, wide, 0.0), axis=1, keepdims=True)
        sx = jnp.sum(jnp.where(lane == sub + SHIFTS, wide, 0.0), axis=1, keepdims=True)
        sy = jnp.broadcast_to(sy, (SHIFTS, COLS))
        pr, pi = turn(sy * kw0 + sx * kx)
        si, cr = small_sincos(sy * (-2.0 * math.pi / BOX))
        img = img_ref[0, pl.ds(pl.multiple_of(i * D, D), D), :].astype(f32)
        gain = gain_ref[i]
        x_ref[0:KY, :] = img[0:KY] * gain
        x_ref[KY:D, :] = img[KY:D] * gain
        rows = pl.ds(pl.multiple_of(i * SHIFTS, SHIFTS), SHIFTS)
        for ky in range(KY):
            xr = x_ref[ky : ky + 1, :]
            xi = x_ref[KY + ky : KY + ky + 1, :]
            aligned_ref[rows, ky * COLS : (ky + 1) * COLS] = (xr * pr - xi * pi).astype(bf16)
            aligned_ref[rows, (KY + ky) * COLS : (KY + ky + 1) * COLS] = (xr * pi + xi * pr).astype(bf16)
            if ky < KY - 1:
                pr, pi = pr * cr - pi * si, pr * si + pi * cr
        return carry

    lax.fori_loop(0, SEG, segment, 0)
    part = jnp.dot(spread_ref[...], aligned_ref[...], preferred_element_type=f32)
    for d in range(D):
        numer_ref[d] += part[:, d * COLS : (d + 1) * COLS]


def align(kw0, recv, meta, gain, spread):
    return pl.pallas_call(
        align_kernel,
        grid=(NA,),
        in_specs=[
            pl.BlockSpec(memory_space=pltpu.SMEM),
            pl.BlockSpec((1, SEG * D, COLS), lambda j: (j, 0, 0)),
            pl.BlockSpec((SEG, COLS), lambda j: (j, 0)),
            pl.BlockSpec((SEG, KY, COLS), lambda j: (j, 0, 0)),
            pl.BlockSpec((CLASSES, SEG * SHIFTS), lambda j: (0, j)),
        ],
        out_specs=[
            pl.BlockSpec((SEG * SHIFTS, D * COLS), lambda j: (j, 0)),
            pl.BlockSpec((D, CLASSES, COLS), lambda j: (0, 0, 0)),
        ],
        out_shape=[
            jax.ShapeDtypeStruct((NA * SEG * SHIFTS, D * COLS), bf16),
            jax.ShapeDtypeStruct((D, CLASSES, COLS), f32),
        ],
        scratch_shapes=[pltpu.VMEM((D, COLS), f32)],
        compiler_params=pltpu.CompilerParams(vmem_limit_bytes=57 << 20),
        cost_estimate=pl.CostEstimate(flops=600_000_000, bytes_accessed=9_000_000, transcendentals=0),
        name="align",
    )(kw0, recv, meta, gain, spread)


def score_kernel(panel_ref, aligned_ref, out_ref, wide_ref, packed_ref):
    step = pl.program_id(0)
    refs = NA * NB

    @pl.when(step == 0)
    def _():
        def widen(q, carry):
            for x in range(4):
                for zl in range(2):
                    a = 2 * x + zl
                    base = pl.multiple_of((x * 2 * NB + zl) * D + q * 2 * D, D)
                    wide_ref[pl.ds(base, D), :] = panel_ref[q, a * D : (a + 1) * D, :].astype(f32)
            return carry

        lax.fori_loop(0, NB, widen, 0)
        for d in range(D):
            packed_ref[:, d * COLS : (d + 1) * COLS] = wide_ref[pl.ds(d, refs, stride=D), :].astype(bf16)

    res = lax.dot_general(
        aligned_ref[...], packed_ref[...], (((1,), (1,)), ((), ())), preferred_element_type=f32
    )
    for i in range(SEG):
        for r in range(NROW):
            out_ref[0, r, i] = res[i * SHIFTS + r * 8 : i * SHIFTS + (r + 1) * 8, :].astype(out_ref.dtype)


def score(panel, aligned):
    refs = NA * NB
    return pl.pallas_call(
        score_kernel,
        grid=(NA,),
        in_specs=[
            pl.BlockSpec(panel.shape, lambda j: (0, 0, 0)),
            pl.BlockSpec((SEG * SHIFTS, D * COLS), lambda j: (j, 0)),
        ],
        out_specs=pl.BlockSpec((1, NROW, SEG, 8, refs), lambda j: (j, 0, 0, 0, 0)),
        out_shape=jax.ShapeDtypeStruct((NA, NROW, SEG, 8, refs), PARTIAL),
        scratch_shapes=[
            pltpu.VMEM((refs * D, COLS), f32),
            pltpu.VMEM((refs, D * COLS), bf16),
        ],
        compiler_params=pltpu.CompilerParams(vmem_limit_bytes=57 << 20),
        cost_estimate=pl.CostEstimate(flops=1_100_000_000, bytes_accessed=10_000_000, transcendentals=0),
        name="score",
    )(panel, aligned)


def contrast(defocus, kw, kx):
    radius = (kw * kw + kx * kx).astype(f32) / float(BOX * BOX)
    return -jnp.sin(200.0 * defocus * radius + 0.1)


def centred(ky):
    return (ky + BOX // 2) % BOX - BOX // 2


def per_device(images, defocus, references, offsets, posterior, class_ids, seg_count):
    row = lax.axis_index(ROW)
    group = lax.axis_index(("x", "zl"))
    fil = lax.axis_index(FIL)
    kx = jnp.arange(COLS, dtype=jnp.int32)

    send = pack(images, defocus, references, offsets, posterior, class_ids, seg_count)
    recv = lax.all_to_all(send, ("x", "zl"), 0, 0, tiled=True)
    sent_refs, meta = chunk(recv)
    panel = lax.all_to_all(sent_refs, ("yh", "zh"), 0, 0, tiled=True)

    weights = meta[:, 2 * SHIFTS : 3 * SHIFTS]
    own_defocus = meta[:, 96] + meta[:, 97] + meta[:, 98]
    own_class = meta[:, 99]
    own_live = meta[:, 100]
    kw_first = centred(row * 64 + group * KY)
    kw = kw_first + jnp.arange(KY, dtype=jnp.int32)
    gain = contrast(own_defocus[:, None, None], kw[:, None], kx[None, :]) * own_live[:, None, None]
    classes = jnp.arange(CLASSES, dtype=f32)
    member = (own_class[None, :] == classes[:, None]).astype(f32)
    spread = (member[:, :, None] * (weights * (1.0 / 256))[None]).astype(bf16).reshape(CLASSES, -1)

    aligned, numer = align(kw_first.reshape(1), recv, meta, gain, spread)
    numer = lax.all_to_all(numer, ("yh", "zh"), 0, 0, tiled=True)
    partial = score(panel, aligned)
    partial = lax.all_to_all(
        partial.reshape(NA * NROW, SEG * 8, COLS), ("x", "zl", *ROW), 0, 0, tiled=True
    )
    scores = jnp.sum(partial.astype(f32), axis=0).reshape(SEG, 8, COLS)

    numer = jnp.sum(numer, axis=0)
    swap = [
        (((hi * 2 + lo) * 4 + zh) * 2 + zl, ((zl * 2 + lo) * 4 + zh) * 2 + hi)
        for hi in range(2) for lo in range(2) for zh in range(4) for zl in range(2)
    ]
    numer = lax.ppermute(numer, ("yh", "zh", "zl"), swap)

    facts = panel[:, NA * D : NA * D + 7, : NA * SEG].astype(f32)
    all_defocus = (facts[:, 0] + facts[:, 1] + facts[:, 2]).reshape(-1)
    all_class = facts[:, 3].reshape(-1)
    all_total = ((facts[:, 5] * 32.0 + facts[:, 6]) * (1.0 / 256)).reshape(-1)
    ctf = contrast(all_defocus[:, None], centred(row * 64 + fil // 2), kx[None, :])
    totals = jnp.where(all_class[None, :] == classes[:, None], all_total[None, :], 0.0)
    denom = jnp.dot(totals, ctf * ctf, precision=lax.Precision.HIGHEST, preferred_element_type=f32)
    averages = numer * lax.rsqrt(denom + 1.0)
    return scores, averages


def solution(mesh):
    fine = Mesh(mesh.devices.reshape(4, 4, 4, 2, 2, 2), (*FIL, *ROW))
    placed = (
        P(FIL, None, ROW, None),
        P(FIL),
        P(FIL, None, ROW, None),
        P(FIL, None, None),
        P(FIL, None),
        P(FIL),
        P(FIL),
    )
    return jax.shard_map(
        per_device,
        mesh=fine,
        in_specs=placed,
        out_specs=(P(FIL, ROW, None), P(None, (*ROW, *FIL))),
        check_vma=False,
    )
```

time: 105 us -> 104 us (level)
  Pallas kernels: 15.3 us -> 26.5 us
  blocking collectives: 10.4 us -> 0 us
  starting transfers between devices: 29.9 us -> 38 us
  local copies, waits for them, and re-layouts: 11.7 us -> 5.11 us
  waiting for transfers between devices: 27.8 us -> 24.6 us
    pallas_call x2 -> x4, Pallas kernels: 15.3 us -> 26.5 us  [the longest x1 15.2 us: align(): pl.pallas_call(align_kernel, grid=(NA,), in_specs=[pl.BlockSpec(memory_sp...]
    all_to_all x1 -> x0, blocking collectives: 10.4 us -> none  [per_device(): recv = lax.all_to_all(send, 'x', 0, 0, tiled=True)]
    all_to_all x3 -> x4, starting transfers between devices: 29.9 us -> 37.3 us  [the longest x1 15.1 us: per_device(): panel = lax.all_to_all(sent_refs, ('yh', 'zh'), 0, 0, tiled=True)]
    all_to_all x3 -> x4, waiting for transfers between devices: 27.8 us -> 24.6 us  [the longest x1 12.4 us: per_device(): lax.all_to_all(partial.reshape(NA * NROW, SEG * 8, COLS), ('x', 'zl', *RO...]
    unnamed x4 -> x18, local copies, waits for them, and re-layouts: 6.6 us -> 4.4 us
    another operation x5 -> x0, other arithmetic: 2.1 us -> none  [the longest x2 1.32 us: per_device(): jnp.stack([*three_parts(defocus), class_ids.astype(f32), live], axis=1)]
    reshape x2 -> x0, local copies, waits for them, and re-layouts: 1.76 us -> none  [the longest x1 0.97 us: per_device(): images.reshape(SEG, 2, NX, KY, COLS).transpose(2, 0, 1, 3, 4)]
    broadcast_in_dim x2 -> x0, local copies, waits for them, and re-layouts: 1.26 us -> none  [the longest x1 1.26 us: per_device(): jnp.broadcast_to(chunk[None], (NYZ, *chunk.shape))]
  transfers between devices with their start and end apart: 3 -> 5, of which waited for: 3 -> 4; matrix products, arithmetic and copies ran while one was open for 5% -> 7% of each run, Pallas kernels for 15% -> 24%
where the time goes in v2:
time: 104 us; the launch traced here: 103 us
  starting transfers between devices  38 us (37%)
  Pallas kernels  26.5 us (25%)
  waiting for transfers between devices  24.6 us (24%)
  local copies, waits for them, and re-layouts  5.11 us (5%)
  other arithmetic  4.31 us (4%)
  matrix products  2.83 us (3%)
  between operations  1.44 us (1%)
    pallas_call x1, Pallas kernels, align(): pl.pallas_call(align_kernel, grid=(NA,), in_specs=[pl.BlockSpec(memory_sp...  15.2 us
    all_to_all x1, starting transfers between devices, per_device(): panel = lax.all_to_all(sent_refs, ('yh', 'zh'), 0, 0, tiled=True)  15.1 us
    all_to_all x1, waiting for transfers between devices, per_device(): lax.all_to_all(partial.reshape(NA * NROW, SEG * 8, COLS), ('x', 'zl', *RO...  12.4 us
    pallas_call x1, Pallas kernels, score(): pl.pallas_call(score_kernel, grid=(NA,), in_specs=[pl.BlockSpec(panel.sha...  8.95 us
    all_to_all x1, starting transfers between devices, per_device(): numer = lax.all_to_all(numer, ('yh', 'zh'), 0, 0, tiled=True)  8.22 us
    all_to_all x1, starting transfers between devices, per_device(): lax.all_to_all(partial.reshape(NA * NROW, SEG * 8, COLS), ('x', 'zl', *RO...  7.33 us
    all_to_all x1, starting transfers between devices, per_device(): recv = lax.all_to_all(send, ('x', 'zl'), 0, 0, tiled=True)  6.66 us
    all_to_all x1, waiting for transfers between devices, per_device(): recv = lax.all_to_all(send, ('x', 'zl'), 0, 0, tiled=True)  6.39 us
  transfers between devices with their start and end apart: 5, of which 4 were waited for; matrix products, arithmetic and copies ran while one was open for 7% of the time, Pallas kernels for 24%

profile of v2, /device:TPU:1, one launch (start us, length us, event | category | flops | bytes accessed | tf_op | source)
XLA Modules:
  0.0 102.7 jit_solution(14945182743610346449)
XLA Ops:
  1.3 0.0 copy-start.2
  1.3 0.9 copy-done.2
  2.2 0.0 copy-start.3
  2.2 0.8 copy-done.3
  3.0 0.0 copy-start.4
  3.0 0.7 copy-done.4
  3.7 0.0 copy-start.5
  3.7 0.7 copy-done.5
  4.4 0.0 copy-start.6
  4.4 0.7 copy-done.6
  5.0 0.0 copy-start.7
  5.0 0.7 copy-done.7
  5.7 1.3 %pack.1 = bf16[8,160,128]{2,1,0:T(8,128)(2,1)} custom-call(f32[8]{0:T(128)S(1)} %copy-done.6, s32[8]{0:T(128)S(1)} %copy-done.7, s32[1]{0:T(128)S(6)} %copy.9.count_ref, bf16[8,2,64,128]{3,2,1,0:T(8,128)(2,1)S(1)} %copy-done.2, bf16[1,2,64,128]{3,2,1,0:T(8,128)(2,1)S(1)} %copy-done.3, s32[8,2,32]{2,1,0:T(2,128)S(1)} %bitcast.4, s32[8,32]{1,0:T(8,128)S(1)} %copy-done.5), custom_call_target="tpu_custom_call" | custom-call | flops 100000 | bytes 700000 | tf_op jit(solution)/shard_map/pack/pallas_call | solution.py:86
  7.0 6.7 %all-to-all-start = ((bf16[8,160,128]{2,1,0:T(8,128)(2,1)}), bf16[8,160,128]{2,1,0:T(8,128)(2,1)S(1)}, u32[]{:S(2)}, u32[]{:S(2)}) async-start(bf16[8,160,128]{2,1,0:T(8,128)(2,1)} %pack.1), calls=%async_computation | async-start | bytes 655360 | tf_op jit(solution)/shard_map/all_to_all | solution.py:262
  13.7 0.1 convert_multiply_fusion
  13.8 6.4 %all-to-all-done.recv_ref.img_ref = bf16[8,160,128]{2,1,0:T(8,128)(2,1)S(1)} async-done(((bf16[8,160,128]{2,1,0:T(8,128)(2,1)}), bf16[8,160,128]{2,1,0:T(8,128)(2,1)S(1)}, u32[]{:S(2)}, u32[]{:S(2)}) %all-to-all-start) | async-done | bytes 327712 | tf_op jit(solution)/shard_map/all_to_all | solution.py:262
  20.2 0.0 copy-start
  20.2 1.0 chunk.1
  21.2 0.0 copy-start.1
  21.2 0.2 slice_reduce_fusion
  21.4 15.1 %all-to-all-start.1 = ((bf16[16,144,128]{2,1,0:T(8,128)(2,1)}), bf16[16,144,128]{2,1,0:T(8,128)(2,1)S(1)}, u32[]{:S(2)}, u32[]{:S(2)}) async-start(bf16[16,144,128]{2,1,0:T(8,128)(2,1)} %get-tuple-element.6), calls=%async_computation.1 | async-start | bytes 1179648 | tf_op jit(solution)/shard_map/all_to_all | solution.py:264
  36.5 0.2 mul.180
  36.7 0.2 mul.181
  36.9 0.1 slice_multiply_fusion
  37.0 0.1 mul.184
  37.1 1.7 %negate_multiply_fusion.gain_ref = f32[64,8,128]{2,1,0:T(8,128)} fusion(f32[64]{0:T(128)S(1)} %get-tuple-element.14, f32[8,128]{1,0:T(8,128)S(1)} %convert_multiply_fusion, f32[64]{0:T(128)S(1)} %get-tuple-element.15), kind=kLoop, calls=%fused_computation.10 | loop fusion | flops 262144 | bytes 266752 | tf_op jit(solution)/shard_map/mul | solution.py:272
  38.8 0.6 multiply_convert_fusion.spread_ref
  39.4 0.0 copy-done
  39.4 0.0 copy-done.1
  39.4 15.2 %align.1 = (bf16[2048,2048]{1,0:T(8,128)(2,1)}, f32[16,16,128]{2,1,0:T(8,128)}) custom-call(s32[1]{0:T(128)} %bitcast.1.kw_ref, bf16[8,160,128]{2,1,0:T(8,128)(2,1)} %copy-done, f32[64,128]{1,0:T(8,128)} %copy-done.1, f32[64,8,128]{2,1,0:T(8,128)} %negate_multiply_fusion.gain_ref, bf16[16,2048]{1,0:T(8,128)(2,1)} %multiply_convert_fusion.spread_ref), custom_call_target="tpu_custom_call" | custom-call | flops 600000000 | bytes 9000000 | tf_op jit(solution)/shard_map/align/pallas_call | solution.py:174
  54.6 3.3 %all-to-all-done.1.panel_ref = bf16[16,144,128]{2,1,0:T(8,128)(2,1)S(1)} async-done(((bf16[16,144,128]{2,1,0:T(8,128)(2,1)}), bf16[16,144,128]{2,1,0:T(8,128)(2,1)S(1)}, u32[]{:S(2)}, u32[]{:S(2)}) %all-to-all-start.1) | async-done | bytes 589856 | tf_op jit(solution)/shard_map/all_to_all | solution.py:264
  57.9 0.0 copy-start.8
  57.9 8.2 %all-to-all-start.3 = ((f32[16,16,128]{2,1,0:T(8,128)}), f32[16,16,128]{2,1,0:T(8,128)S(1)}, u32[]{:S(2)}, u32[]{:S(2)}) async-start(f32[16,16,128]{2,1,0:T(8,128)} %get-tuple-element.9), calls=%async_computation.3 | async-start | bytes 262144 | tf_op jit(solution)/shard_map/all_to_all | solution.py:278
  66.1 0.0 copy-done.8
  66.2 9.0 %score.1 = f32[8,4,8,8,128]{4,3,2,1,0:T(8,128)} custom-call(bf16[16,144,128]{2,1,0:T(8,128)(2,1)} %copy-done.8, bf16[2048,2048]{1,0:T(8,128)(2,1)} %get-tuple-element.8.aligned_ref), custom_call_target="tpu_custom_call" | custom-call | flops 1100000000 | bytes 10000000 | tf_op jit(solution)/shard_map/score/pallas_call | solution.py:227
  75.1 2.6 %all-to-all-done.3 = f32[16,16,128]{2,1,0:T(8,128)S(1)} async-done(((f32[16,16,128]{2,1,0:T(8,128)}), f32[16,16,128]{2,1,0:T(8,128)S(1)}, u32[]{:S(2)}, u32[]{:S(2)}) %all-to-all-start.3) | async-done | bytes 131104 | tf_op jit(solution)/shard_map/all_to_all | solution.py:278
  77.7 7.3 %all-to-all-start.2 = ((f32[32,64,128]{2,1,0:T(8,128)}), f32[32,64,128]{2,1,0:T(8,128)S(1)}, u32[]{:S(2)}, u32[]{:S(2)}) async-start(f32[32,64,128]{2,1,0:T(8,128)} %bitcast.5), calls=%async_computation.2 | async-start | bytes 2097152 | tf_op jit(solution)/shard_map/all_to_all | solution.py:280
  85.1 0.7 collective-permute-start
  85.8 0.8 slice_convert_fusion
  86.5 0.1 slice_reduce_fusion.2
  86.6 0.1 eq.41
  86.7 0.1 mul.191
  86.8 0.1 mul.194
  86.8 0.0 collective-permute-done
  86.8 2.8 %fusion.1 = f32[16,128]{1,0:T(8,128)} fusion(f32[16,128]{1,0:T(8,128)S(1)} %collective-permute-done, f32[128]{0:T(128)S(1)} %convert_multiply_fusion.1, f32[1024]{0:T(1024)S(1)} %mul.194, f32[1024]{0:T(1024)S(1)} %mul.191, f32[1024]{0:T(1024)S(1)} %eq.41), kind=kOutput, calls=%fused_computation.2 | convolution fusion | flops 25595904 | bytes 29184 | tf_op jit(solution)/shard_map/dot_general | solution.py:298
  89.7 12.4 %all-to-all-done.2 = f32[32,64,128]{2,1,0:T(8,128)S(1)} async-done(((f32[32,64,128]{2,1,0:T(8,128)}), f32[32,64,128]{2,1,0:T(8,128)S(1)}, u32[]{:S(2)}, u32[]{:S(2)}) %all-to-all-start.2) | async-done | bytes 1048608 | tf_op jit(solution)/shard_map/all_to_all | solution.py:280
  102.1 0.7 reduce_sum.18
  (5 shorter events, 0.0 us)
Async XLA Ops:
  1.3 1.0 copy-start.2
  2.2 0.8 copy-start.3
  3.0 0.7 copy-start.4
  3.7 0.7 copy-start.5
  4.4 0.7 copy-start.6
  5.0 0.7 copy-start.7
  7.0 13.1 %all-to-all-start = ((bf16[8,160,128]{2,1,0:T(8,128)(2,1)}), bf16[8,160,128]{2,1,0:T(8,128)(2,1)S(1)}, u32[]{:S(2)}, u32[]{:S(2)}) async-start(bf16[8,160,128]{2,1,0:T(8,128)(2,1)} %pack.1), calls=%async_computation | async-start | bytes 655360 | tf_op jit(solution)/shard_map/all_to_all | solution.py:262
  20.2 19.3 %copy-start = (bf16[8,160,128]{2,1,0:T(8,128)(2,1)}, bf16[8,160,128]{2,1,0:T(8,128)(2,1)S(1)}, u32[]{:S(2)}) copy-start(bf16[8,160,128]{2,1,0:T(8,128)(2,1)S(1)} %all-to-all-done.recv_ref.img_ref) | copy-start | bytes 983044
  21.2 18.3 %copy-start.1 = (f32[64,128]{1,0:T(8,128)}, f32[64,128]{1,0:T(8,128)S(1)}, u32[]{:S(2)}) copy-start(f32[64,128]{1,0:T(8,128)S(1)} %get-tuple-element.7.meta_ref) | copy-start | bytes 98308
  21.4 36.5 %all-to-all-start.1 = ((bf16[16,144,128]{2,1,0:T(8,128)(2,1)}), bf16[16,144,128]{2,1,0:T(8,128)(2,1)S(1)}, u32[]{:S(2)}, u32[]{:S(2)}) async-start(bf16[16,144,128]{2,1,0:T(8,128)(2,1)} %get-tuple-element.6), calls=%async_computation.1 | async-start | bytes 1179648 | tf_op jit(solution)/shard_map/all_to_all | solution.py:264
  57.9 8.2 %copy-start.8 = (bf16[16,144,128]{2,1,0:T(8,128)(2,1)}, bf16[16,144,128]{2,1,0:T(8,128)(2,1)S(1)}, u32[]{:S(2)}) copy-start(bf16[16,144,128]{2,1,0:T(8,128)(2,1)S(1)} %all-to-all-done.1.panel_ref) | copy-start | bytes 1769476
  57.9 19.8 %all-to-all-start.3 = ((f32[16,16,128]{2,1,0:T(8,128)}), f32[16,16,128]{2,1,0:T(8,128)S(1)}, u32[]{:S(2)}, u32[]{:S(2)}) async-start(f32[16,16,128]{2,1,0:T(8,128)} %get-tuple-element.9), calls=%async_computation.3 | async-start | bytes 262144 | tf_op jit(solution)/shard_map/all_to_all | solution.py:278
  77.7 24.4 %all-to-all-start.2 = ((f32[32,64,128]{2,1,0:T(8,128)}), f32[32,64,128]{2,1,0:T(8,128)S(1)}, u32[]{:S(2)}, u32[]{:S(2)}) async-start(f32[32,64,128]{2,1,0:T(8,128)} %bitcast.5), calls=%async_computation.2 | async-start | bytes 2097152 | tf_op jit(solution)/shard_map/all_to_all | solution.py:280
  85.1 1.7 %collective-permute-start = (f32[16,128]{1,0:T(8,128)S(1)}, f32[16,128]{1,0:T(8,128)S(1)}, u32[]{:S(2)}, u32[]{:S(2)}) collective-permute-start(f32[16,128]{1,0:T(8,128)S(1)} %reduce_sum.19), channel_id=1, source_target_pairs={{0,0},{4,64},{8,8},{12,72},{16,16},{20,80},{24,24},{28,88},{32,32}... | collective-permute-start | bytes 24584 | tf_op jit(solution)/shard_map/ppermute | solution.py:290

commit v3 on v2

--- a/solution.py
+++ b/solution.py
@@ -23,7 +23,7 @@
 ROW = ("yl", "core")
 bf16 = jnp.bfloat16
 f32 = jnp.float32
-PARTIAL = f32
+PARTIAL = bf16
 
 
 def small_sincos(theta):
@@ -52,7 +52,14 @@
     return hi, mid, rest - mid
 
 
-def pack_kernel(defocus_ref, class_ref, count_ref, img_ref, ref_ref, off_ref, post_ref, out_ref, meta_ref):
+def pack_kernel(*refs):
+    count_ref, given, out_ref, held, meta_ref, sems = refs[0], refs[1:7], refs[7], refs[8:14], refs[14], refs[15]
+    copies = [pltpu.make_async_copy(src, dst, sems.at[k]) for k, (src, dst) in enumerate(zip(given, held))]
+    for copy in copies:
+        copy.start()
+    for copy in copies:
+        copy.wait()
+    defocus_ref, class_ref, img_ref, ref_ref, off_ref, post_ref = held
     sub = lax.broadcasted_iota(jnp.int32, (META, COLS), 0)
     lane = lax.broadcasted_iota(jnp.int32, (META, COLS), 1)
     live = (sub < count_ref[0]).astype(f32)
@@ -81,18 +88,19 @@
 
 
 def pack(images, defocus, references, offsets, posterior, class_ids, seg_count):
-    smem = pl.BlockSpec(memory_space=pltpu.SMEM)
-    vmem = pl.BlockSpec(memory_space=pltpu.VMEM)
+    given = (defocus, class_ids, images, references, offsets.transpose(0, 2, 1), posterior)
+    places = (pltpu.SMEM,) * 2 + (pltpu.VMEM,) * 4
     return pl.pallas_call(
         pack_kernel,
-        in_specs=[smem, smem, smem, vmem, vmem, vmem, vmem],
-        out_specs=vmem,
+        in_specs=[pl.BlockSpec(memory_space=pltpu.SMEM)] + [pl.BlockSpec(memory_space=pltpu.HBM)] * 6,
+        out_specs=pl.BlockSpec(memory_space=pltpu.VMEM),
         out_shape=jax.ShapeDtypeStruct((NA, SEG * D + D + META, COLS), bf16),
-        scratch_shapes=[pltpu.VMEM((META, COLS), f32)],
-        compiler_params=pltpu.CompilerParams(vmem_limit_bytes=4 << 20),
+        scratch_shapes=[place(v.shape, v.dtype) for place, v in zip(places, given)]
+        + [pltpu.VMEM((META, COLS), f32), pltpu.SemaphoreType.DMA((6,))],
+        compiler_params=pltpu.CompilerParams(vmem_limit_bytes=63 << 20),
         cost_estimate=pl.CostEstimate(flops=100_000, bytes_accessed=700_000, transcendentals=0),
         name="pack",
-    )(defocus, class_ids, seg_count, images, references, offsets.transpose(0, 2, 1), posterior)
+    )(seg_count, *given)
 
 
 def chunk_kernel(recv_ref, out_ref, meta_out_ref, wide_ref):
@@ -134,6 +142,7 @@
 def align_kernel(kw_ref, img_ref, meta_ref, gain_ref, spread_ref, aligned_ref, numer_ref, x_ref):
     step = pl.program_id(0)
     kw0 = kw_ref[0].astype(f32)
+    owned = kw_ref[1] * D
     lane = lax.broadcasted_iota(jnp.int32, (SHIFTS, COLS), 1)
     sub = lax.broadcasted_iota(jnp.int32, (SHIFTS, COLS), 0)
     kx = lane.astype(f32)
@@ -166,8 +175,10 @@
 
     lax.fori_loop(0, SEG, segment, 0)
     part = jnp.dot(spread_ref[...], aligned_ref[...], preferred_element_type=f32)
-    for d in range(D):
-        numer_ref[d] += part[:, d * COLS : (d + 1) * COLS]
+    for p in range(2):
+        for ky in range(KY):
+            d = p * KY + ky
+            numer_ref[owned + 2 * ky + p] += part[:, d * COLS : (d + 1) * COLS]
 
 
 def align(kw0, recv, meta, gain, spread):
@@ -183,11 +194,11 @@
         ],
         out_specs=[
             pl.BlockSpec((SEG * SHIFTS, D * COLS), lambda j: (j, 0)),
-            pl.BlockSpec((D, CLASSES, COLS), lambda j: (0, 0, 0)),
+            pl.BlockSpec((2 * D, CLASSES, COLS), lambda j: (0, 0, 0)),
         ],
         out_shape=[
             jax.ShapeDtypeStruct((NA * SEG * SHIFTS, D * COLS), bf16),
-            jax.ShapeDtypeStruct((D, CLASSES, COLS), f32),
+            jax.ShapeDtypeStruct((2 * D, CLASSES, COLS), f32),
         ],
         scratch_shapes=[pltpu.VMEM((D, COLS), f32)],
         compiler_params=pltpu.CompilerParams(vmem_limit_bytes=57 << 20),
@@ -212,11 +223,9 @@
 
         lax.fori_loop(0, NB, widen, 0)
         for d in range(D):
-            packed_ref[:, d * COLS : (d + 1) * COLS] = wide_ref[pl.ds(d, refs, stride=D), :].astype(bf16)
-
-    res = lax.dot_general(
-        aligned_ref[...], packed_ref[...], (((1,), (1,)), ((), ())), preferred_element_type=f32
-    )
+            packed_ref[d * COLS : (d + 1) * COLS, :] = wide_ref[pl.ds(d, refs, stride=D), :].T.astype(bf16)
+
+    res = jnp.dot(aligned_ref[...], packed_ref[...], preferred_element_type=f32)
     for i in range(SEG):
         for r in range(NROW):
             out_ref[0, r, i] = res[i * SHIFTS + r * 8 : i * SHIFTS + (r + 1) * 8, :].astype(out_ref.dtype)
@@ -235,7 +244,7 @@
         out_shape=jax.ShapeDtypeStruct((NA, NROW, SEG, 8, refs), PARTIAL),
         scratch_shapes=[
             pltpu.VMEM((refs * D, COLS), f32),
-            pltpu.VMEM((refs, D * COLS), bf16),
+            pltpu.VMEM((D * COLS, refs), bf16),
         ],
         compiler_params=pltpu.CompilerParams(vmem_limit_bytes=57 << 20),
         cost_estimate=pl.CostEstimate(flops=1_100_000_000, bytes_accessed=10_000_000, transcendentals=0),
@@ -274,8 +283,8 @@
     member = (own_class[None, :] == classes[:, None]).astype(f32)
     spread = (member[:, :, None] * (weights * (1.0 / 256))[None]).astype(bf16).reshape(CLASSES, -1)
 
-    aligned, numer = align(kw_first.reshape(1), recv, meta, gain, spread)
-    numer = lax.all_to_all(numer, ("yh", "zh"), 0, 0, tiled=True)
+    aligned, numer = align(jnp.stack([kw_first, lax.axis_index("zl")]), recv, meta, gain, spread)
+    numer = lax.all_to_all(numer, ("yh", "zh", "zl"), 0, 0, tiled=True)
     partial = score(panel, aligned)
     partial = lax.all_to_all(
         partial.reshape(NA * NROW, SEG * 8, COLS), ("x", "zl", *ROW), 0, 0, tiled=True
@@ -283,11 +292,6 @@
     scores = jnp.sum(partial.astype(f32), axis=0).reshape(SEG, 8, COLS)
 
     numer = jnp.sum(numer, axis=0)
-    swap = [
-        (((hi * 2 + lo) * 4 + zh) * 2 + zl, ((zl * 2 + lo) * 4 + zh) * 2 + hi)
-        for hi in range(2) for lo in range(2) for zh in range(4) for zl in range(2)
-    ]
-    numer = lax.ppermute(numer, ("yh", "zh", "zl"), swap)
 
     facts = panel[:, NA * D : NA * D + 7, : NA * SEG].astype(f32)
     all_defocus = (facts[:, 0] + facts[:, 1] + facts[:, 2]).reshape(-1)

time: 104 us -> 94.7 us (0.911)
  waiting for transfers between devices: 24.6 us -> 19.2 us
  local copies, waits for them, and re-layouts: 5.11 us -> 0.73 us
    all_to_all x1, waiting for transfers between devices: 12.4 us -> 7.16 us  [per_device(): lax.all_to_all(partial.reshape(NA * NROW, SEG * 8, COLS), ('x', 'zl', *RO...]
    unnamed x18 -> x6, local copies, waits for them, and re-layouts: 4.4 us -> 0.01 us
  transfers between devices with their start and end apart: 5 -> 4, of which waited for: 4 -> 4; matrix products, arithmetic and copies ran while one was open for 7% -> 8% of each run, Pallas kernels for 24% -> 26%
where the time goes in v3:
time: 94.7 us; the launch traced here: 93.9 us
  starting transfers between devices  38 us (40%)
  Pallas kernels  26.8 us (28%)
  waiting for transfers between devices  19.2 us (20%)
  other arithmetic  4.9 us (5%)
  matrix products  2.82 us (3%)
  between operations  1.42 us (1%)
    pallas_call x1, Pallas kernels, align(): pl.pallas_call(align_kernel, grid=(NA,), in_specs=[pl.BlockSpec(memory_sp...  15.3 us
    all_to_all x1, starting transfers between devices, per_device(): panel = lax.all_to_all(sent_refs, ('yh', 'zh'), 0, 0, tiled=True)  15.1 us
    all_to_all x1, starting transfers between devices, per_device(): numer = lax.all_to_all(numer, ('yh', 'zh', 'zl'), 0, 0, tiled=True)  8.79 us
    pallas_call x1, Pallas kernels, score(): pl.pallas_call(score_kernel, grid=(NA,), in_specs=[pl.BlockSpec(panel.sha...  8.77 us
    all_to_all x1, starting transfers between devices, per_device(): lax.all_to_all(partial.reshape(NA * NROW, SEG * 8, COLS), ('x', 'zl', *RO...  7.48 us
    all_to_all x1, waiting for transfers between devices, per_device(): lax.all_to_all(partial.reshape(NA * NROW, SEG * 8, COLS), ('x', 'zl', *RO...  7.16 us
    all_to_all x1, starting transfers between devices, per_device(): recv = lax.all_to_all(send, ('x', 'zl'), 0, 0, tiled=True)  6.67 us
    all_to_all x1, waiting for transfers between devices, per_device(): recv = lax.all_to_all(send, ('x', 'zl'), 0, 0, tiled=True)  5.81 us
  transfers between devices with their start and end apart: 4, of which 4 were waited for; matrix products, arithmetic and copies ran while one was open for 8% of the time, Pallas kernels for 26%

profile of v3, /device:TPU:1, one launch (start us, length us, event | category | flops | bytes accessed | tf_op | source)
XLA Modules:
  0.0 93.9 jit_solution(11636785485679842681)
XLA Ops:
  1.3 1.8 %pack.1 = bf16[8,160,128]{2,1,0:T(8,128)(2,1)} custom-call(s32[1]{0:T(128)S(6)} %copy.9.refs_0_, f32[8]{0:T(128)} %refs_1_.1, s32[8]{0:T(128)} %refs_2_.1, bf16[8,2,64,128]{3,2,1,0:T(8,128)(2,1)} %refs_3_.1, bf16[1,2,64,128]{3,2,1,0:T(8,128)(2,1)} %refs_4_.1, s32[8,2,32]{2,1,0:T(2,128)} %bitcast.7, s32[8,32]{1,0:T(8,128)} %refs_6_.1), custom_call_target="tpu_custom_call" | custom-call | flops 100000 | bytes 700000 | tf_op jit(solution)/shard_map/pack/pallas_call | solution.py:93
  3.1 6.7 %all-to-all-start = ((bf16[8,160,128]{2,1,0:T(8,128)(2,1)}), bf16[8,160,128]{2,1,0:T(8,128)(2,1)S(1)}, u32[]{:S(2)}, u32[]{:S(2)}) async-start(bf16[8,160,128]{2,1,0:T(8,128)(2,1)} %pack.1), calls=%async_computation | async-start | bytes 655360 | tf_op jit(solution)/shard_map/all_to_all | solution.py:271
  9.8 0.6 pad_add_fusion.kw_ref
  10.4 0.1 convert_multiply_fusion
  10.4 5.8 %all-to-all-done.recv_ref.img_ref = bf16[8,160,128]{2,1,0:T(8,128)(2,1)S(1)} async-done(((bf16[8,160,128]{2,1,0:T(8,128)(2,1)}), bf16[8,160,128]{2,1,0:T(8,128)(2,1)S(1)}, u32[]{:S(2)}, u32[]{:S(2)}) %all-to-all-start) | async-done | bytes 327712 | tf_op jit(solution)/shard_map/all_to_all | solution.py:271
  16.2 0.0 copy-start
  16.2 1.0 %chunk.1 = (bf16[16,144,128]{2,1,0:T(8,128)(2,1)}, f32[64,128]{1,0:T(8,128)S(1)}) custom-call(bf16[8,160,128]{2,1,0:T(8,128)(2,1)S(1)} %all-to-all-done.recv_ref.img_ref), custom_call_target="tpu_custom_call" | custom-call | flops 100000 | bytes 1000000 | tf_op jit(solution)/shard_map/chunk/pallas_call | solution.py:127
  17.2 0.0 copy-start.1
  17.2 15.1 %all-to-all-start.1 = ((bf16[16,144,128]{2,1,0:T(8,128)(2,1)}), bf16[16,144,128]{2,1,0:T(8,128)(2,1)S(1)}, u32[]{:S(2)}, u32[]{:S(2)}) async-start(bf16[16,144,128]{2,1,0:T(8,128)(2,1)} %get-tuple-element.6), calls=%async_computation.1 | async-start | bytes 1179648 | tf_op jit(solution)/shard_map/all_to_all | solution.py:273
  32.3 0.2 slice_reduce_fusion
  32.6 0.2 mul.180
  32.8 0.2 mul.181
  33.0 0.1 slice_multiply_fusion
  33.1 0.1 mul.184
  33.2 1.7 %negate_multiply_fusion.gain_ref = f32[64,8,128]{2,1,0:T(8,128)} fusion(f32[64]{0:T(128)S(1)} %get-tuple-element.14, f32[8,128]{1,0:T(8,128)S(1)} %convert_multiply_fusion, f32[64]{0:T(128)S(1)} %get-tuple-element.15), kind=kLoop, calls=%fused_computation.11 | loop fusion | flops 262144 | bytes 266752 | tf_op jit(solution)/shard_map/mul | solution.py:281
  34.8 0.6 multiply_convert_fusion.spread_ref
  35.5 0.0 copy-done
  35.5 0.0 copy-done.1
  35.5 15.3 %align.1 = (bf16[2048,2048]{1,0:T(8,128)(2,1)}, f32[32,16,128]{2,1,0:T(8,128)}) custom-call(s32[2]{0:T(128)} %pad_add_fusion.kw_ref, bf16[8,160,128]{2,1,0:T(8,128)(2,1)} %copy-done, f32[64,128]{1,0:T(8,128)} %copy-done.1, f32[64,8,128]{2,1,0:T(8,128)} %negate_multiply_fusion.gain_ref, bf16[16,2048]{1,0:T(8,128)(2,1)} %multiply_convert_fusion.spread_ref), custom_call_target="tpu_custom_call" | custom-call | flops 600000000 | bytes 9000000 | tf_op jit(solution)/shard_map/align/pallas_call | solution.py:185
  50.7 3.0 %all-to-all-done.1.panel_ref = bf16[16,144,128]{2,1,0:T(8,128)(2,1)S(1)} async-done(((bf16[16,144,128]{2,1,0:T(8,128)(2,1)}), bf16[16,144,128]{2,1,0:T(8,128)(2,1)S(1)}, u32[]{:S(2)}, u32[]{:S(2)}) %all-to-all-start.1) | async-done | bytes 589856 | tf_op jit(solution)/shard_map/all_to_all | solution.py:273
  53.7 0.0 copy-start.2
  53.7 8.8 %all-to-all-start.3 = ((f32[32,16,128]{2,1,0:T(8,128)}), f32[32,16,128]{2,1,0:T(8,128)S(1)}, u32[]{:S(2)}, u32[]{:S(2)}) async-start(f32[32,16,128]{2,1,0:T(8,128)} %get-tuple-element.9), calls=%async_computation.3 | async-start | bytes 524288 | tf_op jit(solution)/shard_map/all_to_all | solution.py:287
  62.5 0.0 copy-done.2
  62.5 8.8 %score.1 = bf16[8,4,8,8,128]{4,3,2,1,0:T(8,128)(2,1)} custom-call(bf16[16,144,128]{2,1,0:T(8,128)(2,1)} %copy-done.2, bf16[2048,2048]{1,0:T(8,128)(2,1)} %get-tuple-element.8.aligned_ref), custom_call_target="tpu_custom_call" | custom-call | flops 1100000000 | bytes 10000000 | tf_op jit(solution)/shard_map/score/pallas_call | solution.py:236
  71.3 3.3 %all-to-all-done.3 = f32[32,16,128]{2,1,0:T(8,128)S(1)} async-done(((f32[32,16,128]{2,1,0:T(8,128)}), f32[32,16,128]{2,1,0:T(8,128)S(1)}, u32[]{:S(2)}, u32[]{:S(2)}) %all-to-all-start.3) | async-done | bytes 262176 | tf_op jit(solution)/shard_map/all_to_all | solution.py:287
  74.6 7.5 %all-to-all-start.2 = ((bf16[32,64,128]{2,1,0:T(8,128)(2,1)}), bf16[32,64,128]{2,1,0:T(8,128)(2,1)S(1)}, u32[]{:S(2)}, u32[]{:S(2)}) async-start(bf16[32,64,128]{2,1,0:T(8,128)(2,1)} %bitcast.5), calls=%async_computation.2 | async-start | bytes 1048576 | tf_op jit(solution)/shard_map/all_to_all | solution.py:289
  82.2 0.8 slice_convert_fusion
  82.9 0.1 slice_reduce_fusion.2
  83.0 0.1 mul.194
  83.1 0.1 mul.191
  83.2 0.1 eq.41
  83.3 2.8 %fusion.1 = f32[16,128]{1,0:T(8,128)} fusion(f32[16,128]{1,0:T(8,128)S(1)} %reduce_sum.19, f32[128]{0:T(128)S(1)} %convert_multiply_fusion.1, f32[1024]{0:T(1024)S(1)} %mul.194, f32[1024]{0:T(1024)S(1)} %mul.191, f32[1024]{0:T(1024)S(1)} %eq.41), kind=kOutput, calls=%fused_computation.2 | convolution fusion | flops 25595904 | bytes 29184 | tf_op jit(solution)/shard_map/dot_general | solution.py:302
  86.1 7.2 %all-to-all-done.2 = bf16[32,64,128]{2,1,0:T(8,128)(2,1)S(1)} async-done(((bf16[32,64,128]{2,1,0:T(8,128)(2,1)}), bf16[32,64,128]{2,1,0:T(8,128)(2,1)S(1)}, u32[]{:S(2)}, u32[]{:S(2)}) %all-to-all-start.2) | async-done | bytes 524320 | tf_op jit(solution)/shard_map/all_to_all | solution.py:289
  93.2 0.7 convert_reduce_fusion
  (5 shorter events, 0.1 us)
Async XLA Ops:
  3.1 13.2 %all-to-all-start = ((bf16[8,160,128]{2,1,0:T(8,128)(2,1)}), bf16[8,160,128]{2,1,0:T(8,128)(2,1)S(1)}, u32[]{:S(2)}, u32[]{:S(2)}) async-start(bf16[8,160,128]{2,1,0:T(8,128)(2,1)} %pack.1), calls=%async_computation | async-start | bytes 655360 | tf_op jit(solution)/shard_map/all_to_all | solution.py:271
  16.2 19.2 %copy-start = (bf16[8,160,128]{2,1,0:T(8,128)(2,1)}, bf16[8,160,128]{2,1,0:T(8,128)(2,1)S(1)}, u32[]{:S(2)}) copy-start(bf16[8,160,128]{2,1,0:T(8,128)(2,1)S(1)} %all-to-all-done.recv_ref.img_ref) | copy-start | bytes 983044
  17.2 18.2 %copy-start.1 = (f32[64,128]{1,0:T(8,128)}, f32[64,128]{1,0:T(8,128)S(1)}, u32[]{:S(2)}) copy-start(f32[64,128]{1,0:T(8,128)S(1)} %get-tuple-element.7.meta_ref) | copy-start | bytes 98308
  17.2 36.5 %all-to-all-start.1 = ((bf16[16,144,128]{2,1,0:T(8,128)(2,1)}), bf16[16,144,128]{2,1,0:T(8,128)(2,1)S(1)}, u32[]{:S(2)}, u32[]{:S(2)}) async-start(bf16[16,144,128]{2,1,0:T(8,128)(2,1)} %get-tuple-element.6), calls=%async_computation.1 | async-start | bytes 1179648 | tf_op jit(solution)/shard_map/all_to_all | solution.py:273
  53.7 8.8 %copy-start.2 = (bf16[16,144,128]{2,1,0:T(8,128)(2,1)}, bf16[16,144,128]{2,1,0:T(8,128)(2,1)S(1)}, u32[]{:S(2)}) copy-start(bf16[16,144,128]{2,1,0:T(8,128)(2,1)S(1)} %all-to-all-done.1.panel_ref) | copy-start | bytes 1769476
  53.7 20.9 %all-to-all-start.3 = ((f32[32,16,128]{2,1,0:T(8,128)}), f32[32,16,128]{2,1,0:T(8,128)S(1)}, u32[]{:S(2)}, u32[]{:S(2)}) async-start(f32[32,16,128]{2,1,0:T(8,128)} %get-tuple-element.9), calls=%async_computation.3 | async-start | bytes 524288 | tf_op jit(solution)/shard_map/all_to_all | solution.py:287
  74.6 18.7 %all-to-all-start.2 = ((bf16[32,64,128]{2,1,0:T(8,128)(2,1)}), bf16[32,64,128]{2,1,0:T(8,128)(2,1)S(1)}, u32[]{:S(2)}, u32[]{:S(2)}) async-start(bf16[32,64,128]{2,1,0:T(8,128)(2,1)} %bitcast.5), calls=%async_computation.2 | async-start | bytes 1048576 | tf_op jit(solution)/shard_map/all_to_all | solution.py:289

commit v4 on v3

v4 whole, which is shorter than its diff:
```python
import math

import jax
import jax.numpy as jnp
from jax import lax
from jax.experimental import pallas as pl
from jax.experimental.pallas import tpu as pltpu
from jax.sharding import Mesh
from jax.sharding import PartitionSpec as P

BOX = 256
SHIFTS = 32
CLASSES = 16
SEG = 8
NA = 8
NB = 32
NX = 4
NROW = 4
SEGS = NA * SEG
KY = 8
D = 2 * KY
COLS = 128
META = 8
A_REF = SEG * D
A_META = A_REF + 2 * D
A_ROWS = A_META + META
B_NUM = NX * D
B_FACT = B_NUM + CLASSES
B_ROWS = B_FACT + META
FIL = ("x", "yh", "zh", "zl")
ROW = ("yl", "core")
bf16 = jnp.bfloat16
f32 = jnp.float32
PARTIAL = bf16


def small_sincos(theta):
    t2 = theta * theta
    sin = theta * (1.0 + t2 * (-1.0 / 6 + t2 * (1.0 / 120 + t2 * (-1.0 / 5040 + t2 * (1.0 / 362880)))))
    cos = 1.0 + t2 * (-0.5 + t2 * (1.0 / 24 + t2 * (-1.0 / 720 + t2 * (1.0 / 40320 + t2 * (-1.0 / 3628800)))))
    return sin, cos


def quarter(n, sin, cos):
    quad = n - 4.0 * jnp.floor(n * 0.25)
    odd = (quad == 1.0) | (quad == 3.0)
    c = jnp.where(odd, sin, cos)
    s = jnp.where(odd, cos, sin)
    c = jnp.where((quad == 1.0) | (quad == 2.0), -c, c)
    return jnp.where(quad >= 2.0, -s, s), c


def turn(m):
    n = jnp.floor(m * (1.0 / 64) + 0.5)
    sin, cos = quarter(n, *small_sincos((m - 64.0 * n) * (math.pi / 128)))
    return cos, -sin


def sine(arg):
    n = jnp.floor(arg * (2.0 / math.pi) + 0.5)
    rest = ((arg - n * 1.5703125) - n * 4.837512969970703125e-4) - n * 7.54978995489188216e-8
    return quarter(n, *small_sincos(rest))[0]


def halves(v):
    hi = v.astype(bf16)
    return hi, (v - hi.astype(f32)).astype(bf16)


def parts_of(v):
    hi = v.astype(bf16).astype(f32)
    rest = v - hi
    mid = rest.astype(bf16).astype(f32)
    return hi, mid, rest - mid


def pack_kernel(*refs):
    count_ref, given, out_ref, held, meta_ref, sems = refs[0], refs[1:7], refs[7], refs[8:14], refs[14], refs[15]
    copies = [pltpu.make_async_copy(src, dst, sems.at[k]) for k, (src, dst) in enumerate(zip(given, held))]
    for copy in copies:
        copy.start()
    for copy in copies:
        copy.wait()
    defocus_ref, class_ref, img_ref, ref_ref, off_ref, post_ref = held
    sub = lax.broadcasted_iota(jnp.int32, (META, COLS), 0)
    lane = lax.broadcasted_iota(jnp.int32, (META, COLS), 1)
    live = (sub < count_ref[0]).astype(f32)
    defocus = jnp.zeros((META, COLS), f32)
    ids = jnp.zeros((META, COLS), f32)
    for i in range(SEG):
        defocus = jnp.where(sub == i, defocus_ref[i], defocus)
        ids = jnp.where(sub == i, class_ref[i].astype(f32), ids)
    hi, mid, low = parts_of(defocus)
    facts = jnp.where(lane == 96, hi, jnp.where(lane == 97, mid, jnp.where(lane == 98, low, 0.0)))
    facts = jnp.where(lane == 99, ids, jnp.where(lane == 100, live, facts))
    meta_ref[...] = facts
    for i in range(SEG):
        both = off_ref[i].astype(f32)
        meta_ref[i : i + 1, 0:SHIFTS] = both[0:1]
        meta_ref[i : i + 1, SHIFTS : 2 * SHIFTS] = both[1:2]
    meta_ref[0:SEG, 2 * SHIFTS : 3 * SHIFTS] = post_ref[...].astype(f32) * live[0:SEG, 0:SHIFTS]
    meta = meta_ref[...].astype(bf16)
    for j in range(NA):
        for p in range(2):
            for i in range(SEG):
                out_ref[j, i * D + p * KY : i * D + (p + 1) * KY] = img_ref[i, p, j * KY : (j + 1) * KY]
            for half in range(2):
                base = A_REF + half * D + p * KY
                first = (j // 2) * 2 * KY + half * KY
                out_ref[j, base : base + KY] = ref_ref[0, p, first : first + KY]
        out_ref[j, A_META:A_ROWS] = meta


def pack(images, defocus, references, offsets, posterior, class_ids, seg_count):
    given = (defocus, class_ids, images, references, offsets.transpose(0, 2, 1), posterior)
    places = (pltpu.SMEM,) * 2 + (pltpu.VMEM,) * 4
    return pl.pallas_call(
        pack_kernel,
        in_specs=[pl.BlockSpec(memory_space=pltpu.SMEM)] + [pl.BlockSpec(memory_space=pltpu.HBM)] * 6,
        out_specs=pl.BlockSpec(memory_space=pltpu.VMEM),
        out_shape=jax.ShapeDtypeStruct((NA, A_ROWS, COLS), bf16),
        scratch_shapes=[place(v.shape, v.dtype) for place, v in zip(places, given)]
        + [pltpu.VMEM((META, COLS), f32), pltpu.SemaphoreType.DMA((6,))],
        compiler_params=pltpu.CompilerParams(vmem_limit_bytes=63 << 20),
        cost_estimate=pl.CostEstimate(flops=100_000, bytes_accessed=700_000, transcendentals=0),
        name="pack",
    )(seg_count, *given)


def front_kernel(place_ref, recv_ref, out_ref, meta_out_ref, gx_ref, wide_ref, y_ref, col_ref):
    kw0 = place_ref[0]
    zl = place_ref[1]
    lane = lax.broadcasted_iota(jnp.int32, (KY, COLS), 1)
    sub = lax.broadcasted_iota(jnp.int32, (KY, COLS), 0)
    kw = (sub + kw0).astype(f32)
    kx = lane.astype(f32)
    radius = (kw * kw + kx * kx) * (1.0 / (BOX * BOX))
    first = (lane % (2 * SHIFTS)) < SHIFTS
    lane_s = lax.broadcasted_iota(jnp.int32, (SHIFTS, COLS), 1)
    sub_s = lax.broadcasted_iota(jnp.int32, (SHIFTS, COLS), 0)

    c, s = turn((sub_s - 8).astype(f32) * lane_s.astype(f32))
    (c_hi, c_lo), (s_hi, s_lo) = halves(c), halves(s)
    table = jnp.concatenate([c_hi, s_hi, c_lo, s_lo], axis=1)

    for a in range(NA):
        meta = recv_ref[a, A_META:A_ROWS].astype(f32)
        rows = slice(a * SEG, (a + 1) * SEG)
        meta_out_ref[rows] = meta
        wide_ref[rows] = meta
        wide_ref[SEGS + a * SEG : SEGS + (a + 1) * SEG] = meta

        def pick(at):
            return jnp.sum(jnp.where(lane == at, meta, 0.0), axis=1, keepdims=True)

        defocus = jnp.broadcast_to(pick(96) + pick(97) + pick(98), (SEG, COLS))
        alive = jnp.broadcast_to(pick(100), (SEG, COLS))
        sy = jnp.where(lane < SHIFTS, meta, 0.0)
        sy = sy + pltpu.roll(sy, SHIFTS, 1)
        sy = sy + pltpu.roll(sy, 2 * SHIFTS, 1)
        w = jnp.where((lane >= 2 * SHIFTS) & (lane < 3 * SHIFTS), meta, 0.0) * (1.0 / 256)
        w = w + pltpu.roll(w, SHIFTS, 1)
        w = w + pltpu.roll(w, 2 * SHIFTS, 1)

        hot = []
        for i in range(SEG):
            spread = jnp.broadcast_to(meta[i : i + 1], (SHIFTS, COLS))
            sx = jnp.sum(jnp.where(lane_s == sub_s + SHIFTS, spread, 0.0), axis=1, keepdims=True)
            hot.append((jnp.broadcast_to(sx, (SHIFTS, SHIFTS)) == (lane_s[:, :SHIFTS] - 8).astype(f32)).astype(f32).astype(bf16))
        col_ref[...] = jnp.dot(jnp.concatenate(hot, axis=0), table, preferred_element_type=f32).astype(bf16)

        for i in range(SEG):
            c, s = turn(jnp.broadcast_to(sy[i : i + 1], (KY, COLS)) * kw)
            wi = jnp.broadcast_to(w[i : i + 1], (KY, COLS))
            c, s = c * wi, s * wi
            left = jnp.concatenate([jnp.where(first, c, -s), jnp.where(first, s, c)], axis=0)
            hi, lo = halves(left)
            right = jnp.concatenate(
                [col_ref[i * SHIFTS : (i + 1) * SHIFTS, q * COLS : (q + 1) * COLS] for q in range(4)], axis=0
            )
            both = jnp.dot(jnp.concatenate([hi, lo], axis=0), right, preferred_element_type=f32)
            q_re = both[0:KY] + both[D : D + KY]
            q_im = both[KY:D] + both[D + KY : 2 * D]
            arg = (200.0 * jnp.broadcast_to(defocus[i : i + 1], (KY, COLS))) * radius + 0.1
            gain = -sine(arg) * jnp.broadcast_to(alive[i : i + 1], (KY, COLS))
            img = recv_ref[a, i * D : (i + 1) * D].astype(f32)
            xr, xi = img[0:KY] * gain, img[KY:D] * gain
            at = (a * SEG + i) * D
            gx_ref[at : at + KY] = xr
            gx_ref[at + KY : at + D] = xi
            y_ref[at : at + KY] = xr * q_re - xi * q_im
            y_ref[at + KY : at + D] = xr * q_im + xi * q_re

    flat = wide_ref[...].T
    ids = jnp.broadcast_to(flat[99:100], (CLASSES, COLS))
    member = (ids == lax.broadcasted_iota(jnp.int32, (CLASSES, COLS), 0).astype(f32)).astype(f32).astype(bf16)
    for p in range(2):
        for ky in range(KY):
            hi, lo = halves(y_ref[pl.ds(p * KY + ky, SEGS, stride=D), :])
            sums = jnp.dot(member, jnp.concatenate([hi, lo], axis=0), preferred_element_type=f32)
            out_ref[zl * D + 2 * ky + p, B_NUM:B_FACT] = sums.astype(bf16)
            out_ref[(1 - zl) * D + 2 * ky + p, B_NUM:B_FACT] = jnp.zeros((CLASSES, COLS), bf16)

    for x in range(NX):
        wide_ref[x * SEG : (x + 1) * SEG] = recv_ref[2 * x + zl, A_META:A_ROWS].astype(f32)
    flat = wide_ref[...].T
    total = jnp.sum(flat[2 * SHIFTS : 3 * SHIFTS], axis=0, keepdims=True)
    total_hi = jnp.floor(total * (1.0 / 32))
    facts = jnp.where(sub == 5, total_hi, jnp.where(sub == 6, total - 32.0 * total_hi, flat[96:104]))
    facts = facts.astype(bf16)
    for q in range(NB):
        for x in range(NX):
            base = A_REF + (q % 2) * D
            out_ref[q, x * D : (x + 1) * D] = recv_ref[2 * x + zl, base : base + D]
        out_ref[q, B_FACT:B_ROWS] = facts


def front(place, recv):
    vmem = pl.BlockSpec(memory_space=pltpu.VMEM)
    return pl.pallas_call(
        front_kernel,
        in_specs=[pl.BlockSpec(memory_space=pltpu.SMEM), vmem],
        out_specs=[vmem, vmem, vmem],
        out_shape=[
            jax.ShapeDtypeStruct((NB, B_ROWS, COLS), bf16),
            jax.ShapeDtypeStruct((SEGS, COLS), f32),
            jax.ShapeDtypeStruct((SEGS * D, COLS), f32),
        ],
        scratch_shapes=[
            pltpu.VMEM((COLS, COLS), f32),
            pltpu.VMEM((SEGS * D, COLS), f32),
            pltpu.VMEM((SEG * SHIFTS, 4 * COLS), bf16),
        ],
        compiler_params=pltpu.CompilerParams(vmem_limit_bytes=8 << 20),
        cost_estimate=pl.CostEstimate(flops=100_000_000, bytes_accessed=2_000_000, transcendentals=0),
        name="front",
    )(place, recv)


def align_kernel(place_ref, gx_ref, meta_ref, aligned_ref):
    kw0 = place_ref[0].astype(f32)
    lane = lax.broadcasted_iota(jnp.int32, (SHIFTS, COLS), 1)
    sub = lax.broadcasted_iota(jnp.int32, (SHIFTS, COLS), 0)
    kx = lane.astype(f32)

    def segment(i, carry):
        wide = jnp.broadcast_to(meta_ref[pl.ds(i, 1), :], (SHIFTS, COLS))
        sy = jnp.sum(jnp.where(lane == sub, wide, 0.0), axis=1, keepdims=True)
        sx = jnp.sum(jnp.where(lane == sub + SHIFTS, wide, 0.0), axis=1, keepdims=True)
        sy = jnp.broadcast_to(sy, (SHIFTS, COLS))
        pr, pi = turn(sy * kw0 + sx * kx)
        si, cr = small_sincos(sy * (-2.0 * math.pi / BOX))
        rows = pl.ds(pl.multiple_of(i * SHIFTS, SHIFTS), SHIFTS)
        for ky in range(KY):
            xr = gx_ref[pl.ds(i * D + ky, 1), :]
            xi = gx_ref[pl.ds(i * D + KY + ky, 1), :]
            aligned_ref[rows, ky * COLS : (ky + 1) * COLS] = (xr * pr - xi * pi).astype(bf16)
            aligned_ref[rows, (KY + ky) * COLS : (KY + ky + 1) * COLS] = (xr * pi + xi * pr).astype(bf16)
            if ky < KY - 1:
                pr, pi = pr * cr - pi * si, pr * si + pi * cr
        return carry

    lax.fori_loop(0, SEG, segment, 0)


def align(place, gx, meta):
    return pl.pallas_call(
        align_kernel,
        grid=(NA,),
        in_specs=[
            pl.BlockSpec(memory_space=pltpu.SMEM),
            pl.BlockSpec((SEG * D, COLS), lambda j: (j, 0)),
            pl.BlockSpec((SEG, COLS), lambda j: (j, 0)),
        ],
        out_specs=pl.BlockSpec((SEG * SHIFTS, D * COLS), lambda j: (j, 0)),
        out_shape=jax.ShapeDtypeStruct((SEGS * SHIFTS, D * COLS), bf16),
        compiler_params=pltpu.CompilerParams(vmem_limit_bytes=57 << 20),
        cost_estimate=pl.CostEstimate(flops=600_000_000, bytes_accessed=9_000_000, transcendentals=0),
        name="align",
    )(place, gx, meta)


def score_kernel(panel_ref, aligned_ref, out_ref, wide_ref, packed_ref):
    step = pl.program_id(0)
    refs = NX * NB

    @pl.when(step == 0)
    def _():
        def widen(q, carry):
            for x in range(NX):
                base = pl.multiple_of((x * NB + q) * D, D)
                wide_ref[pl.ds(base, D), :] = panel_ref[q, x * D : (x + 1) * D, :].astype(f32)
            return carry

        lax.fori_loop(0, NB, widen, 0)
        for d in range(D):
            packed_ref[d * COLS : (d + 1) * COLS, :] = wide_ref[pl.ds(d, refs, stride=D), :].T.astype(bf16)

    res = jnp.dot(aligned_ref[...], packed_ref[...], preferred_element_type=f32)
    for i in range(SEG):
        for r in range(NROW):
            out_ref[0, r, i] = res[i * SHIFTS + r * 8 : i * SHIFTS + (r + 1) * 8, :].astype(out_ref.dtype)


def score(panel, aligned):
    refs = NX * NB
    return pl.pallas_call(
        score_kernel,
        grid=(NA,),
        in_specs=[
            pl.BlockSpec(panel.shape, lambda j: (0, 0, 0)),
            pl.BlockSpec((SEG * SHIFTS, D * COLS), lambda j: (j, 0)),
        ],
        out_specs=pl.BlockSpec((1, NROW, SEG, 8, refs), lambda j: (j, 0, 0, 0, 0)),
        out_shape=jax.ShapeDtypeStruct((NA, NROW, SEG, 8, refs), PARTIAL),
        scratch_shapes=[
            pltpu.VMEM((refs * D, COLS), f32),
            pltpu.VMEM((D * COLS, refs), bf16),
        ],
        compiler_params=pltpu.CompilerParams(vmem_limit_bytes=57 << 20),
        cost_estimate=pl.CostEstimate(flops=1_100_000_000, bytes_accessed=10_000_000, transcendentals=0),
        name="score",
    )(panel, aligned)


def contrast(defocus, kw, kx):
    radius = (kw * kw + kx * kx).astype(f32) / float(BOX * BOX)
    return -jnp.sin(200.0 * defocus * radius + 0.1)


def centred(ky):
    return (ky + BOX // 2) % BOX - BOX // 2


def per_device(images, defocus, references, offsets, posterior, class_ids, seg_count):
    row = lax.axis_index(ROW)
    fil = lax.axis_index(FIL)
    kx = jnp.arange(COLS, dtype=jnp.int32)
    kw_first = centred(row * 64 + lax.axis_index(("x", "zl")) * KY)
    place = jnp.stack([kw_first, lax.axis_index("zl")])

    send = pack(images, defocus, references, offsets, posterior, class_ids, seg_count)
    recv = lax.all_to_all(send, ("x", "zl"), 0, 0, tiled=True)
    sent, meta, gx = front(place, recv)
    panel = lax.all_to_all(sent, ("yh", "zh", "zl"), 0, 0, tiled=True)
    aligned = align(place, gx, meta)
    partial = score(panel, aligned)
    partial = lax.all_to_all(
        partial.reshape(NA * NROW, SEG * 8, COLS), ("x", "zl", *ROW), 0, 0, tiled=True
    )
    scores = jnp.sum(partial.astype(f32), axis=0).reshape(SEG, 8, COLS)

    numer = jnp.sum(panel[:, B_NUM:B_FACT].astype(f32), axis=0)
    facts = panel[:, B_FACT:B_ROWS, : NX * SEG].astype(f32)
    all_defocus = (facts[:, 0] + facts[:, 1] + facts[:, 2]).reshape(-1)
    all_class = facts[:, 3].reshape(-1)
    all_total = ((facts[:, 5] * 32.0 + facts[:, 6]) * (1.0 / 256)).reshape(-1)
    ctf = contrast(all_defocus[:, None], centred(row * 64 + fil // 2), kx[None, :])
    classes = jnp.arange(CLASSES, dtype=f32)
    totals = jnp.where(all_class[None, :] == classes[:, None], all_total[None, :], 0.0)
    denom = jnp.dot(totals, ctf * ctf, precision=lax.Precision.HIGHEST, preferred_element_type=f32)
    averages = numer * lax.rsqrt(denom + 1.0)
    return scores, averages


def solution(mesh):
    fine = Mesh(mesh.devices.reshape(4, 4, 4, 2, 2, 2), (*FIL, *ROW))
    placed = (
        P(FIL, None, ROW, None),
        P(FIL),
        P(FIL, None, ROW, None),
        P(FIL, None, None),
        P(FIL, None),
        P(FIL),
        P(FIL),
    )
    return jax.shard_map(
        per_device,
        mesh=fine,
        in_specs=placed,
        out_specs=(P(FIL, ROW, None), P(None, (*ROW, *FIL))),
        check_vma=False,
    )
```

time: 94.7 us -> 88 us (0.929)
  starting transfers between devices: 38 us -> 28.5 us
  other arithmetic: 4.9 us -> 2.77 us
  local copies, waits for them, and re-layouts: 0.73 us -> 2.58 us
  Pallas kernels: 26.8 us -> 28.6 us
  waiting for transfers between devices: 19.2 us -> 20.8 us
    all_to_all x2 -> x1, starting transfers between devices: 23.9 us -> 15.4 us  [per_device(): panel = lax.all_to_all(sent, ('yh', 'zh', 'zl'), 0, 0, tiled=True)]
    pallas_call x1, Pallas kernels: 0.97 us -> 4.14 us  [front(): pl.pallas_call(front_kernel, in_specs=[pl.BlockSpec(memory_space=pltpu.SM...]
    unnamed x6 -> x8, local copies, waits for them, and re-layouts: 0.01 us -> 2.37 us
    all_to_all x2 -> x1, waiting for transfers between devices: 6.27 us -> 8.24 us  [per_device(): panel = lax.all_to_all(sent, ('yh', 'zh', 'zl'), 0, 0, tiled=True)]
    mul x4 -> x0, other arithmetic: 1.76 us -> none  [the longest x1 1.68 us: per_device(): contrast(own_defocus[:, None, None], kw[:, None], kx[None, :])]
    pallas_call x1, Pallas kernels: 15.3 us -> 13.7 us  [align(): pl.pallas_call(align_kernel, grid=(NA,), in_specs=[pl.BlockSpec(memory_sp...]
    all_to_all x1, starting transfers between devices: 7.48 us -> 6.34 us  [per_device(): lax.all_to_all(partial.reshape(NA * NROW, SEG * 8, COLS), ('x', 'zl', *RO...]
    all_to_all x1, waiting for transfers between devices: 7.16 us -> 6.05 us  [per_device(): lax.all_to_all(partial.reshape(NA * NROW, SEG * 8, COLS), ('x', 'zl', *RO...]
  transfers between devices with their start and end apart: 4 -> 3, of which waited for: 4 -> 3; matrix products, arithmetic and copies ran while one was open for 8% -> 6% of each run, Pallas kernels for 26% -> 16%
where the time goes in v4:
time: 88 us; the launch traced here: 87.3 us
  Pallas kernels  28.6 us (32%)
  starting transfers between devices  28.5 us (32%)
  waiting for transfers between devices  20.8 us (24%)
  matrix products  2.82 us (3%)
  other arithmetic  2.77 us (3%)
  local copies, waits for them, and re-layouts  2.58 us (3%)
  between operations  1.38 us (2%)
    all_to_all x1, starting transfers between devices, per_device(): panel = lax.all_to_all(sent, ('yh', 'zh', 'zl'), 0, 0, tiled=True)  15.4 us
    pallas_call x1, Pallas kernels, align(): pl.pallas_call(align_kernel, grid=(NA,), in_specs=[pl.BlockSpec(memory_sp...  13.7 us
    pallas_call x1, Pallas kernels, score(): pl.pallas_call(score_kernel, grid=(NA,), in_specs=[pl.BlockSpec(panel.sha...  8.86 us
    all_to_all x1, waiting for transfers between devices, per_device(): panel = lax.all_to_all(sent, ('yh', 'zh', 'zl'), 0, 0, tiled=True)  8.24 us
    all_to_all x1, starting transfers between devices, per_device(): recv = lax.all_to_all(send, ('x', 'zl'), 0, 0, tiled=True)  6.67 us
    all_to_all x1, waiting for transfers between devices, per_device(): recv = lax.all_to_all(send, ('x', 'zl'), 0, 0, tiled=True)  6.49 us
    all_to_all x1, starting transfers between devices, per_device(): lax.all_to_all(partial.reshape(NA * NROW, SEG * 8, COLS), ('x', 'zl', *RO...  6.34 us
    all_to_all x1, waiting for transfers between devices, per_device(): lax.all_to_all(partial.reshape(NA * NROW, SEG * 8, COLS), ('x', 'zl', *RO...  6.05 us
  transfers between devices with their start and end apart: 3, of which 3 were waited for; matrix products, arithmetic and copies ran while one was open for 6% of the time, Pallas kernels for 16%

profile of v4, /device:TPU:1, one launch (start us, length us, event | category | flops | bytes accessed | tf_op | source)
XLA Modules:
  0.0 87.3 jit_solution(16877119562678807437)
XLA Ops:
  1.3 1.8 %pack.1 = bf16[8,168,128]{2,1,0:T(8,128)(2,1)} custom-call(s32[1]{0:T(128)S(6)} %copy.9.refs_0_, f32[8]{0:T(128)} %refs_1_.1, s32[8]{0:T(128)} %refs_2_.1, bf16[8,2,64,128]{3,2,1,0:T(8,128)(2,1)} %refs_3_.1, bf16[1,2,64,128]{3,2,1,0:T(8,128)(2,1)} %refs_4_.1, s32[8,2,32]{2,1,0:T(2,128)} %bitcast.7, s32[8,32]{1,0:T(8,128)} %refs_6_.1), custom_call_target="tpu_custom_call" | custom-call | flops 100000 | bytes 700000 | tf_op jit(solution)/shard_map/pack/pallas_call | solution.py:117
  3.1 6.7 %all-to-all-start = ((bf16[8,168,128]{2,1,0:T(8,128)(2,1)}), bf16[8,168,128]{2,1,0:T(8,128)(2,1)S(1)}, u32[]{:S(2)}, u32[]{:S(2)}) async-start(bf16[8,168,128]{2,1,0:T(8,128)(2,1)} %pack.1), calls=%async_computation | async-start | bytes 688128 | tf_op jit(solution)/shard_map/all_to_all | solution.py:343
  9.8 0.1 pad_add_fusion.place_ref
  9.8 0.0 copy-start.2
  9.8 6.5 %all-to-all-done.recv_ref = bf16[8,168,128]{2,1,0:T(8,128)(2,1)S(1)} async-done(((bf16[8,168,128]{2,1,0:T(8,128)(2,1)}), bf16[8,168,128]{2,1,0:T(8,128)(2,1)S(1)}, u32[]{:S(2)}, u32[]{:S(2)}) %all-to-all-start) | async-done | bytes 344096 | tf_op jit(solution)/shard_map/all_to_all | solution.py:343
  16.3 4.1 %front.1 = (bf16[32,88,128]{2,1,0:T(8,128)(2,1)}, f32[64,128]{1,0:T(8,128)S(1)}, f32[1024,128]{1,0:T(8,128)S(1)}) custom-call(s32[2]{0:T(128)S(1)} %pad_add_fusion.place_ref, bf16[8,168,128]{2,1,0:T(8,128)(2,1)S(1)} %all-to-all-done.recv_ref), custom_call_target="tpu_custom_call" | custom-call | flops 100000000 | bytes 2000000 | tf_op jit(solution)/shard_map/front/pallas_call | solution.py:220
  20.5 0.0 copy-start
  20.5 0.8 copy-done
  21.3 0.0 copy-start.1
  21.3 0.6 copy-done.1
  21.9 15.4 %all-to-all-start.1 = ((bf16[32,88,128]{2,1,0:T(8,128)(2,1)}), bf16[32,88,128]{2,1,0:T(8,128)(2,1)S(1)}, u32[]{:S(2)}, u32[]{:S(2)}) async-start(bf16[32,88,128]{2,1,0:T(8,128)(2,1)} %get-tuple-element.5), calls=%async_computation.1 | async-start | bytes 1441792 | tf_op jit(solution)/shard_map/all_to_all | solution.py:345
  37.4 0.0 copy-done.2
  37.4 13.7 %align.1.aligned_ref = bf16[2048,2048]{1,0:T(8,128)(2,1)} custom-call(s32[2]{0:T(128)} %copy-done.2, f32[1024,128]{1,0:T(8,128)} %copy-done, f32[64,128]{1,0:T(8,128)} %copy-done.1), custom_call_target="tpu_custom_call" | custom-call | flops 600000000 | bytes 9000000 | tf_op jit(solution)/shard_map/align/pallas_call | solution.py:267
  51.1 8.2 %all-to-all-done.1.panel_ref = bf16[32,88,128]{2,1,0:T(8,128)(2,1)S(1)} async-done(((bf16[32,88,128]{2,1,0:T(8,128)(2,1)}), bf16[32,88,128]{2,1,0:T(8,128)(2,1)S(1)}, u32[]{:S(2)}, u32[]{:S(2)}) %all-to-all-start.1) | async-done | bytes 720928 | tf_op jit(solution)/shard_map/all_to_all | solution.py:345
  59.4 0.0 copy-start.3
  59.4 0.9 %copy-done.3 = bf16[32,88,128]{2,1,0:T(8,128)(2,1)} copy-done((bf16[32,88,128]{2,1,0:T(8,128)(2,1)}, bf16[32,88,128]{2,1,0:T(8,128)(2,1)S(1)}, u32[]{:S(2)}) %copy-start.3) | copy-done | bytes 720920
  60.3 8.9 %score.1 = bf16[8,4,8,8,128]{4,3,2,1,0:T(8,128)(2,1)} custom-call(bf16[32,88,128]{2,1,0:T(8,128)(2,1)} %copy-done.3, bf16[2048,2048]{1,0:T(8,128)(2,1)} %align.1.aligned_ref), custom_call_target="tpu_custom_call" | custom-call | flops 1100000000 | bytes 10000000 | tf_op jit(solution)/shard_map/score/pallas_call | solution.py:307
  69.2 6.3 %all-to-all-start.2 = ((bf16[32,64,128]{2,1,0:T(8,128)(2,1)}), bf16[32,64,128]{2,1,0:T(8,128)(2,1)S(1)}, u32[]{:S(2)}, u32[]{:S(2)}) async-start(bf16[32,64,128]{2,1,0:T(8,128)(2,1)} %bitcast.5), calls=%async_computation.2 | async-start | bytes 1048576 | tf_op jit(solution)/shard_map/all_to_all | solution.py:348
  75.6 0.9 slice_convert_fusion
  76.4 0.2 slice_reduce_fusion
  76.6 0.1 mul.101
  76.7 0.1 mul.98
  76.8 0.1 eq.18
  76.8 0.9 %convert_reduce_fusion.1 = f32[16,128]{1,0:T(8,128)S(1)} fusion(bf16[32,88,128]{2,1,0:T(8,128)(2,1)} %copy-done.3), kind=kLoop, calls=%fused_computation.11 | loop fusion | flops 129024 | bytes 139264 | tf_op jit(solution)/shard_map/reduce_sum | solution.py:353
  77.8 2.8 %fusion.1 = f32[16,128]{1,0:T(8,128)} fusion(f32[16,128]{1,0:T(8,128)S(1)} %convert_reduce_fusion.1, f32[128]{0:T(128)S(1)} %convert_multiply_fusion, f32[1024]{0:T(1024)S(1)} %mul.101, f32[1024]{0:T(1024)S(1)} %mul.98, f32[1024]{0:T(1024)S(1)} %eq.18), kind=kOutput, calls=%fused_computation.2 | convolution fusion | flops 25595904 | bytes 29184 | tf_op jit(solution)/shard_map/dot_general | solution.py:361
  80.6 6.0 %all-to-all-done.2 = bf16[32,64,128]{2,1,0:T(8,128)(2,1)S(1)} async-done(((bf16[32,64,128]{2,1,0:T(8,128)(2,1)}), bf16[32,64,128]{2,1,0:T(8,128)(2,1)S(1)}, u32[]{:S(2)}, u32[]{:S(2)}) %all-to-all-start.2) | async-done | bytes 524320 | tf_op jit(solution)/shard_map/all_to_all | solution.py:348
  86.7 0.7 convert_reduce_fusion
  (1 shorter events, 0.0 us)
Async XLA Ops:
  3.1 13.2 %all-to-all-start = ((bf16[8,168,128]{2,1,0:T(8,128)(2,1)}), bf16[8,168,128]{2,1,0:T(8,128)(2,1)S(1)}, u32[]{:S(2)}, u32[]{:S(2)}) async-start(bf16[8,168,128]{2,1,0:T(8,128)(2,1)} %pack.1), calls=%async_computation | async-start | bytes 688128 | tf_op jit(solution)/shard_map/all_to_all | solution.py:343
  9.8 27.5 %copy-start.2 = (s32[2]{0:T(128)}, s32[2]{0:T(128)S(1)}, u32[]{:S(2)}) copy-start(s32[2]{0:T(128)S(1)} %pad_add_fusion.place_ref) | copy-start | bytes 28
  20.5 0.8 copy-start
  21.3 0.6 copy-start.1
  21.9 37.5 %all-to-all-start.1 = ((bf16[32,88,128]{2,1,0:T(8,128)(2,1)}), bf16[32,88,128]{2,1,0:T(8,128)(2,1)S(1)}, u32[]{:S(2)}, u32[]{:S(2)}) async-start(bf16[32,88,128]{2,1,0:T(8,128)(2,1)} %get-tuple-element.5), calls=%async_computation.1 | async-start | bytes 1441792 | tf_op jit(solution)/shard_map/all_to_all | solution.py:345
  59.4 0.9 %copy-start.3 = (bf16[32,88,128]{2,1,0:T(8,128)(2,1)}, bf16[32,88,128]{2,1,0:T(8,128)(2,1)S(1)}, u32[]{:S(2)}) copy-start(bf16[32,88,128]{2,1,0:T(8,128)(2,1)S(1)} %all-to-all-done.1.panel_ref) | copy-start | bytes 2162692
  69.2 17.5 %all-to-all-start.2 = ((bf16[32,64,128]{2,1,0:T(8,128)(2,1)}), bf16[32,64,128]{2,1,0:T(8,128)(2,1)S(1)}, u32[]{:S(2)}, u32[]{:S(2)}) async-start(bf16[32,64,128]{2,1,0:T(8,128)(2,1)} %bitcast.5), calls=%async_computation.2 | async-start | bytes 1048576 | tf_op jit(solution)/shard_map/all_to_all | solution.py:348

commit v5 on v4

--- a/solution.py
+++ b/solution.py
@@ -121,10 +121,10 @@
         out_shape=jax.ShapeDtypeStruct((NA, A_ROWS, COLS), bf16),
         scratch_shapes=[place(v.shape, v.dtype) for place, v in zip(places, given)]
         + [pltpu.VMEM((META, COLS), f32), pltpu.SemaphoreType.DMA((6,))],
-        compiler_params=pltpu.CompilerParams(vmem_limit_bytes=63 << 20),
+        compiler_params=pltpu.CompilerParams(vmem_limit_bytes=4 << 20),
         cost_estimate=pl.CostEstimate(flops=100_000, bytes_accessed=700_000, transcendentals=0),
         name="pack",
-    )(seg_count, *given)
+    )(seg_count, *(pltpu.with_memory_space_constraint(v, pltpu.HBM) for v in given))
 
 
 def front_kernel(place_ref, recv_ref, out_ref, meta_out_ref, gx_ref, wide_ref, y_ref, col_ref):
@@ -273,54 +273,61 @@
             pl.BlockSpec((SEG, COLS), lambda j: (j, 0)),
         ],
         out_specs=pl.BlockSpec((SEG * SHIFTS, D * COLS), lambda j: (j, 0)),
-        out_shape=jax.ShapeDtypeStruct((SEGS * SHIFTS, D * COLS), bf16),
-        compiler_params=pltpu.CompilerParams(vmem_limit_bytes=57 << 20),
+        out_shape=pltpu.HBM((SEGS * SHIFTS, D * COLS), bf16),
+        compiler_params=pltpu.CompilerParams(vmem_limit_bytes=10 << 20),
         cost_estimate=pl.CostEstimate(flops=600_000_000, bytes_accessed=9_000_000, transcendentals=0),
         name="align",
     )(place, gx, meta)
 
 
-def score_kernel(panel_ref, aligned_ref, out_ref, wide_ref, packed_ref):
-    step = pl.program_id(0)
+def score_kernel(panel_ref, aligned_ref, out_ref, wide_ref, packed_ref, held_ref, sems):
     refs = NX * NB
-
-    @pl.when(step == 0)
-    def _():
-        def widen(q, carry):
-            for x in range(NX):
-                base = pl.multiple_of((x * NB + q) * D, D)
-                wide_ref[pl.ds(base, D), :] = panel_ref[q, x * D : (x + 1) * D, :].astype(f32)
-            return carry
-
-        lax.fori_loop(0, NB, widen, 0)
-        for d in range(D):
-            packed_ref[d * COLS : (d + 1) * COLS, :] = wide_ref[pl.ds(d, refs, stride=D), :].T.astype(bf16)
-
-    res = jnp.dot(aligned_ref[...], packed_ref[...], preferred_element_type=f32)
-    for i in range(SEG):
-        for r in range(NROW):
-            out_ref[0, r, i] = res[i * SHIFTS + r * 8 : i * SHIFTS + (r + 1) * 8, :].astype(out_ref.dtype)
+    block = SEG * SHIFTS
+    copies = [
+        pltpu.make_async_copy(
+            aligned_ref.at[j * block : (j + 1) * block], held_ref.at[j * block : (j + 1) * block], sems.at[j]
+        )
+        for j in range(NA)
+    ]
+    for copy in copies:
+        copy.start()
+
+    def widen(q, carry):
+        for x in range(NX):
+            base = pl.multiple_of((x * NB + q) * D, D)
+            wide_ref[pl.ds(base, D), :] = panel_ref[q, x * D : (x + 1) * D, :].astype(f32)
+        return carry
+
+    lax.fori_loop(0, NB, widen, 0)
+    for d in range(D):
+        packed_ref[d * COLS : (d + 1) * COLS, :] = wide_ref[pl.ds(d, refs, stride=D), :].T.astype(bf16)
+
+    for j in range(NA):
+        copies[j].wait()
+        res = jnp.dot(held_ref[j * block : (j + 1) * block], packed_ref[...], preferred_element_type=f32)
+        for i in range(SEG):
+            for r in range(NROW):
+                out_ref[j, r, i] = res[i * SHIFTS + r * 8 : i * SHIFTS + (r + 1) * 8, :].astype(out_ref.dtype)
 
 
 def score(panel, aligned):
     refs = NX * NB
+    vmem = pl.BlockSpec(memory_space=pltpu.VMEM)
     return pl.pallas_call(
         score_kernel,
-        grid=(NA,),
-        in_specs=[
-            pl.BlockSpec(panel.shape, lambda j: (0, 0, 0)),
-            pl.BlockSpec((SEG * SHIFTS, D * COLS), lambda j: (j, 0)),
-        ],
-        out_specs=pl.BlockSpec((1, NROW, SEG, 8, refs), lambda j: (j, 0, 0, 0, 0)),
+        in_specs=[vmem, pl.BlockSpec(memory_space=pltpu.HBM)],
+        out_specs=vmem,
         out_shape=jax.ShapeDtypeStruct((NA, NROW, SEG, 8, refs), PARTIAL),
         scratch_shapes=[
             pltpu.VMEM((refs * D, COLS), f32),
             pltpu.VMEM((D * COLS, refs), bf16),
+            pltpu.VMEM(aligned.shape, bf16),
+            pltpu.SemaphoreType.DMA((NA,)),
         ],
-        compiler_params=pltpu.CompilerParams(vmem_limit_bytes=57 << 20),
+        compiler_params=pltpu.CompilerParams(vmem_limit_bytes=20 << 20),
         cost_estimate=pl.CostEstimate(flops=1_100_000_000, bytes_accessed=10_000_000, transcendentals=0),
         name="score",
-    )(panel, aligned)
+    )(panel, pltpu.with_memory_space_constraint(aligned, pltpu.HBM))
 
 
 def contrast(defocus, kw, kx):

time: 88 us -> 82.1 us (0.933)
  Pallas kernels: 28.6 us -> 24.9 us
  local copies, waits for them, and re-layouts: 2.58 us -> 0.21 us
  waiting for transfers between devices: 20.8 us -> 22.9 us
  other arithmetic: 2.77 us -> 1.01 us
    pallas_call x1, Pallas kernels: 8.86 us -> 5.54 us  [score(): pl.pallas_call(score_kernel, in_specs=[vmem, pl.BlockSpec(memory_space=pl...]
    unnamed x8 -> x0, local copies, waits for them, and re-layouts: 2.37 us -> none
    all_to_all x1, waiting for transfers between devices: 6.05 us -> 7.78 us  [per_device(): lax.all_to_all(partial.reshape(NA * NROW, SEG * 8, COLS), ('x', 'zl', *RO...]
    reduce_sum x1, other arithmetic: 0.95 us -> 0.04 us  [per_device(): numer = jnp.sum(panel[:, B_NUM:B_FACT].astype(f32), axis=0)]
  transfers between devices with their start and end apart: 3 -> 3, of which waited for: 3 -> 3; matrix products, arithmetic and copies ran while one was open for 6% -> 4% of each run, Pallas kernels for 16% -> 16%
where the time goes in v5:
time: 82.1 us; the launch traced here: 81.7 us
  starting transfers between devices  28.5 us (35%)
  Pallas kernels  24.9 us (30%)
  waiting for transfers between devices  22.9 us (28%)
  matrix products  2.83 us (3%)
  between operations  1.39 us (2%)
  other arithmetic  1.01 us (1%)
    all_to_all x1, starting transfers between devices, per_device(): panel = lax.all_to_all(sent, ('yh', 'zh', 'zl'), 0, 0, tiled=True)  15.4 us
    pallas_call x1, Pallas kernels, align(): pl.pallas_call(align_kernel, grid=(NA,), in_specs=[pl.BlockSpec(memory_sp...  13.4 us
    all_to_all x1, waiting for transfers between devices, per_device(): panel = lax.all_to_all(sent, ('yh', 'zh', 'zl'), 0, 0, tiled=True)  8.64 us
    all_to_all x1, waiting for transfers between devices, per_device(): lax.all_to_all(partial.reshape(NA * NROW, SEG * 8, COLS), ('x', 'zl', *RO...  7.78 us
    all_to_all x1, starting transfers between devices, per_device(): recv = lax.all_to_all(send, ('x', 'zl'), 0, 0, tiled=True)  6.67 us
    all_to_all x1, waiting for transfers between devices, per_device(): recv = lax.all_to_all(send, ('x', 'zl'), 0, 0, tiled=True)  6.5 us
    all_to_all x1, starting transfers between devices, per_device(): lax.all_to_all(partial.reshape(NA * NROW, SEG * 8, COLS), ('x', 'zl', *RO...  6.35 us
    pallas_call x1, Pallas kernels, score(): pl.pallas_call(score_kernel, in_specs=[vmem, pl.BlockSpec(memory_space=pl...  5.54 us
  transfers between devices with their start and end apart: 3, of which 3 were waited for; matrix products, arithmetic and copies ran while one was open for 4% of the time, Pallas kernels for 16%

profile of v5, /device:TPU:1, one launch (start us, length us, event | category | flops | bytes accessed | tf_op | source)
XLA Modules:
  0.0 81.7 jit_solution(12890863516157634405)
XLA Ops:
  1.3 1.8 %pack.1 = bf16[8,168,128]{2,1,0:T(8,128)(2,1)} custom-call(s32[1]{0:T(128)S(6)} %copy.9.refs_0_, f32[8]{0:T(128)} %refs_1_.1, s32[8]{0:T(128)} %refs_2_.1, bf16[8,2,64,128]{3,2,1,0:T(8,128)(2,1)} %refs_3_.1, bf16[1,2,64,128]{3,2,1,0:T(8,128)(2,1)} %refs_4_.1, s32[8,2,32]{2,1,0:T(2,128)} %bitcast.6, s32[8,32]{1,0:T(8,128)} %refs_6_.1), custom_call_target="tpu_custom_call" | custom-call | flops 100000 | bytes 700000 | tf_op jit(solution)/shard_map/pack/pallas_call | solution.py:117
  3.1 6.7 %all-to-all-start = ((bf16[8,168,128]{2,1,0:T(8,128)(2,1)}), bf16[8,168,128]{2,1,0:T(8,128)(2,1)S(1)}, u32[]{:S(2)}, u32[]{:S(2)}) async-start(bf16[8,168,128]{2,1,0:T(8,128)(2,1)} %pack.1), calls=%async_computation | async-start | bytes 688128 | tf_op jit(solution)/shard_map/all_to_all | solution.py:350
  9.8 0.1 pad_add_fusion.place_ref
  9.8 6.5 %all-to-all-done.recv_ref = bf16[8,168,128]{2,1,0:T(8,128)(2,1)S(1)} async-done(((bf16[8,168,128]{2,1,0:T(8,128)(2,1)}), bf16[8,168,128]{2,1,0:T(8,128)(2,1)S(1)}, u32[]{:S(2)}, u32[]{:S(2)}) %all-to-all-start) | async-done | bytes 344096 | tf_op jit(solution)/shard_map/all_to_all | solution.py:350
  16.3 4.1 %front.1 = (bf16[32,88,128]{2,1,0:T(8,128)(2,1)}, f32[64,128]{1,0:T(8,128)S(1)}, f32[1024,128]{1,0:T(8,128)S(1)}) custom-call(s32[2]{0:T(128)S(1)} %pad_add_fusion.place_ref, bf16[8,168,128]{2,1,0:T(8,128)(2,1)S(1)} %all-to-all-done.recv_ref), custom_call_target="tpu_custom_call" | custom-call | flops 100000000 | bytes 2000000 | tf_op jit(solution)/shard_map/front/pallas_call | solution.py:220
  20.5 15.4 %all-to-all-start.1 = ((bf16[32,88,128]{2,1,0:T(8,128)(2,1)}), bf16[32,88,128]{2,1,0:T(8,128)(2,1)S(1)}, u32[]{:S(2)}, u32[]{:S(2)}) async-start(bf16[32,88,128]{2,1,0:T(8,128)(2,1)} %get-tuple-element.5), calls=%async_computation.1 | async-start | bytes 1441792 | tf_op jit(solution)/shard_map/all_to_all | solution.py:352
  35.9 13.4 %align.1.aligned_ref = bf16[2048,2048]{1,0:T(8,128)(2,1)} custom-call(s32[2]{0:T(128)S(1)} %pad_add_fusion.place_ref, f32[1024,128]{1,0:T(8,128)S(1)} %get-tuple-element.6.gx_ref, f32[64,128]{1,0:T(8,128)S(1)} %get-tuple-element.7.meta_ref), custom_call_target="tpu_custom_call" | custom-call | flops 600000000 | bytes 9000000 | tf_op jit(solution)/shard_map/align/pallas_call | solution.py:267
  49.3 8.6 %all-to-all-done.1.panel_ref = bf16[32,88,128]{2,1,0:T(8,128)(2,1)S(1)} async-done(((bf16[32,88,128]{2,1,0:T(8,128)(2,1)}), bf16[32,88,128]{2,1,0:T(8,128)(2,1)S(1)}, u32[]{:S(2)}, u32[]{:S(2)}) %all-to-all-start.1) | async-done | bytes 720928 | tf_op jit(solution)/shard_map/all_to_all | solution.py:352
  57.9 5.5 %score.1 = bf16[8,4,8,8,128]{4,3,2,1,0:T(8,128)(2,1)} custom-call(bf16[32,88,128]{2,1,0:T(8,128)(2,1)S(1)} %all-to-all-done.1.panel_ref, bf16[2048,2048]{1,0:T(8,128)(2,1)} %align.1.aligned_ref), custom_call_target="tpu_custom_call" | custom-call | flops 1100000000 | bytes 10000000 | tf_op jit(solution)/shard_map/score/pallas_call | solution.py:316
  63.5 6.3 %all-to-all-start.2 = ((bf16[32,64,128]{2,1,0:T(8,128)(2,1)}), bf16[32,64,128]{2,1,0:T(8,128)(2,1)S(1)}, u32[]{:S(2)}, u32[]{:S(2)}) async-start(bf16[32,64,128]{2,1,0:T(8,128)(2,1)} %bitcast.3), calls=%async_computation.2 | async-start | bytes 1048576 | tf_op jit(solution)/shard_map/all_to_all | solution.py:355
  69.9 0.2 slice_reduce_fusion
  70.1 0.1 mul.101
  70.2 0.1 mul.98
  70.3 0.1 eq.18
  70.4 2.8 %fusion.1 = f32[16,128]{1,0:T(8,128)} fusion(f32[16,128]{1,0:T(8,128)S(1)} %convert_reduce_fusion.1, f32[128]{0:T(128)S(1)} %convert_multiply_fusion, f32[1024]{0:T(1024)S(1)} %mul.101, f32[1024]{0:T(1024)S(1)} %mul.98, f32[1024]{0:T(1024)S(1)} %eq.18), kind=kOutput, calls=%fused_computation.2 | convolution fusion | flops 25595904 | bytes 29184 | tf_op jit(solution)/shard_map/dot_general | solution.py:368
  73.2 7.8 %all-to-all-done.2 = bf16[32,64,128]{2,1,0:T(8,128)(2,1)S(1)} async-done(((bf16[32,64,128]{2,1,0:T(8,128)(2,1)}), bf16[32,64,128]{2,1,0:T(8,128)(2,1)S(1)}, u32[]{:S(2)}, u32[]{:S(2)}) %all-to-all-start.2) | async-done | bytes 524320 | tf_op jit(solution)/shard_map/all_to_all | solution.py:355
  81.0 0.7 convert_reduce_fusion
  (3 shorter events, 0.1 us)
Async XLA Ops:
  3.1 13.2 %all-to-all-start = ((bf16[8,168,128]{2,1,0:T(8,128)(2,1)}), bf16[8,168,128]{2,1,0:T(8,128)(2,1)S(1)}, u32[]{:S(2)}, u32[]{:S(2)}) async-start(bf16[8,168,128]{2,1,0:T(8,128)(2,1)} %pack.1), calls=%async_computation | async-start | bytes 688128 | tf_op jit(solution)/shard_map/all_to_all | solution.py:350
  20.5 37.5 %all-to-all-start.1 = ((bf16[32,88,128]{2,1,0:T(8,128)(2,1)}), bf16[32,88,128]{2,1,0:T(8,128)(2,1)S(1)}, u32[]{:S(2)}, u32[]{:S(2)}) async-start(bf16[32,88,128]{2,1,0:T(8,128)(2,1)} %get-tuple-element.5), calls=%async_computation.1 | async-start | bytes 1441792 | tf_op jit(solution)/shard_map/all_to_all | solution.py:352
  63.5 17.5 %all-to-all-start.2 = ((bf16[32,64,128]{2,1,0:T(8,128)(2,1)}), bf16[32,64,128]{2,1,0:T(8,128)(2,1)S(1)}, u32[]{:S(2)}, u32[]{:S(2)}) async-start(bf16[32,64,128]{2,1,0:T(8,128)(2,1)} %bitcast.3), calls=%async_computation.2 | async-start | bytes 1048576 | tf_op jit(solution)/shard_map/all_to_all | solution.py:355

commit v6 on v5

--- a/solution.py
+++ b/solution.py
@@ -13,8 +13,9 @@
 CLASSES = 16
 SEG = 8
 NA = 8
-NB = 32
 NX = 4
+NY = 4
+NZ = 8
 NROW = 4
 SEGS = NA * SEG
 KY = 8
@@ -24,9 +25,11 @@
 A_REF = SEG * D
 A_META = A_REF + 2 * D
 A_ROWS = A_META + META
-B_NUM = NX * D
-B_FACT = B_NUM + CLASSES
-B_ROWS = B_FACT + META
+Y_FACT = NX * 2 * D
+Y_ROWS = Y_FACT + META
+Z_NUM = NX * NY * D
+Z_FACT = Z_NUM + 2 * CLASSES
+Z_ROWS = Z_FACT + META
 FIL = ("x", "yh", "zh", "zl")
 ROW = ("yl", "core")
 bf16 = jnp.bfloat16
@@ -127,9 +130,68 @@
     )(seg_count, *(pltpu.with_memory_space_constraint(v, pltpu.HBM) for v in given))
 
 
-def front_kernel(place_ref, recv_ref, out_ref, meta_out_ref, gx_ref, wide_ref, y_ref, col_ref):
+def chunk_kernel(place_ref, recv_ref, out_ref, wide_ref):
+    zl = place_ref[1]
+    wide_ref[...] = jnp.zeros_like(wide_ref)
+    for x in range(NX):
+        wide_ref[x * SEG : (x + 1) * SEG] = recv_ref[2 * x + zl, A_META:A_ROWS].astype(f32)
+    flat = wide_ref[...].T
+    total = jnp.sum(flat[2 * SHIFTS : 3 * SHIFTS], axis=0, keepdims=True)
+    total_hi = jnp.floor(total * (1.0 / 32))
+    sub = lax.broadcasted_iota(jnp.int32, (META, COLS), 0)
+    facts = jnp.where(sub == 5, total_hi, jnp.where(sub == 6, total - 32.0 * total_hi, flat[96:104]))
+    facts = facts.astype(bf16)
+    for q in range(NY):
+        for x in range(NX):
+            out_ref[q, x * 2 * D : (x + 1) * 2 * D] = recv_ref[2 * x + zl, A_REF : A_REF + 2 * D]
+        out_ref[q, Y_FACT:Y_ROWS] = facts
+
+
+def chunk(place, recv):
+    vmem = pl.BlockSpec(memory_space=pltpu.VMEM)
+    return pl.pallas_call(
+        chunk_kernel,
+        in_specs=[pl.BlockSpec(memory_space=pltpu.SMEM), vmem],
+        out_specs=vmem,
+        out_shape=jax.ShapeDtypeStruct((NY, Y_ROWS, COLS), bf16),
+        scratch_shapes=[pltpu.VMEM((COLS, COLS), f32)],
+        compiler_params=pltpu.CompilerParams(vmem_limit_bytes=4 << 20),
+        cost_estimate=pl.CostEstimate(flops=100_000, bytes_accessed=500_000, transcendentals=0),
+        name="chunk",
+    )(place, recv)
+
+
+def merge_kernel(panel_ref, numer_ref, out_ref):
+    lane = lax.broadcasted_iota(jnp.int32, (META, COLS), 1)
+    facts = jnp.zeros((META, COLS), f32)
+    for y in range(NY):
+        own = jnp.where(lane < NX * SEG, panel_ref[y, Y_FACT:Y_ROWS].astype(f32), 0.0)
+        facts += pltpu.roll(own, y * NX * SEG, 1) if y else own
+    facts = facts.astype(bf16)
+    for q in range(NZ):
+        for y in range(NY):
+            for x in range(NX):
+                base = x * 2 * D + (q % 2) * D
+                out_ref[q, (y * NX + x) * D : (y * NX + x + 1) * D] = panel_ref[y, base : base + D]
+        out_ref[q, Z_NUM:Z_FACT] = numer_ref[q]
+        out_ref[q, Z_FACT:Z_ROWS] = facts
+
+
+def merge(panel, numer):
+    vmem = pl.BlockSpec(memory_space=pltpu.VMEM)
+    return pl.pallas_call(
+        merge_kernel,
+        in_specs=[vmem, vmem],
+        out_specs=vmem,
+        out_shape=jax.ShapeDtypeStruct((NZ, Z_ROWS, COLS), bf16),
+        compiler_params=pltpu.CompilerParams(vmem_limit_bytes=4 << 20),
+        cost_estimate=pl.CostEstimate(flops=100_000, bytes_accessed=1_000_000, transcendentals=0),
+        name="merge",
+    )(panel, numer)
+
+
+def front_kernel(place_ref, recv_ref, numer_ref, meta_out_ref, gx_ref, wide_ref, y_ref, col_ref):
     kw0 = place_ref[0]
-    zl = place_ref[1]
     lane = lax.broadcasted_iota(jnp.int32, (KY, COLS), 1)
     sub = lax.broadcasted_iota(jnp.int32, (KY, COLS), 0)
     kw = (sub + kw0).astype(f32)
@@ -198,21 +260,8 @@
         for ky in range(KY):
             hi, lo = halves(y_ref[pl.ds(p * KY + ky, SEGS, stride=D), :])
             sums = jnp.dot(member, jnp.concatenate([hi, lo], axis=0), preferred_element_type=f32)
-            out_ref[zl * D + 2 * ky + p, B_NUM:B_FACT] = sums.astype(bf16)
-            out_ref[(1 - zl) * D + 2 * ky + p, B_NUM:B_FACT] = jnp.zeros((CLASSES, COLS), bf16)
-
-    for x in range(NX):
-        wide_ref[x * SEG : (x + 1) * SEG] = recv_ref[2 * x + zl, A_META:A_ROWS].astype(f32)
-    flat = wide_ref[...].T
-    total = jnp.sum(flat[2 * SHIFTS : 3 * SHIFTS], axis=0, keepdims=True)
-    total_hi = jnp.floor(total * (1.0 / 32))
-    facts = jnp.where(sub == 5, total_hi, jnp.where(sub == 6, total - 32.0 * total_hi, flat[96:104]))
-    facts = facts.astype(bf16)
-    for q in range(NB):
-        for x in range(NX):
-            base = A_REF + (q % 2) * D
-            out_ref[q, x * D : (x + 1) * D] = recv_ref[2 * x + zl, base : base + D]
-        out_ref[q, B_FACT:B_ROWS] = facts
+            high = ky // 4
+            numer_ref[2 * (ky % 4) + p, high * CLASSES : (high + 1) * CLASSES] = sums.astype(bf16)
 
 
 def front(place, recv):
@@ -222,7 +271,7 @@
         in_specs=[pl.BlockSpec(memory_space=pltpu.SMEM), vmem],
         out_specs=[vmem, vmem, vmem],
         out_shape=[
-            jax.ShapeDtypeStruct((NB, B_ROWS, COLS), bf16),
+            jax.ShapeDtypeStruct((NZ, 2 * CLASSES, COLS), bf16),
             jax.ShapeDtypeStruct((SEGS, COLS), f32),
             jax.ShapeDtypeStruct((SEGS * D, COLS), f32),
         ],
@@ -281,7 +330,7 @@
 
 
 def score_kernel(panel_ref, aligned_ref, out_ref, wide_ref, packed_ref, held_ref, sems):
-    refs = NX * NB
+    refs = NX * NY * NZ
     block = SEG * SHIFTS
     copies = [
         pltpu.make_async_copy(
@@ -292,13 +341,15 @@
     for copy in copies:
         copy.start()
 
-    def widen(q, carry):
-        for x in range(NX):
-            base = pl.multiple_of((x * NB + q) * D, D)
-            wide_ref[pl.ds(base, D), :] = panel_ref[q, x * D : (x + 1) * D, :].astype(f32)
+    def widen(z, carry):
+        for y in range(NY):
+            for x in range(NX):
+                base = pl.multiple_of(((x * NY + y) * NZ + z) * D, D)
+                at = (y * NX + x) * D
+                wide_ref[pl.ds(base, D), :] = panel_ref[z, at : at + D, :].astype(f32)
         return carry
 
-    lax.fori_loop(0, NB, widen, 0)
+    lax.fori_loop(0, NZ, widen, 0)
     for d in range(D):
         packed_ref[d * COLS : (d + 1) * COLS, :] = wide_ref[pl.ds(d, refs, stride=D), :].T.astype(bf16)
 
@@ -311,7 +362,7 @@
 
 
 def score(panel, aligned):
-    refs = NX * NB
+    refs = NX * NY * NZ
     vmem = pl.BlockSpec(memory_space=pltpu.VMEM)
     return pl.pallas_call(
         score_kernel,
@@ -348,17 +399,23 @@
 
     send = pack(images, defocus, references, offsets, posterior, class_ids, seg_count)
     recv = lax.all_to_all(send, ("x", "zl"), 0, 0, tiled=True)
-    sent, meta, gx = front(place, recv)
-    panel = lax.all_to_all(sent, ("yh", "zh", "zl"), 0, 0, tiled=True)
+    panel = lax.all_to_all(chunk(place, recv), "yh", 0, 0, tiled=True)
+    numer, meta, gx = front(place, recv)
+    panel = lax.all_to_all(merge(panel, numer), ("zh", "zl"), 0, 0, tiled=True)
     aligned = align(place, gx, meta)
+
+    numer = panel[:, Z_NUM:Z_FACT].astype(f32).reshape(NZ // 2, 2, 2, CLASSES, COLS)
+    numer = jnp.sum(numer, axis=0).reshape(NY, CLASSES, COLS)
+    numer, panel = lax.optimization_barrier((numer, panel))
+    numer = lax.psum_scatter(numer, "yh", scatter_dimension=0, tiled=True)[0]
+
     partial = score(panel, aligned)
     partial = lax.all_to_all(
         partial.reshape(NA * NROW, SEG * 8, COLS), ("x", "zl", *ROW), 0, 0, tiled=True
     )
     scores = jnp.sum(partial.astype(f32), axis=0).reshape(SEG, 8, COLS)
 
-    numer = jnp.sum(panel[:, B_NUM:B_FACT].astype(f32), axis=0)
-    facts = panel[:, B_FACT:B_ROWS, : NX * SEG].astype(f32)
+    facts = panel[:, Z_FACT:Z_ROWS].astype(f32)
     all_defocus = (facts[:, 0] + facts[:, 1] + facts[:, 2]).reshape(-1)
     all_class = facts[:, 3].reshape(-1)
     all_total = ((facts[:, 5] * 32.0 + facts[:, 6]) * (1.0 / 256)).reshape(-1)

time: 82.1 us -> 116 us (1.41); the launches traced: 81.7 us -> 114 us
  waiting for transfers between devices: 22.9 us -> 37.9 us
  between operations: 1.39 us -> 14.8 us
  starting transfers between devices: 28.5 us -> 30.4 us
  Pallas kernels: 24.9 us -> 26.1 us
    reduce_scatter x0 -> x1, waiting for transfers between devices: none -> 23.3 us  [per_device(): numer = lax.psum_scatter(numer, 'yh', scatter_dimension=0, tiled=True)[0]]
    all_to_all x1, waiting for transfers between devices: 7.78 us -> 0.01 us  [per_device(): lax.all_to_all(partial.reshape(NA * NROW, SEG * 8, COLS), ('x', 'zl', *RO...]
    pallas_call x0 -> x2, Pallas kernels: none -> 2.27 us  [the longest x1 1.3 us: chunk(): pl.pallas_call(chunk_kernel, in_specs=[pl.BlockSpec(memory_space=pltpu.SM...]
    all_to_all x1 -> x2, waiting for transfers between devices: 8.64 us -> 7.44 us  [the longest x1 4.17 us: per_device(): panel = lax.all_to_all(chunk(place, recv), 'yh', 0, 0, tiled=True)]
    all_to_all x1 -> x2, starting transfers between devices: 15.4 us -> 16.6 us  [the longest x1 9.13 us: per_device(): panel = lax.all_to_all(merge(panel, numer), ('zh', 'zl'), 0, 0, tiled=True)]
  transfers between devices with their start and end apart: 3 -> 5, of which waited for: 3 -> 4; matrix products, arithmetic and copies ran while one was open for 4% -> 3% of each run, Pallas kernels for 16% -> 14%
where the time goes in v6:
time: 116 us; the launch traced here: 114 us
  waiting for transfers between devices  37.9 us (33%)
  starting transfers between devices  30.4 us (26%)
  Pallas kernels  26.1 us (22%)
  between operations  14.8 us (13%)
  matrix products  3.52 us (3%)
  other arithmetic  1.43 us (1%)
    reduce_scatter x1, waiting for transfers between devices, per_device(): numer = lax.psum_scatter(numer, 'yh', scatter_dimension=0, tiled=True)[0]  23.3 us
    pallas_call x1, Pallas kernels, align(): pl.pallas_call(align_kernel, grid=(NA,), in_specs=[pl.BlockSpec(memory_sp...  13.4 us
    all_to_all x1, starting transfers between devices, per_device(): panel = lax.all_to_all(merge(panel, numer), ('zh', 'zl'), 0, 0, tiled=True)  9.13 us
    all_to_all x1, starting transfers between devices, per_device(): panel = lax.all_to_all(chunk(place, recv), 'yh', 0, 0, tiled=True)  7.48 us
    all_to_all x1, starting transfers between devices, per_device(): lax.all_to_all(partial.reshape(NA * NROW, SEG * 8, COLS), ('x', 'zl', *RO...  7.12 us
    all_to_all x1, starting transfers between devices, per_device(): recv = lax.all_to_all(send, ('x', 'zl'), 0, 0, tiled=True)  6.67 us
    all_to_all x1, waiting for transfers between devices, per_device(): recv = lax.all_to_all(send, ('x', 'zl'), 0, 0, tiled=True)  6.5 us
    pallas_call x1, Pallas kernels, score(): pl.pallas_call(score_kernel, in_specs=[vmem, pl.BlockSpec(memory_space=pl...  5.55 us
  transfers between devices with their start and end apart: 5, of which 4 were waited for; matrix products, arithmetic and copies ran while one was open for 3% of the time, Pallas kernels for 14%

profile of v6, /device:TPU:1, one launch (start us, length us, event | category | flops | bytes accessed | tf_op | source)
XLA Modules:
  0.0 114.2 jit_solution(6007756828457678037)
XLA Ops:
  7.8 1.8 %pack.1 = bf16[8,168,128]{2,1,0:T(8,128)(2,1)} custom-call(s32[1]{0:T(128)S(6)} %copy.9.refs_0_, f32[8]{0:T(128)} %refs_1_.1, s32[8]{0:T(128)} %refs_2_.1, bf16[8,2,64,128]{3,2,1,0:T(8,128)(2,1)} %refs_3_.1, bf16[1,2,64,128]{3,2,1,0:T(8,128)(2,1)} %refs_4_.1, s32[8,2,32]{2,1,0:T(2,128)} %bitcast.16, s32[8,32]{1,0:T(8,128)} %refs_6_.1), custom_call_target="tpu_custom_call" | custom-call | flops 100000 | bytes 700000 | tf_op jit(solution)/shard_map/pack/pallas_call | solution.py:120
  9.6 6.7 %all-to-all-start = ((bf16[8,168,128]{2,1,0:T(8,128)(2,1)}), bf16[8,168,128]{2,1,0:T(8,128)(2,1)S(1)}, u32[]{:S(2)}, u32[]{:S(2)}) async-start(bf16[8,168,128]{2,1,0:T(8,128)(2,1)} %pack.1), calls=%async_computation | async-start | bytes 688128 | tf_op jit(solution)/shard_map/all_to_all | solution.py:401
  16.3 0.1 pad_add_fusion.place_ref
  16.4 6.5 %all-to-all-done.recv_ref = bf16[8,168,128]{2,1,0:T(8,128)(2,1)S(1)} async-done(((bf16[8,168,128]{2,1,0:T(8,128)(2,1)}), bf16[8,168,128]{2,1,0:T(8,128)(2,1)S(1)}, u32[]{:S(2)}, u32[]{:S(2)}) %all-to-all-start) | async-done | bytes 344096 | tf_op jit(solution)/shard_map/all_to_all | solution.py:401
  22.9 1.3 %chunk.1 = bf16[4,136,128]{2,1,0:T(8,128)(2,1)} custom-call(s32[2]{0:T(128)S(1)} %pad_add_fusion.place_ref, bf16[8,168,128]{2,1,0:T(8,128)(2,1)S(1)} %all-to-all-done.recv_ref), custom_call_target="tpu_custom_call" | custom-call | flops 100000 | bytes 500000 | tf_op jit(solution)/shard_map/chunk/pallas_call | solution.py:152
  24.2 7.5 %all-to-all-start.1 = ((bf16[4,136,128]{2,1,0:T(8,128)(2,1)}), bf16[4,136,128]{2,1,0:T(8,128)(2,1)S(1)}, u32[]{:S(2)}, u32[]{:S(2)}) async-start(bf16[4,136,128]{2,1,0:T(8,128)(2,1)} %chunk.1), calls=%async_computation.1 | async-start | bytes 278528 | tf_op jit(solution)/shard_map/all_to_all | solution.py:402
  31.7 3.1 %front.1 = (bf16[8,32,128]{2,1,0:T(8,128)(2,1)S(1)}, f32[64,128]{1,0:T(8,128)S(1)}, f32[1024,128]{1,0:T(8,128)S(1)}) custom-call(s32[2]{0:T(128)S(1)} %pad_add_fusion.place_ref, bf16[8,168,128]{2,1,0:T(8,128)(2,1)S(1)} %all-to-all-done.recv_ref), custom_call_target="tpu_custom_call" | custom-call | flops 100000000 | bytes 2000000 | tf_op jit(solution)/shard_map/front/pallas_call | solution.py:269
  34.8 4.2 %all-to-all-done.1.panel_ref = bf16[4,136,128]{2,1,0:T(8,128)(2,1)S(1)} async-done(((bf16[4,136,128]{2,1,0:T(8,128)(2,1)}), bf16[4,136,128]{2,1,0:T(8,128)(2,1)S(1)}, u32[]{:S(2)}, u32[]{:S(2)}) %all-to-all-start.1) | async-done | bytes 139296 | tf_op jit(solution)/shard_map/all_to_all | solution.py:402
  39.0 1.0 merge.1
  39.9 9.1 %all-to-all-start.2 = ((bf16[8,296,128]{2,1,0:T(8,128)(2,1)}), bf16[8,296,128]{2,1,0:T(8,128)(2,1)S(1)}, u32[]{:S(2)}, u32[]{:S(2)}) async-start(bf16[8,296,128]{2,1,0:T(8,128)(2,1)} %merge.1), calls=%async_computation.2 | async-start | bytes 1212416 | tf_op jit(solution)/shard_map/all_to_all | solution.py:404
  49.1 13.4 %align.1.aligned_ref = bf16[2048,2048]{1,0:T(8,128)(2,1)} custom-call(s32[2]{0:T(128)S(1)} %pad_add_fusion.place_ref, f32[1024,128]{1,0:T(8,128)S(1)} %get-tuple-element.9.gx_ref, f32[64,128]{1,0:T(8,128)S(1)} %get-tuple-element.10.meta_ref), custom_call_target="tpu_custom_call" | custom-call | flops 600000000 | bytes 9000000 | tf_op jit(solution)/shard_map/align/pallas_call | solution.py:316
  62.4 3.3 %all-to-all-done.2.panel_ref = bf16[8,296,128]{2,1,0:T(8,128)(2,1)S(1)} async-done(((bf16[8,296,128]{2,1,0:T(8,128)(2,1)}), bf16[8,296,128]{2,1,0:T(8,128)(2,1)S(1)}, u32[]{:S(2)}, u32[]{:S(2)}) %all-to-all-start.2) | async-done | bytes 606240 | tf_op jit(solution)/shard_map/all_to_all | solution.py:404
  65.7 0.6 convert_reduce_fusion.1
  66.3 5.5 %score.1 = bf16[8,4,8,8,128]{4,3,2,1,0:T(8,128)(2,1)} custom-call(bf16[8,296,128]{2,1,0:T(8,128)(2,1)S(1)} %all-to-all-done.2.panel_ref, bf16[2048,2048]{1,0:T(8,128)(2,1)} %align.1.aligned_ref), custom_call_target="tpu_custom_call" | custom-call | flops 1100000000 | bytes 10000000 | tf_op jit(solution)/shard_map/score/pallas_call | solution.py:367
  71.9 7.1 %all-to-all-start.3 = ((bf16[32,64,128]{2,1,0:T(8,128)(2,1)}), bf16[32,64,128]{2,1,0:T(8,128)(2,1)S(1)}, u32[]{:S(2)}, u32[]{:S(2)}) async-start(bf16[32,64,128]{2,1,0:T(8,128)(2,1)} %bitcast.5), calls=%async_computation.3 | async-start | bytes 1048576 | tf_op jit(solution)/shard_map/all_to_all | solution.py:413
  79.0 0.0 reduce-scatter.2.cloned.1.call-start
  79.1 0.6 reduce-scatter.2.cloned.1.call-update
  79.8 23.3 %reduce-scatter.2.cloned.1.call-done = f32[1,16,128]{2,1,0:T(8,128)} async-done(((f32[4,16,128]{2,1,0:T(8,128)}), f32[1,16,128]{2,1,0:T(8,128)}) %reduce-scatter.2.cloned.1.call-update) | async-done | bytes 8208 | tf_op jit(solution)/shard_map/reduce_scatter | solution.py:410
  103.1 3.5 %fusion.1 = f32[16,128]{1,0:T(8,128)} fusion(f32[128]{0:T(128)S(1)} %convert_multiply_fusion, f32[1024]{0:T(1024)S(1)} %bitcast.19, f32[1024]{0:T(1024)S(1)} %bitcast.18, f32[1024]{0:T(1024)S(1)} %bitcast.17, f32[1,16,128]{2,1,0:T(8,128)} %reduce-scatter.2.cloned.1.call-done), kind=kOutput, calls=%fused_computation.2 | convolution fusion | flops 25595904 | bytes 29184 | tf_op jit(solution)/shard_map/dot_general | solution.py:425
  106.6 0.0 all-to-all-done.3
  106.6 0.7 convert_reduce_fusion
  (4 shorter events, 0.0 us)
Async XLA Ops:
  9.6 13.2 %all-to-all-start = ((bf16[8,168,128]{2,1,0:T(8,128)(2,1)}), bf16[8,168,128]{2,1,0:T(8,128)(2,1)S(1)}, u32[]{:S(2)}, u32[]{:S(2)}) async-start(bf16[8,168,128]{2,1,0:T(8,128)(2,1)} %pack.1), calls=%async_computation | async-start | bytes 688128 | tf_op jit(solution)/shard_map/all_to_all | solution.py:401
  24.2 14.8 %all-to-all-start.1 = ((bf16[4,136,128]{2,1,0:T(8,128)(2,1)}), bf16[4,136,128]{2,1,0:T(8,128)(2,1)S(1)}, u32[]{:S(2)}, u32[]{:S(2)}) async-start(bf16[4,136,128]{2,1,0:T(8,128)(2,1)} %chunk.1), calls=%async_computation.1 | async-start | bytes 278528 | tf_op jit(solution)/shard_map/all_to_all | solution.py:402
  39.9 25.8 %all-to-all-start.2 = ((bf16[8,296,128]{2,1,0:T(8,128)(2,1)}), bf16[8,296,128]{2,1,0:T(8,128)(2,1)S(1)}, u32[]{:S(2)}, u32[]{:S(2)}) async-start(bf16[8,296,128]{2,1,0:T(8,128)(2,1)} %merge.1), calls=%async_computation.2 | async-start | bytes 1212416 | tf_op jit(solution)/shard_map/all_to_all | solution.py:404
  71.9 34.7 %all-to-all-start.3 = ((bf16[32,64,128]{2,1,0:T(8,128)(2,1)}), bf16[32,64,128]{2,1,0:T(8,128)(2,1)S(1)}, u32[]{:S(2)}, u32[]{:S(2)}) async-start(bf16[32,64,128]{2,1,0:T(8,128)(2,1)} %bitcast.5), calls=%async_computation.3 | async-start | bytes 1048576 | tf_op jit(solution)/shard_map/all_to_all | solution.py:413
  79.0 24.1 %reduce-scatter.2.cloned.1.call-start = ((), (), s32[]{:S(2)}) async-start(), calls=%async_computation.5 | async-start | bytes 40960 | tf_op jit(solution)/shard_map/reduce_scatter | solution.py:410
Sparse Core Ops, SparseCore 0:
  83.2 19.8 reduce-scatter.1

commit v7 on v5

--- a/solution.py
+++ b/solution.py
@@ -1,3 +1,4 @@
+import functools
 import math
 
 import jax
@@ -25,12 +26,12 @@
 A_META = A_REF + 2 * D
 A_ROWS = A_META + META
 B_NUM = NX * D
-B_FACT = B_NUM + CLASSES
-B_ROWS = B_FACT + META
+B_ROWS = B_NUM + CLASSES
 FIL = ("x", "yh", "zh", "zl")
 ROW = ("yl", "core")
 bf16 = jnp.bfloat16
 f32 = jnp.float32
+NEAR = 2
 PARTIAL = bf16
 
 
@@ -198,21 +199,19 @@
         for ky in range(KY):
             hi, lo = halves(y_ref[pl.ds(p * KY + ky, SEGS, stride=D), :])
             sums = jnp.dot(member, jnp.concatenate([hi, lo], axis=0), preferred_element_type=f32)
-            out_ref[zl * D + 2 * ky + p, B_NUM:B_FACT] = sums.astype(bf16)
-            out_ref[(1 - zl) * D + 2 * ky + p, B_NUM:B_FACT] = jnp.zeros((CLASSES, COLS), bf16)
-
-    for x in range(NX):
-        wide_ref[x * SEG : (x + 1) * SEG] = recv_ref[2 * x + zl, A_META:A_ROWS].astype(f32)
-    flat = wide_ref[...].T
+            out_ref[zl * D + 2 * ky + p, B_NUM:B_ROWS] = sums.astype(bf16)
+
     total = jnp.sum(flat[2 * SHIFTS : 3 * SHIFTS], axis=0, keepdims=True)
     total_hi = jnp.floor(total * (1.0 / 32))
     facts = jnp.where(sub == 5, total_hi, jnp.where(sub == 6, total - 32.0 * total_hi, flat[96:104]))
-    facts = facts.astype(bf16)
-    for q in range(NB):
-        for x in range(NX):
-            base = A_REF + (q % 2) * D
-            out_ref[q, x * D : (x + 1) * D] = recv_ref[2 * x + zl, base : base + D]
-        out_ref[q, B_FACT:B_ROWS] = facts
+    facts = jnp.concatenate([facts, jnp.zeros((CLASSES - META, COLS), f32)], axis=0).astype(bf16)
+    for q in range(D):
+        out_ref[(1 - zl) * D + q, B_NUM:B_ROWS] = facts
+    for half in range(2):
+        refs = [recv_ref[2 * x + zl, A_REF + half * D : A_REF + (half + 1) * D] for x in range(NX)]
+        for q in range(half, NB, 2):
+            for x in range(NX):
+                out_ref[q, x * D : (x + 1) * D] = refs[x]
 
 
 def front(place, recv):
@@ -237,13 +236,14 @@
     )(place, recv)
 
 
-def align_kernel(place_ref, gx_ref, meta_ref, aligned_ref):
+def align_kernel(place_ref, gx_ref, meta_ref, near_ref, far_ref):
+    step = pl.program_id(0)
     kw0 = place_ref[0].astype(f32)
     lane = lax.broadcasted_iota(jnp.int32, (SHIFTS, COLS), 1)
     sub = lax.broadcasted_iota(jnp.int32, (SHIFTS, COLS), 0)
     kx = lane.astype(f32)
 
-    def segment(i, carry):
+    def segment(aligned_ref, i, carry):
         wide = jnp.broadcast_to(meta_ref[pl.ds(i, 1), :], (SHIFTS, COLS))
         sy = jnp.sum(jnp.where(lane == sub, wide, 0.0), axis=1, keepdims=True)
         sx = jnp.sum(jnp.where(lane == sub + SHIFTS, wide, 0.0), axis=1, keepdims=True)
@@ -260,7 +260,13 @@
                 pr, pi = pr * cr - pi * si, pr * si + pi * cr
         return carry
 
-    lax.fori_loop(0, SEG, segment, 0)
+    @pl.when(step < NEAR)
+    def _():
+        lax.fori_loop(0, SEG, functools.partial(segment, near_ref), 0)
+
+    @pl.when(step >= NEAR)
+    def _():
+        lax.fori_loop(0, SEG, functools.partial(segment, far_ref), 0)
 
 
 def align(place, gx, meta):
@@ -272,22 +278,28 @@
             pl.BlockSpec((SEG * D, COLS), lambda j: (j, 0)),
             pl.BlockSpec((SEG, COLS), lambda j: (j, 0)),
         ],
-        out_specs=pl.BlockSpec((SEG * SHIFTS, D * COLS), lambda j: (j, 0)),
-        out_shape=pltpu.HBM((SEGS * SHIFTS, D * COLS), bf16),
+        out_specs=[
+            pl.BlockSpec((SEG * SHIFTS, D * COLS), lambda j: (jnp.minimum(j, NEAR - 1), 0)),
+            pl.BlockSpec((SEG * SHIFTS, D * COLS), lambda j: (jnp.maximum(j - NEAR, 0), 0)),
+        ],
+        out_shape=[
+            jax.ShapeDtypeStruct((NEAR * SEG * SHIFTS, D * COLS), bf16),
+            pltpu.HBM(((NA - NEAR) * SEG * SHIFTS, D * COLS), bf16),
+        ],
         compiler_params=pltpu.CompilerParams(vmem_limit_bytes=10 << 20),
         cost_estimate=pl.CostEstimate(flops=600_000_000, bytes_accessed=9_000_000, transcendentals=0),
         name="align",
     )(place, gx, meta)
 
 
-def score_kernel(panel_ref, aligned_ref, out_ref, wide_ref, packed_ref, held_ref, sems):
+def score_kernel(panel_ref, near_ref, far_ref, out_ref, wide_ref, packed_ref, held_ref, sems):
     refs = NX * NB
     block = SEG * SHIFTS
     copies = [
         pltpu.make_async_copy(
-            aligned_ref.at[j * block : (j + 1) * block], held_ref.at[j * block : (j + 1) * block], sems.at[j]
+            far_ref.at[j * block : (j + 1) * block], held_ref.at[j * block : (j + 1) * block], sems.at[j]
         )
-        for j in range(NA)
+        for j in range(NA - NEAR)
     ]
     for copy in copies:
         copy.start()
@@ -303,31 +315,35 @@
         packed_ref[d * COLS : (d + 1) * COLS, :] = wide_ref[pl.ds(d, refs, stride=D), :].T.astype(bf16)
 
     for j in range(NA):
-        copies[j].wait()
-        res = jnp.dot(held_ref[j * block : (j + 1) * block], packed_ref[...], preferred_element_type=f32)
+        if j < NEAR:
+            left = near_ref[j * block : (j + 1) * block]
+        else:
+            copies[j - NEAR].wait()
+            left = held_ref[(j - NEAR) * block : (j - NEAR + 1) * block]
+        res = jnp.dot(left, packed_ref[...], preferred_element_type=f32)
         for i in range(SEG):
             for r in range(NROW):
                 out_ref[j, r, i] = res[i * SHIFTS + r * 8 : i * SHIFTS + (r + 1) * 8, :].astype(out_ref.dtype)
 
 
-def score(panel, aligned):
+def score(panel, near, far):
     refs = NX * NB
     vmem = pl.BlockSpec(memory_space=pltpu.VMEM)
     return pl.pallas_call(
         score_kernel,
-        in_specs=[vmem, pl.BlockSpec(memory_space=pltpu.HBM)],
+        in_specs=[vmem, vmem, pl.BlockSpec(memory_space=pltpu.HBM)],
         out_specs=vmem,
         out_shape=jax.ShapeDtypeStruct((NA, NROW, SEG, 8, refs), PARTIAL),
         scratch_shapes=[
             pltpu.VMEM((refs * D, COLS), f32),
             pltpu.VMEM((D * COLS, refs), bf16),
-            pltpu.VMEM(aligned.shape, bf16),
-            pltpu.SemaphoreType.DMA((NA,)),
+            pltpu.VMEM(far.shape, bf16),
+            pltpu.SemaphoreType.DMA((NA - NEAR,)),
         ],
         compiler_params=pltpu.CompilerParams(vmem_limit_bytes=20 << 20),
         cost_estimate=pl.CostEstimate(flops=1_100_000_000, bytes_accessed=10_000_000, transcendentals=0),
         name="score",
-    )(panel, pltpu.with_memory_space_constraint(aligned, pltpu.HBM))
+    )(panel, near, pltpu.with_memory_space_constraint(far, pltpu.HBM))
 
 
 def contrast(defocus, kw, kx):
@@ -350,15 +366,18 @@
     recv = lax.all_to_all(send, ("x", "zl"), 0, 0, tiled=True)
     sent, meta, gx = front(place, recv)
     panel = lax.all_to_all(sent, ("yh", "zh", "zl"), 0, 0, tiled=True)
-    aligned = align(place, gx, meta)
-    partial = score(panel, aligned)
+    near, far = align(place, gx, meta)
+    partial = score(panel, near, far)
     partial = lax.all_to_all(
         partial.reshape(NA * NROW, SEG * 8, COLS), ("x", "zl", *ROW), 0, 0, tiled=True
     )
     scores = jnp.sum(partial.astype(f32), axis=0).reshape(SEG, 8, COLS)
 
-    numer = jnp.sum(panel[:, B_NUM:B_FACT].astype(f32), axis=0)
-    facts = panel[:, B_FACT:B_ROWS, : NX * SEG].astype(f32)
+    owner = lax.axis_index("yh") // 2
+    rest = panel[:, B_NUM:B_ROWS].reshape(NB // 2, 2, CLASSES, COLS)
+    numer = jnp.where(owner == 0, rest[:, 0], rest[:, 1]).astype(f32)
+    numer = jnp.sum(numer, axis=0)
+    facts = jnp.where(owner == 0, rest[:, 1, :, :SEGS], rest[:, 0, :, :SEGS]).astype(f32)
     all_defocus = (facts[:, 0] + facts[:, 1] + facts[:, 2]).reshape(-1)
     all_class = facts[:, 3].reshape(-1)
     all_total = ((facts[:, 5] * 32.0 + facts[:, 6]) * (1.0 / 256)).reshape(-1)

time: 82.1 us -> 79.8 us (0.972)
  waiting for transfers between devices: 22.9 us -> 21.5 us
  Pallas kernels: 24.9 us -> 23.9 us
    all_to_all x1, waiting for transfers between devices: 8.64 us -> 7.1 us  [per_device(): panel = lax.all_to_all(sent, ('yh', 'zh', 'zl'), 0, 0, tiled=True)]
    pallas_call x1, Pallas kernels: 5.54 us -> 4.64 us  [score(): pl.pallas_call(score_kernel, in_specs=[vmem, vmem, pl.BlockSpec(memory_sp...]
  transfers between devices with their start and end apart: 3 -> 3, of which waited for: 3 -> 3; matrix products, arithmetic and copies ran while one was open for 4% -> 4% of each run, Pallas kernels for 16% -> 17%
where the time goes in v7:
time: 79.8 us; the launch traced here: 79.4 us
  starting transfers between devices  28.6 us (36%)
  Pallas kernels  23.9 us (30%)
  waiting for transfers between devices  21.5 us (27%)
  matrix products  2.83 us (4%)
  between operations  1.4 us (2%)
  other arithmetic  0.92 us (1%)
    all_to_all x1, starting transfers between devices, per_device(): panel = lax.all_to_all(sent, ('yh', 'zh', 'zl'), 0, 0, tiled=True)  15.4 us
    pallas_call x1, Pallas kernels, align(): pl.pallas_call(align_kernel, grid=(NA,), in_specs=[pl.BlockSpec(memory_sp...  13.4 us
    all_to_all x1, waiting for transfers between devices, per_device(): lax.all_to_all(partial.reshape(NA * NROW, SEG * 8, COLS), ('x', 'zl', *RO...  7.86 us
    all_to_all x1, waiting for transfers between devices, per_device(): panel = lax.all_to_all(sent, ('yh', 'zh', 'zl'), 0, 0, tiled=True)  7.1 us
    all_to_all x1, starting transfers between devices, per_device(): recv = lax.all_to_all(send, ('x', 'zl'), 0, 0, tiled=True)  6.67 us
    all_to_all x1, starting transfers between devices, per_device(): lax.all_to_all(partial.reshape(NA * NROW, SEG * 8, COLS), ('x', 'zl', *RO...  6.53 us
    all_to_all x1, waiting for transfers between devices, per_device(): recv = lax.all_to_all(send, ('x', 'zl'), 0, 0, tiled=True)  6.5 us
    pallas_call x1, Pallas kernels, score(): pl.pallas_call(score_kernel, in_specs=[vmem, vmem, pl.BlockSpec(memory_sp...  4.64 us
  transfers between devices with their start and end apart: 3, of which 3 were waited for; matrix products, arithmetic and copies ran while one was open for 4% of the time, Pallas kernels for 17%

profile of v7, /device:TPU:1, one launch (start us, length us, event | category | flops | bytes accessed | tf_op | source)
XLA Modules:
  0.0 79.4 jit_solution(641488802154344170)
XLA Ops:
  1.3 1.8 %pack.1 = bf16[8,168,128]{2,1,0:T(8,128)(2,1)} custom-call(s32[1]{0:T(128)S(6)} %copy.9.refs_0_, f32[8]{0:T(128)} %refs_1_.1, s32[8]{0:T(128)} %refs_2_.1, bf16[8,2,64,128]{3,2,1,0:T(8,128)(2,1)} %refs_3_.1, bf16[1,2,64,128]{3,2,1,0:T(8,128)(2,1)} %refs_4_.1, s32[8,2,32]{2,1,0:T(2,128)} %bitcast.14, s32[8,32]{1,0:T(8,128)} %refs_6_.1), custom_call_target="tpu_custom_call" | custom-call | flops 100000 | bytes 700000 | tf_op jit(solution)/shard_map/pack/pallas_call | solution.py:118
  3.1 6.7 %all-to-all-start = ((bf16[8,168,128]{2,1,0:T(8,128)(2,1)}), bf16[8,168,128]{2,1,0:T(8,128)(2,1)S(1)}, u32[]{:S(2)}, u32[]{:S(2)}) async-start(bf16[8,168,128]{2,1,0:T(8,128)(2,1)} %pack.1), calls=%async_computation | async-start | bytes 688128 | tf_op jit(solution)/shard_map/all_to_all | solution.py:366
  9.8 0.1 pad_add_fusion.place_ref
  9.8 6.5 %all-to-all-done.recv_ref = bf16[8,168,128]{2,1,0:T(8,128)(2,1)S(1)} async-done(((bf16[8,168,128]{2,1,0:T(8,128)(2,1)}), bf16[8,168,128]{2,1,0:T(8,128)(2,1)S(1)}, u32[]{:S(2)}, u32[]{:S(2)}) %all-to-all-start) | async-done | bytes 344096 | tf_op jit(solution)/shard_map/all_to_all | solution.py:366
  16.3 4.1 %front.1 = (bf16[32,80,128]{2,1,0:T(8,128)(2,1)}, f32[64,128]{1,0:T(8,128)S(1)}, f32[1024,128]{1,0:T(8,128)S(1)}) custom-call(s32[2]{0:T(128)S(1)} %pad_add_fusion.place_ref, bf16[8,168,128]{2,1,0:T(8,128)(2,1)S(1)} %all-to-all-done.recv_ref), custom_call_target="tpu_custom_call" | custom-call | flops 100000000 | bytes 2000000 | tf_op jit(solution)/shard_map/front/pallas_call | solution.py:219
  20.4 15.4 %all-to-all-start.1 = ((bf16[32,80,128]{2,1,0:T(8,128)(2,1)}), bf16[32,80,128]{2,1,0:T(8,128)(2,1)S(1)}, u32[]{:S(2)}, u32[]{:S(2)}) async-start(bf16[32,80,128]{2,1,0:T(8,128)(2,1)} %get-tuple-element.7), calls=%async_computation.1 | async-start | bytes 1310720 | tf_op jit(solution)/shard_map/all_to_all | solution.py:368
  35.9 13.4 %align.1 = (bf16[512,2048]{1,0:T(8,128)(2,1)S(1)}, bf16[1536,2048]{1,0:T(8,128)(2,1)}) custom-call(s32[2]{0:T(128)S(1)} %pad_add_fusion.place_ref, f32[1024,128]{1,0:T(8,128)S(1)} %get-tuple-element.8.gx_ref, f32[64,128]{1,0:T(8,128)S(1)} %get-tuple-element.9.meta_ref), custom_call_target="tpu_custom_call" | custom-call | flops 600000000 | bytes 9000000 | tf_op jit(solution)/shard_map/align/pallas_call | solution.py:273
  49.3 7.1 %all-to-all-done.1.panel_ref = bf16[32,80,128]{2,1,0:T(8,128)(2,1)S(1)} async-done(((bf16[32,80,128]{2,1,0:T(8,128)(2,1)}), bf16[32,80,128]{2,1,0:T(8,128)(2,1)S(1)}, u32[]{:S(2)}, u32[]{:S(2)}) %all-to-all-start.1) | async-done | bytes 655392 | tf_op jit(solution)/shard_map/all_to_all | solution.py:368
  56.4 4.6 %score.1 = bf16[8,4,8,8,128]{4,3,2,1,0:T(8,128)(2,1)} custom-call(bf16[32,80,128]{2,1,0:T(8,128)(2,1)S(1)} %all-to-all-done.1.panel_ref, bf16[512,2048]{1,0:T(8,128)(2,1)S(1)} %get-tuple-element.10.near_ref, bf16[1536,2048]{1,0:T(8,128)(2,1)} %get-tuple-element.11.far_ref), custom_call_target="tpu_custom_call" | custom-call | flops 1100000000 | bytes 10000000 | tf_op jit(solution)/shard_map/score/pallas_call | solution.py:332
  61.0 6.5 %all-to-all-start.2 = ((bf16[32,64,128]{2,1,0:T(8,128)(2,1)}), bf16[32,64,128]{2,1,0:T(8,128)(2,1)S(1)}, u32[]{:S(2)}, u32[]{:S(2)}) async-start(bf16[32,64,128]{2,1,0:T(8,128)(2,1)} %bitcast.3), calls=%async_computation.2 | async-start | bytes 1048576 | tf_op jit(solution)/shard_map/all_to_all | solution.py:371
  67.7 0.1 slice_reduce_fusion
  67.8 0.1 mul.101
  67.9 0.1 mul.98
  67.9 0.1 eq.23
  68.0 2.8 %fusion.1 = f32[16,128]{1,0:T(8,128)} fusion(f32[16,128]{1,0:T(8,128)S(1)} %convert_reduce_fusion.1, f32[128]{0:T(128)S(1)} %convert_multiply_fusion, f32[1024]{0:T(1024)S(1)} %mul.101, f32[1024]{0:T(1024)S(1)} %mul.98, f32[1024]{0:T(1024)S(1)} %eq.23), kind=kOutput, calls=%fused_computation.2 | convolution fusion | flops 25595904 | bytes 29184 | tf_op jit(solution)/shard_map/dot_general | solution.py:387
  70.8 7.9 %all-to-all-done.2 = bf16[32,64,128]{2,1,0:T(8,128)(2,1)S(1)} async-done(((bf16[32,64,128]{2,1,0:T(8,128)(2,1)}), bf16[32,64,128]{2,1,0:T(8,128)(2,1)S(1)}, u32[]{:S(2)}, u32[]{:S(2)}) %all-to-all-start.2) | async-done | bytes 524320 | tf_op jit(solution)/shard_map/all_to_all | solution.py:371
  78.7 0.7 convert_reduce_fusion
  (4 shorter events, 0.1 us)
Async XLA Ops:
  3.1 13.2 %all-to-all-start = ((bf16[8,168,128]{2,1,0:T(8,128)(2,1)}), bf16[8,168,128]{2,1,0:T(8,128)(2,1)S(1)}, u32[]{:S(2)}, u32[]{:S(2)}) async-start(bf16[8,168,128]{2,1,0:T(8,128)(2,1)} %pack.1), calls=%async_computation | async-start | bytes 688128 | tf_op jit(solution)/shard_map/all_to_all | solution.py:366
  20.4 36.0 %all-to-all-start.1 = ((bf16[32,80,128]{2,1,0:T(8,128)(2,1)}), bf16[32,80,128]{2,1,0:T(8,128)(2,1)S(1)}, u32[]{:S(2)}, u32[]{:S(2)}) async-start(bf16[32,80,128]{2,1,0:T(8,128)(2,1)} %get-tuple-element.7), calls=%async_computation.1 | async-start | bytes 1310720 | tf_op jit(solution)/shard_map/all_to_all | solution.py:368
  61.0 17.7 %all-to-all-start.2 = ((bf16[32,64,128]{2,1,0:T(8,128)(2,1)}), bf16[32,64,128]{2,1,0:T(8,128)(2,1)S(1)}, u32[]{:S(2)}, u32[]{:S(2)}) async-start(bf16[32,64,128]{2,1,0:T(8,128)(2,1)} %bitcast.3), calls=%async_computation.2 | async-start | bytes 1048576 | tf_op jit(solution)/shard_map/all_to_all | solution.py:371

commit v8 on v7

--- a/solution.py
+++ b/solution.py
@@ -227,7 +227,7 @@
         ],
         scratch_shapes=[
             pltpu.VMEM((COLS, COLS), f32),
-            pltpu.VMEM((SEGS * D, COLS), f32),
+            pltpu.VMEM((SEGS * D + D, COLS), f32),
             pltpu.VMEM((SEG * SHIFTS, 4 * COLS), bf16),
         ],
         compiler_params=pltpu.CompilerParams(vmem_limit_bytes=8 << 20),
@@ -292,7 +292,7 @@
     )(place, gx, meta)
 
 
-def score_kernel(panel_ref, near_ref, far_ref, out_ref, wide_ref, packed_ref, held_ref, sems):
+def score_kernel(panel_ref, near_ref, far_ref, out_ref, wide_ref, packed_ref, held_ref, made_ref, sems, out_sems):
     refs = NX * NB
     block = SEG * SHIFTS
     copies = [
@@ -314,6 +314,7 @@
     for d in range(D):
         packed_ref[d * COLS : (d + 1) * COLS, :] = wide_ref[pl.ds(d, refs, stride=D), :].T.astype(bf16)
 
+    done = []
     for j in range(NA):
         if j < NEAR:
             left = near_ref[j * block : (j + 1) * block]
@@ -323,7 +324,11 @@
         res = jnp.dot(left, packed_ref[...], preferred_element_type=f32)
         for i in range(SEG):
             for r in range(NROW):
-                out_ref[j, r, i] = res[i * SHIFTS + r * 8 : i * SHIFTS + (r + 1) * 8, :].astype(out_ref.dtype)
+                made_ref[j, r, i] = res[i * SHIFTS + r * 8 : i * SHIFTS + (r + 1) * 8, :].astype(out_ref.dtype)
+        done.append(pltpu.make_async_copy(made_ref.at[j], out_ref.at[j], out_sems.at[j]))
+        done[-1].start()
+    for copy in done:
+        copy.wait()
 
 
 def score(panel, near, far):
@@ -332,13 +337,15 @@
     return pl.pallas_call(
         score_kernel,
         in_specs=[vmem, vmem, pl.BlockSpec(memory_space=pltpu.HBM)],
-        out_specs=vmem,
-        out_shape=jax.ShapeDtypeStruct((NA, NROW, SEG, 8, refs), PARTIAL),
+        out_specs=pl.BlockSpec(memory_space=pltpu.HBM),
+        out_shape=pltpu.HBM((NA, NROW, SEG, 8, refs), PARTIAL),
         scratch_shapes=[
-            pltpu.VMEM((refs * D, COLS), f32),
+            pltpu.VMEM((refs * D + D, COLS), f32),
             pltpu.VMEM((D * COLS, refs), bf16),
             pltpu.VMEM(far.shape, bf16),
+            pltpu.VMEM((NA, NROW, SEG, 8, refs), PARTIAL),
             pltpu.SemaphoreType.DMA((NA - NEAR,)),
+            pltpu.SemaphoreType.DMA((NA,)),
         ],
         compiler_params=pltpu.CompilerParams(vmem_limit_bytes=20 << 20),
         cost_estimate=pl.CostEstimate(flops=1_100_000_000, bytes_accessed=10_000_000, transcendentals=0),

time: 79.8 us -> 79.7 us (level)
  no operation moved by 1% of the time
where the time goes in v8:
time: 79.7 us; the launch traced here: 79.3 us
  starting transfers between devices  28.6 us (36%)
  Pallas kernels  23.8 us (30%)
  waiting for transfers between devices  21.5 us (27%)
  matrix products  2.83 us (4%)
  between operations  1.4 us (2%)
  other arithmetic  0.92 us (1%)
    all_to_all x1, starting transfers between devices, per_device(): panel = lax.all_to_all(sent, ('yh', 'zh', 'zl'), 0, 0, tiled=True)  15.4 us
    pallas_call x1, Pallas kernels, align(): pl.pallas_call(align_kernel, grid=(NA,), in_specs=[pl.BlockSpec(memory_sp...  13.4 us
    all_to_all x1, waiting for transfers between devices, per_device(): lax.all_to_all(partial.reshape(NA * NROW, SEG * 8, COLS), ('x', 'zl', *RO...  7.86 us
    all_to_all x1, waiting for transfers between devices, per_device(): panel = lax.all_to_all(sent, ('yh', 'zh', 'zl'), 0, 0, tiled=True)  7.11 us
    all_to_all x1, starting transfers between devices, per_device(): recv = lax.all_to_all(send, ('x', 'zl'), 0, 0, tiled=True)  6.67 us
    all_to_all x1, starting transfers between devices, per_device(): lax.all_to_all(partial.reshape(NA * NROW, SEG * 8, COLS), ('x', 'zl', *RO...  6.51 us
    all_to_all x1, waiting for transfers between devices, per_device(): recv = lax.all_to_all(send, ('x', 'zl'), 0, 0, tiled=True)  6.5 us
    pallas_call x1, Pallas kernels, score(): pl.pallas_call(score_kernel, in_specs=[vmem, vmem, pl.BlockSpec(memory_sp...  4.52 us
  transfers between devices with their start and end apart: 3, of which 3 were waited for; matrix products, arithmetic and copies ran while one was open for 4% of the time, Pallas kernels for 17%

profile of v8, /device:TPU:1, one launch (start us, length us, event | category | flops | bytes accessed | tf_op | source)
XLA Modules:
  0.0 79.3 jit_solution(8653221604369725815)
XLA Ops:
  1.3 1.8 %pack.1 = bf16[8,168,128]{2,1,0:T(8,128)(2,1)} custom-call(s32[1]{0:T(128)S(6)} %copy.9.refs_0_, f32[8]{0:T(128)} %refs_1_.1, s32[8]{0:T(128)} %refs_2_.1, bf16[8,2,64,128]{3,2,1,0:T(8,128)(2,1)} %refs_3_.1, bf16[1,2,64,128]{3,2,1,0:T(8,128)(2,1)} %refs_4_.1, s32[8,2,32]{2,1,0:T(2,128)} %bitcast.15, s32[8,32]{1,0:T(8,128)} %refs_6_.1), custom_call_target="tpu_custom_call" | custom-call | flops 100000 | bytes 700000 | tf_op jit(solution)/shard_map/pack/pallas_call | solution.py:118
  3.1 6.7 %all-to-all-start = ((bf16[8,168,128]{2,1,0:T(8,128)(2,1)}), bf16[8,168,128]{2,1,0:T(8,128)(2,1)S(1)}, u32[]{:S(2)}, u32[]{:S(2)}) async-start(bf16[8,168,128]{2,1,0:T(8,128)(2,1)} %pack.1), calls=%async_computation | async-start | bytes 688128 | tf_op jit(solution)/shard_map/all_to_all | solution.py:373
  9.8 0.1 pad_add_fusion.place_ref
  9.8 6.5 %all-to-all-done.recv_ref = bf16[8,168,128]{2,1,0:T(8,128)(2,1)S(1)} async-done(((bf16[8,168,128]{2,1,0:T(8,128)(2,1)}), bf16[8,168,128]{2,1,0:T(8,128)(2,1)S(1)}, u32[]{:S(2)}, u32[]{:S(2)}) %all-to-all-start) | async-done | bytes 344096 | tf_op jit(solution)/shard_map/all_to_all | solution.py:373
  16.3 4.1 %front.1 = (bf16[32,80,128]{2,1,0:T(8,128)(2,1)}, f32[64,128]{1,0:T(8,128)S(1)}, f32[1024,128]{1,0:T(8,128)S(1)}) custom-call(s32[2]{0:T(128)S(1)} %pad_add_fusion.place_ref, bf16[8,168,128]{2,1,0:T(8,128)(2,1)S(1)} %all-to-all-done.recv_ref), custom_call_target="tpu_custom_call" | custom-call | flops 100000000 | bytes 2000000 | tf_op jit(solution)/shard_map/front/pallas_call | solution.py:219
  20.4 15.4 %all-to-all-start.1 = ((bf16[32,80,128]{2,1,0:T(8,128)(2,1)}), bf16[32,80,128]{2,1,0:T(8,128)(2,1)S(1)}, u32[]{:S(2)}, u32[]{:S(2)}) async-start(bf16[32,80,128]{2,1,0:T(8,128)(2,1)} %get-tuple-element.7), calls=%async_computation.1 | async-start | bytes 1310720 | tf_op jit(solution)/shard_map/all_to_all | solution.py:375
  35.9 13.4 %align.1 = (bf16[512,2048]{1,0:T(8,128)(2,1)S(1)}, bf16[1536,2048]{1,0:T(8,128)(2,1)}) custom-call(s32[2]{0:T(128)S(1)} %pad_add_fusion.place_ref, f32[1024,128]{1,0:T(8,128)S(1)} %get-tuple-element.8.gx_ref, f32[64,128]{1,0:T(8,128)S(1)} %get-tuple-element.9.meta_ref), custom_call_target="tpu_custom_call" | custom-call | flops 600000000 | bytes 9000000 | tf_op jit(solution)/shard_map/align/pallas_call | solution.py:273
  49.3 7.1 %all-to-all-done.1.panel_ref = bf16[32,80,128]{2,1,0:T(8,128)(2,1)S(1)} async-done(((bf16[32,80,128]{2,1,0:T(8,128)(2,1)}), bf16[32,80,128]{2,1,0:T(8,128)(2,1)S(1)}, u32[]{:S(2)}, u32[]{:S(2)}) %all-to-all-start.1) | async-done | bytes 655392 | tf_op jit(solution)/shard_map/all_to_all | solution.py:375
  56.4 4.5 %score.1 = bf16[8,4,8,8,128]{4,3,2,1,0:T(8,128)(2,1)} custom-call(bf16[32,80,128]{2,1,0:T(8,128)(2,1)S(1)} %all-to-all-done.1.panel_ref, bf16[512,2048]{1,0:T(8,128)(2,1)S(1)} %get-tuple-element.10.near_ref, bf16[1536,2048]{1,0:T(8,128)(2,1)} %get-tuple-element.11.far_ref), custom_call_target="tpu_custom_call" | custom-call | flops 1100000000 | bytes 10000000 | tf_op jit(solution)/shard_map/score/pallas_call | solution.py:337
  60.9 6.5 %all-to-all-start.2 = ((bf16[32,64,128]{2,1,0:T(8,128)(2,1)}), bf16[32,64,128]{2,1,0:T(8,128)(2,1)S(1)}, u32[]{:S(2)}, u32[]{:S(2)}) async-start(bf16[32,64,128]{2,1,0:T(8,128)(2,1)} %bitcast.11), calls=%async_computation.2 | async-start | bytes 1048576 | tf_op jit(solution)/shard_map/all_to_all | solution.py:378
  67.5 0.1 slice_reduce_fusion
  67.7 0.1 mul.101
  67.7 0.1 mul.98
  67.8 0.1 eq.23
  67.9 2.8 %fusion.1 = f32[16,128]{1,0:T(8,128)} fusion(f32[16,128]{1,0:T(8,128)S(1)} %convert_reduce_fusion.1, f32[128]{0:T(128)S(1)} %convert_multiply_fusion, f32[1024]{0:T(1024)S(1)} %mul.101, f32[1024]{0:T(1024)S(1)} %mul.98, f32[1024]{0:T(1024)S(1)} %eq.23), kind=kOutput, calls=%fused_computation.2 | convolution fusion | flops 25595904 | bytes 29184 | tf_op jit(solution)/shard_map/dot_general | solution.py:394
  70.7 7.9 %all-to-all-done.2 = bf16[32,64,128]{2,1,0:T(8,128)(2,1)S(1)} async-done(((bf16[32,64,128]{2,1,0:T(8,128)(2,1)}), bf16[32,64,128]{2,1,0:T(8,128)(2,1)S(1)}, u32[]{:S(2)}, u32[]{:S(2)}) %all-to-all-start.2) | async-done | bytes 524320 | tf_op jit(solution)/shard_map/all_to_all | solution.py:378
  78.6 0.7 convert_reduce_fusion
  (4 shorter events, 0.1 us)
Async XLA Ops:
  3.1 13.2 %all-to-all-start = ((bf16[8,168,128]{2,1,0:T(8,128)(2,1)}), bf16[8,168,128]{2,1,0:T(8,128)(2,1)S(1)}, u32[]{:S(2)}, u32[]{:S(2)}) async-start(bf16[8,168,128]{2,1,0:T(8,128)(2,1)} %pack.1), calls=%async_computation | async-start | bytes 688128 | tf_op jit(solution)/shard_map/all_to_all | solution.py:373
  20.4 36.0 %all-to-all-start.1 = ((bf16[32,80,128]{2,1,0:T(8,128)(2,1)}), bf16[32,80,128]{2,1,0:T(8,128)(2,1)S(1)}, u32[]{:S(2)}, u32[]{:S(2)}) async-start(bf16[32,80,128]{2,1,0:T(8,128)(2,1)} %get-tuple-element.7), calls=%async_computation.1 | async-start | bytes 1310720 | tf_op jit(solution)/shard_map/all_to_all | solution.py:375
  60.9 17.7 %all-to-all-start.2 = ((bf16[32,64,128]{2,1,0:T(8,128)(2,1)}), bf16[32,64,128]{2,1,0:T(8,128)(2,1)S(1)}, u32[]{:S(2)}, u32[]{:S(2)}) async-start(bf16[32,64,128]{2,1,0:T(8,128)(2,1)} %bitcast.11), calls=%async_computation.2 | async-start | bytes 1048576 | tf_op jit(solution)/shard_map/all_to_all | solution.py:378

commit v9 on v8

--- a/solution.py
+++ b/solution.py
@@ -199,19 +199,20 @@
         for ky in range(KY):
             hi, lo = halves(y_ref[pl.ds(p * KY + ky, SEGS, stride=D), :])
             sums = jnp.dot(member, jnp.concatenate([hi, lo], axis=0), preferred_element_type=f32)
-            out_ref[zl * D + 2 * ky + p, B_NUM:B_ROWS] = sums.astype(bf16)
+            out_ref[(2 * (ky % 4) + p) * 4 + 2 * zl + ky // 4, B_NUM:B_ROWS] = sums.astype(bf16)
 
     total = jnp.sum(flat[2 * SHIFTS : 3 * SHIFTS], axis=0, keepdims=True)
     total_hi = jnp.floor(total * (1.0 / 32))
     facts = jnp.where(sub == 5, total_hi, jnp.where(sub == 6, total - 32.0 * total_hi, flat[96:104]))
     facts = jnp.concatenate([facts, jnp.zeros((CLASSES - META, COLS), f32)], axis=0).astype(bf16)
     for q in range(D):
-        out_ref[(1 - zl) * D + q, B_NUM:B_ROWS] = facts
+        out_ref[(q // 2) * 4 + 2 * (1 - zl) + q % 2, B_NUM:B_ROWS] = facts
     for half in range(2):
         refs = [recv_ref[2 * x + zl, A_REF + half * D : A_REF + (half + 1) * D] for x in range(NX)]
-        for q in range(half, NB, 2):
-            for x in range(NX):
-                out_ref[q, x * D : (x + 1) * D] = refs[x]
+        for q in range(NB):
+            if (q // 4) % 2 == half:
+                for x in range(NX):
+                    out_ref[q, x * D : (x + 1) * D] = refs[x]
 
 
 def front(place, recv):
@@ -306,7 +307,7 @@
 
     def widen(q, carry):
         for x in range(NX):
-            base = pl.multiple_of((x * NB + q) * D, D)
+            base = pl.multiple_of((x * NB + (q % 4) * (NB // 4) + q // 4) * D, D)
             wide_ref[pl.ds(base, D), :] = panel_ref[q, x * D : (x + 1) * D, :].astype(f32)
         return carry
 
@@ -325,7 +326,7 @@
         for i in range(SEG):
             for r in range(NROW):
                 made_ref[j, r, i] = res[i * SHIFTS + r * 8 : i * SHIFTS + (r + 1) * 8, :].astype(out_ref.dtype)
-        done.append(pltpu.make_async_copy(made_ref.at[j], out_ref.at[j], out_sems.at[j]))
+        done.append(pltpu.make_async_copy(made_ref.at[j], out_ref.at[:, j % 2, j // 2], out_sems.at[j]))
         done[-1].start()
     for copy in done:
         copy.wait()
@@ -338,7 +339,7 @@
         score_kernel,
         in_specs=[vmem, vmem, pl.BlockSpec(memory_space=pltpu.HBM)],
         out_specs=pl.BlockSpec(memory_space=pltpu.HBM),
-        out_shape=pltpu.HBM((NA, NROW, SEG, 8, refs), PARTIAL),
+        out_shape=pltpu.HBM((NROW, 2, NX, SEG, 8, refs), PARTIAL),
         scratch_shapes=[
             pltpu.VMEM((refs * D + D, COLS), f32),
             pltpu.VMEM((D * COLS, refs), bf16),
@@ -372,19 +373,20 @@
     send = pack(images, defocus, references, offsets, posterior, class_ids, seg_count)
     recv = lax.all_to_all(send, ("x", "zl"), 0, 0, tiled=True)
     sent, meta, gx = front(place, recv)
-    panel = lax.all_to_all(sent, ("yh", "zh", "zl"), 0, 0, tiled=True)
+    panel = lax.all_to_all(sent, ("zh", "zl", "yh"), 0, 0, tiled=True)
     near, far = align(place, gx, meta)
     partial = score(panel, near, far)
     partial = lax.all_to_all(
-        partial.reshape(NA * NROW, SEG * 8, COLS), ("x", "zl", *ROW), 0, 0, tiled=True
+        partial.reshape(NA * NROW, SEG * 8, COLS), (*ROW, "zl", "x"), 0, 0, tiled=True
     )
     scores = jnp.sum(partial.astype(f32), axis=0).reshape(SEG, 8, COLS)
 
     owner = lax.axis_index("yh") // 2
-    rest = panel[:, B_NUM:B_ROWS].reshape(NB // 2, 2, CLASSES, COLS)
+    rest = panel[:, B_NUM:B_ROWS].reshape(NB // 8, 2, 4, CLASSES, COLS)
     numer = jnp.where(owner == 0, rest[:, 0], rest[:, 1]).astype(f32)
-    numer = jnp.sum(numer, axis=0)
-    facts = jnp.where(owner == 0, rest[:, 1, :, :SEGS], rest[:, 0, :, :SEGS]).astype(f32)
+    numer = jnp.sum(numer, axis=(0, 1))
+    facts = jnp.where(owner == 0, rest[:, 1, :, :, :SEGS], rest[:, 0, :, :, :SEGS]).astype(f32)
+    facts = facts.reshape(NB // 2, CLASSES, SEGS)
     all_defocus = (facts[:, 0] + facts[:, 1] + facts[:, 2]).reshape(-1)
     all_class = facts[:, 3].reshape(-1)
     all_total = ((facts[:, 5] * 32.0 + facts[:, 6]) * (1.0 / 256)).reshape(-1)

time: 79.7 us -> 80.3 us (level)
  starting transfers between devices: 28.6 us -> 29.5 us
    all_to_all x2, starting transfers between devices: 22 us -> 22.8 us  [the longest x1 15.4 us: per_device(): panel = lax.all_to_all(sent, ('zh', 'zl', 'yh'), 0, 0, tiled=True)]
where the time goes in v9:
time: 80.3 us; the launch traced here: 79.9 us
  starting transfers between devices  29.5 us (37%)
  Pallas kernels  23.9 us (30%)
  waiting for transfers between devices  21.2 us (26%)
  matrix products  2.82 us (4%)
  between operations  1.41 us (2%)
  other arithmetic  0.93 us (1%)
    all_to_all x1, starting transfers between devices, per_device(): panel = lax.all_to_all(sent, ('zh', 'zl', 'yh'), 0, 0, tiled=True)  15.4 us
    pallas_call x1, Pallas kernels, align(): pl.pallas_call(align_kernel, grid=(NA,), in_specs=[pl.BlockSpec(memory_sp...  13.4 us
    all_to_all x1, waiting for transfers between devices, per_device(): lax.all_to_all(partial.reshape(NA * NROW, SEG * 8, COLS), (*ROW, 'zl', 'x...  7.62 us
    all_to_all x1, starting transfers between devices, per_device(): lax.all_to_all(partial.reshape(NA * NROW, SEG * 8, COLS), (*ROW, 'zl', 'x...  7.39 us
    all_to_all x1, waiting for transfers between devices, per_device(): panel = lax.all_to_all(sent, ('zh', 'zl', 'yh'), 0, 0, tiled=True)  7.04 us
    all_to_all x1, starting transfers between devices, per_device(): recv = lax.all_to_all(send, ('x', 'zl'), 0, 0, tiled=True)  6.67 us
    all_to_all x1, waiting for transfers between devices, per_device(): recv = lax.all_to_all(send, ('x', 'zl'), 0, 0, tiled=True)  6.5 us
    pallas_call x1, Pallas kernels, score(): pl.pallas_call(score_kernel, in_specs=[vmem, vmem, pl.BlockSpec(memory_sp...  4.61 us
  transfers between devices with their start and end apart: 3, of which 3 were waited for; matrix products, arithmetic and copies ran while one was open for 4% of the time, Pallas kernels for 17%

profile of v9, /device:TPU:1, one launch (start us, length us, event | category | flops | bytes accessed | tf_op | source)
XLA Modules:
  0.0 79.9 jit_solution(9131524337184105661)
XLA Ops:
  1.3 1.8 %pack.1 = bf16[8,168,128]{2,1,0:T(8,128)(2,1)} custom-call(s32[1]{0:T(128)S(6)} %copy.9.refs_0_, f32[8]{0:T(128)} %refs_1_.1, s32[8]{0:T(128)} %refs_2_.1, bf16[8,2,64,128]{3,2,1,0:T(8,128)(2,1)} %refs_3_.1, bf16[1,2,64,128]{3,2,1,0:T(8,128)(2,1)} %refs_4_.1, s32[8,2,32]{2,1,0:T(2,128)} %bitcast.13, s32[8,32]{1,0:T(8,128)} %refs_6_.1), custom_call_target="tpu_custom_call" | custom-call | flops 100000 | bytes 700000 | tf_op jit(solution)/shard_map/pack/pallas_call | solution.py:118
  3.1 6.7 %all-to-all-start = ((bf16[8,168,128]{2,1,0:T(8,128)(2,1)}), bf16[8,168,128]{2,1,0:T(8,128)(2,1)S(1)}, u32[]{:S(2)}, u32[]{:S(2)}) async-start(bf16[8,168,128]{2,1,0:T(8,128)(2,1)} %pack.1), calls=%async_computation | async-start | bytes 688128 | tf_op jit(solution)/shard_map/all_to_all | solution.py:374
  9.8 0.1 pad_add_fusion.place_ref
  9.8 6.5 %all-to-all-done.recv_ref = bf16[8,168,128]{2,1,0:T(8,128)(2,1)S(1)} async-done(((bf16[8,168,128]{2,1,0:T(8,128)(2,1)}), bf16[8,168,128]{2,1,0:T(8,128)(2,1)S(1)}, u32[]{:S(2)}, u32[]{:S(2)}) %all-to-all-start) | async-done | bytes 344096 | tf_op jit(solution)/shard_map/all_to_all | solution.py:374
  16.3 4.1 %front.1 = (bf16[32,80,128]{2,1,0:T(8,128)(2,1)}, f32[64,128]{1,0:T(8,128)S(1)}, f32[1024,128]{1,0:T(8,128)S(1)}) custom-call(s32[2]{0:T(128)S(1)} %pad_add_fusion.place_ref, bf16[8,168,128]{2,1,0:T(8,128)(2,1)S(1)} %all-to-all-done.recv_ref), custom_call_target="tpu_custom_call" | custom-call | flops 100000000 | bytes 2000000 | tf_op jit(solution)/shard_map/front/pallas_call | solution.py:220
  20.4 15.4 %all-to-all-start.1 = ((bf16[32,80,128]{2,1,0:T(8,128)(2,1)}), bf16[32,80,128]{2,1,0:T(8,128)(2,1)S(1)}, u32[]{:S(2)}, u32[]{:S(2)}) async-start(bf16[32,80,128]{2,1,0:T(8,128)(2,1)} %get-tuple-element.7), calls=%async_computation.1 | async-start | bytes 1310720 | tf_op jit(solution)/shard_map/all_to_all | solution.py:376
  35.9 13.4 %align.1 = (bf16[512,2048]{1,0:T(8,128)(2,1)S(1)}, bf16[1536,2048]{1,0:T(8,128)(2,1)}) custom-call(s32[2]{0:T(128)S(1)} %pad_add_fusion.place_ref, f32[1024,128]{1,0:T(8,128)S(1)} %get-tuple-element.8.gx_ref, f32[64,128]{1,0:T(8,128)S(1)} %get-tuple-element.9.meta_ref), custom_call_target="tpu_custom_call" | custom-call | flops 600000000 | bytes 9000000 | tf_op jit(solution)/shard_map/align/pallas_call | solution.py:274
  49.3 7.0 %all-to-all-done.1.panel_ref = bf16[32,80,128]{2,1,0:T(8,128)(2,1)S(1)} async-done(((bf16[32,80,128]{2,1,0:T(8,128)(2,1)}), bf16[32,80,128]{2,1,0:T(8,128)(2,1)S(1)}, u32[]{:S(2)}, u32[]{:S(2)}) %all-to-all-start.1) | async-done | bytes 655392 | tf_op jit(solution)/shard_map/all_to_all | solution.py:376
  56.4 4.6 %score.1 = bf16[4,2,4,8,8,128]{5,4,3,2,1,0:T(8,128)(2,1)} custom-call(bf16[32,80,128]{2,1,0:T(8,128)(2,1)S(1)} %all-to-all-done.1.panel_ref, bf16[512,2048]{1,0:T(8,128)(2,1)S(1)} %get-tuple-element.10.near_ref, bf16[1536,2048]{1,0:T(8,128)(2,1)} %get-tuple-element.11.far_ref), custom_call_target="tpu_custom_call" | custom-call | flops 1100000000 | bytes 10000000 | tf_op jit(solution)/shard_map/score/pallas_call | solution.py:338
  61.0 7.4 %all-to-all-start.2 = ((bf16[32,64,128]{2,1,0:T(8,128)(2,1)}), bf16[32,64,128]{2,1,0:T(8,128)(2,1)S(1)}, u32[]{:S(2)}, u32[]{:S(2)}) async-start(bf16[32,64,128]{2,1,0:T(8,128)(2,1)} %bitcast.9), calls=%async_computation.2 | async-start | bytes 1048576 | tf_op jit(solution)/shard_map/all_to_all | solution.py:379
  68.5 0.1 slice_reduce_fusion
  68.6 0.1 mul.101
  68.6 0.1 mul.98
  68.7 0.1 eq.23
  68.8 2.8 %fusion.1 = f32[16,128]{1,0:T(8,128)} fusion(f32[16,128]{1,0:T(8,128)S(1)} %convert_reduce_fusion.1, f32[128]{0:T(128)S(1)} %convert_multiply_fusion, f32[1024]{0:T(1024)S(1)} %mul.101, f32[1024]{0:T(1024)S(1)} %mul.98, f32[1024]{0:T(1024)S(1)} %eq.23), kind=kOutput, calls=%fused_computation.2 | convolution fusion | flops 25595904 | bytes 29184 | tf_op jit(solution)/shard_map/dot_general | solution.py:396
  71.6 7.6 %all-to-all-done.2 = bf16[32,64,128]{2,1,0:T(8,128)(2,1)S(1)} async-done(((bf16[32,64,128]{2,1,0:T(8,128)(2,1)}), bf16[32,64,128]{2,1,0:T(8,128)(2,1)S(1)}, u32[]{:S(2)}, u32[]{:S(2)}) %all-to-all-start.2) | async-done | bytes 524320 | tf_op jit(solution)/shard_map/all_to_all | solution.py:379
  79.3 0.7 convert_reduce_fusion
  (5 shorter events, 0.1 us)
Async XLA Ops:
  3.1 13.2 %all-to-all-start = ((bf16[8,168,128]{2,1,0:T(8,128)(2,1)}), bf16[8,168,128]{2,1,0:T(8,128)(2,1)S(1)}, u32[]{:S(2)}, u32[]{:S(2)}) async-start(bf16[8,168,128]{2,1,0:T(8,128)(2,1)} %pack.1), calls=%async_computation | async-start | bytes 688128 | tf_op jit(solution)/shard_map/all_to_all | solution.py:374
  20.4 36.0 %all-to-all-start.1 = ((bf16[32,80,128]{2,1,0:T(8,128)(2,1)}), bf16[32,80,128]{2,1,0:T(8,128)(2,1)S(1)}, u32[]{:S(2)}, u32[]{:S(2)}) async-start(bf16[32,80,128]{2,1,0:T(8,128)(2,1)} %get-tuple-element.7), calls=%async_computation.1 | async-start | bytes 1310720 | tf_op jit(solution)/shard_map/all_to_all | solution.py:376
  61.0 18.3 %all-to-all-start.2 = ((bf16[32,64,128]{2,1,0:T(8,128)(2,1)}), bf16[32,64,128]{2,1,0:T(8,128)(2,1)S(1)}, u32[]{:S(2)}, u32[]{:S(2)}) async-start(bf16[32,64,128]{2,1,0:T(8,128)(2,1)} %bitcast.9), calls=%async_computation.2 | async-start | bytes 1048576 | tf_op jit(solution)/shard_map/all_to_all | solution.py:379

commit v10 on v8

--- a/solution.py
+++ b/solution.py
@@ -76,11 +76,12 @@
 
 
 def pack_kernel(*refs):
-    count_ref, given, out_ref, held, meta_ref, sems = refs[0], refs[1:7], refs[7], refs[8:14], refs[14], refs[15]
+    count_ref, given, out_hbm, held = refs[0], refs[1:7], refs[7], refs[8:14]
+    meta_ref, out_ref, sems, out_sems = refs[14:18]
     copies = [pltpu.make_async_copy(src, dst, sems.at[k]) for k, (src, dst) in enumerate(zip(given, held))]
     for copy in copies:
         copy.start()
-    for copy in copies:
+    for copy in copies[:2] + copies[4:]:
         copy.wait()
     defocus_ref, class_ref, img_ref, ref_ref, off_ref, post_ref = held
     sub = lax.broadcasted_iota(jnp.int32, (META, COLS), 0)
@@ -101,6 +102,9 @@
         meta_ref[i : i + 1, SHIFTS : 2 * SHIFTS] = both[1:2]
     meta_ref[0:SEG, 2 * SHIFTS : 3 * SHIFTS] = post_ref[...].astype(f32) * live[0:SEG, 0:SHIFTS]
     meta = meta_ref[...].astype(bf16)
+    copies[2].wait()
+    copies[3].wait()
+    done = []
     for j in range(NA):
         for p in range(2):
             for i in range(SEG):
@@ -110,6 +114,10 @@
                 first = (j // 2) * 2 * KY + half * KY
                 out_ref[j, base : base + KY] = ref_ref[0, p, first : first + KY]
         out_ref[j, A_META:A_ROWS] = meta
+        done.append(pltpu.make_async_copy(out_ref.at[j], out_hbm.at[j], out_sems.at[j]))
+        done[-1].start()
+    for copy in done:
+        copy.wait()
 
 
 def pack(images, defocus, references, offsets, posterior, class_ids, seg_count):
@@ -118,10 +126,10 @@
     return pl.pallas_call(
         pack_kernel,
         in_specs=[pl.BlockSpec(memory_space=pltpu.SMEM)] + [pl.BlockSpec(memory_space=pltpu.HBM)] * 6,
-        out_specs=pl.BlockSpec(memory_space=pltpu.VMEM),
-        out_shape=jax.ShapeDtypeStruct((NA, A_ROWS, COLS), bf16),
+        out_specs=pl.BlockSpec(memory_space=pltpu.HBM),
+        out_shape=pltpu.HBM((NA, A_ROWS, COLS), bf16),
         scratch_shapes=[place(v.shape, v.dtype) for place, v in zip(places, given)]
-        + [pltpu.VMEM((META, COLS), f32), pltpu.SemaphoreType.DMA((6,))],
+        + [pltpu.VMEM((META, COLS), f32), pltpu.VMEM((NA, A_ROWS, COLS), bf16), pltpu.SemaphoreType.DMA((6,)), pltpu.SemaphoreType.DMA((NA,))],
         compiler_params=pltpu.CompilerParams(vmem_limit_bytes=4 << 20),
         cost_estimate=pl.CostEstimate(flops=100_000, bytes_accessed=700_000, transcendentals=0),
         name="pack",

time: 79.7 us -> 79.7 us (level)
  no operation moved by 1% of the time
where the time goes in v10:
time: 79.7 us; the launch traced here: 79.3 us
  starting transfers between devices  28.6 us (36%)
  Pallas kernels  23.8 us (30%)
  waiting for transfers between devices  21.5 us (27%)
  matrix products  2.83 us (4%)
  between operations  1.4 us (2%)
  other arithmetic  0.92 us (1%)
    all_to_all x1, starting transfers between devices, per_device(): panel = lax.all_to_all(sent, ('yh', 'zh', 'zl'), 0, 0, tiled=True)  15.4 us
    pallas_call x1, Pallas kernels, align(): pl.pallas_call(align_kernel, grid=(NA,), in_specs=[pl.BlockSpec(memory_sp...  13.4 us
    all_to_all x1, waiting for transfers between devices, per_device(): lax.all_to_all(partial.reshape(NA * NROW, SEG * 8, COLS), ('x', 'zl', *RO...  7.86 us
    all_to_all x1, waiting for transfers between devices, per_device(): panel = lax.all_to_all(sent, ('yh', 'zh', 'zl'), 0, 0, tiled=True)  7.1 us
    all_to_all x1, starting transfers between devices, per_device(): recv = lax.all_to_all(send, ('x', 'zl'), 0, 0, tiled=True)  6.67 us
    all_to_all x1, starting transfers between devices, per_device(): lax.all_to_all(partial.reshape(NA * NROW, SEG * 8, COLS), ('x', 'zl', *RO...  6.52 us
    all_to_all x1, waiting for transfers between devices, per_device(): recv = lax.all_to_all(send, ('x', 'zl'), 0, 0, tiled=True)  6.5 us
    pallas_call x1, Pallas kernels, score(): pl.pallas_call(score_kernel, in_specs=[vmem, vmem, pl.BlockSpec(memory_sp...  4.52 us
  transfers between devices with their start and end apart: 3, of which 3 were waited for; matrix products, arithmetic and copies ran while one was open for 4% of the time, Pallas kernels for 17%

profile of v10, /device:TPU:1, one launch (start us, length us, event | category | flops | bytes accessed | tf_op | source)
XLA Modules:
  0.0 79.3 jit_solution(15011545547208719540)
XLA Ops:
  1.3 1.8 %pack.1 = bf16[8,168,128]{2,1,0:T(8,128)(2,1)} custom-call(s32[1]{0:T(128)S(6)} %copy.9.refs_0_, f32[8]{0:T(128)} %refs_1_.1, s32[8]{0:T(128)} %refs_2_.1, bf16[8,2,64,128]{3,2,1,0:T(8,128)(2,1)} %refs_3_.1, bf16[1,2,64,128]{3,2,1,0:T(8,128)(2,1)} %refs_4_.1, s32[8,2,32]{2,1,0:T(2,128)} %bitcast.15, s32[8,32]{1,0:T(8,128)} %refs_6_.1), custom_call_target="tpu_custom_call" | custom-call | flops 100000 | bytes 700000 | tf_op jit(solution)/shard_map/pack/pallas_call | solution.py:126
  3.1 6.7 %all-to-all-start = ((bf16[8,168,128]{2,1,0:T(8,128)(2,1)}), bf16[8,168,128]{2,1,0:T(8,128)(2,1)S(1)}, u32[]{:S(2)}, u32[]{:S(2)}) async-start(bf16[8,168,128]{2,1,0:T(8,128)(2,1)} %pack.1), calls=%async_computation | async-start | bytes 688128 | tf_op jit(solution)/shard_map/all_to_all | solution.py:381
  9.8 0.1 pad_add_fusion.place_ref
  9.8 6.5 %all-to-all-done.recv_ref = bf16[8,168,128]{2,1,0:T(8,128)(2,1)S(1)} async-done(((bf16[8,168,128]{2,1,0:T(8,128)(2,1)}), bf16[8,168,128]{2,1,0:T(8,128)(2,1)S(1)}, u32[]{:S(2)}, u32[]{:S(2)}) %all-to-all-start) | async-done | bytes 344096 | tf_op jit(solution)/shard_map/all_to_all | solution.py:381
  16.3 4.1 %front.1 = (bf16[32,80,128]{2,1,0:T(8,128)(2,1)}, f32[64,128]{1,0:T(8,128)S(1)}, f32[1024,128]{1,0:T(8,128)S(1)}) custom-call(s32[2]{0:T(128)S(1)} %pad_add_fusion.place_ref, bf16[8,168,128]{2,1,0:T(8,128)(2,1)S(1)} %all-to-all-done.recv_ref), custom_call_target="tpu_custom_call" | custom-call | flops 100000000 | bytes 2000000 | tf_op jit(solution)/shard_map/front/pallas_call | solution.py:227
  20.4 15.4 %all-to-all-start.1 = ((bf16[32,80,128]{2,1,0:T(8,128)(2,1)}), bf16[32,80,128]{2,1,0:T(8,128)(2,1)S(1)}, u32[]{:S(2)}, u32[]{:S(2)}) async-start(bf16[32,80,128]{2,1,0:T(8,128)(2,1)} %get-tuple-element.7), calls=%async_computation.1 | async-start | bytes 1310720 | tf_op jit(solution)/shard_map/all_to_all | solution.py:383
  35.9 13.4 %align.1 = (bf16[512,2048]{1,0:T(8,128)(2,1)S(1)}, bf16[1536,2048]{1,0:T(8,128)(2,1)}) custom-call(s32[2]{0:T(128)S(1)} %pad_add_fusion.place_ref, f32[1024,128]{1,0:T(8,128)S(1)} %get-tuple-element.8.gx_ref, f32[64,128]{1,0:T(8,128)S(1)} %get-tuple-element.9.meta_ref), custom_call_target="tpu_custom_call" | custom-call | flops 600000000 | bytes 9000000 | tf_op jit(solution)/shard_map/align/pallas_call | solution.py:281
  49.3 7.1 %all-to-all-done.1.panel_ref = bf16[32,80,128]{2,1,0:T(8,128)(2,1)S(1)} async-done(((bf16[32,80,128]{2,1,0:T(8,128)(2,1)}), bf16[32,80,128]{2,1,0:T(8,128)(2,1)S(1)}, u32[]{:S(2)}, u32[]{:S(2)}) %all-to-all-start.1) | async-done | bytes 655392 | tf_op jit(solution)/shard_map/all_to_all | solution.py:383
  56.4 4.5 %score.1 = bf16[8,4,8,8,128]{4,3,2,1,0:T(8,128)(2,1)} custom-call(bf16[32,80,128]{2,1,0:T(8,128)(2,1)S(1)} %all-to-all-done.1.panel_ref, bf16[512,2048]{1,0:T(8,128)(2,1)S(1)} %get-tuple-element.10.near_ref, bf16[1536,2048]{1,0:T(8,128)(2,1)} %get-tuple-element.11.far_ref), custom_call_target="tpu_custom_call" | custom-call | flops 1100000000 | bytes 10000000 | tf_op jit(solution)/shard_map/score/pallas_call | solution.py:345
  60.9 6.5 %all-to-all-start.2 = ((bf16[32,64,128]{2,1,0:T(8,128)(2,1)}), bf16[32,64,128]{2,1,0:T(8,128)(2,1)S(1)}, u32[]{:S(2)}, u32[]{:S(2)}) async-start(bf16[32,64,128]{2,1,0:T(8,128)(2,1)} %bitcast.11), calls=%async_computation.2 | async-start | bytes 1048576 | tf_op jit(solution)/shard_map/all_to_all | solution.py:386
  67.5 0.1 slice_reduce_fusion
  67.6 0.1 mul.101
  67.7 0.1 mul.98
  67.8 0.1 eq.23
  67.9 2.8 %fusion.1 = f32[16,128]{1,0:T(8,128)} fusion(f32[16,128]{1,0:T(8,128)S(1)} %convert_reduce_fusion.1, f32[128]{0:T(128)S(1)} %convert_multiply_fusion, f32[1024]{0:T(1024)S(1)} %mul.101, f32[1024]{0:T(1024)S(1)} %mul.98, f32[1024]{0:T(1024)S(1)} %eq.23), kind=kOutput, calls=%fused_computation.2 | convolution fusion | flops 25595904 | bytes 29184 | tf_op jit(solution)/shard_map/dot_general | solution.py:402
  70.7 7.9 %all-to-all-done.2 = bf16[32,64,128]{2,1,0:T(8,128)(2,1)S(1)} async-done(((bf16[32,64,128]{2,1,0:T(8,128)(2,1)}), bf16[32,64,128]{2,1,0:T(8,128)(2,1)S(1)}, u32[]{:S(2)}, u32[]{:S(2)}) %all-to-all-start.2) | async-done | bytes 524320 | tf_op jit(solution)/shard_map/all_to_all | solution.py:386
  78.6 0.7 convert_reduce_fusion
  (4 shorter events, 0.1 us)
Async XLA Ops:
  3.1 13.2 %all-to-all-start = ((bf16[8,168,128]{2,1,0:T(8,128)(2,1)}), bf16[8,168,128]{2,1,0:T(8,128)(2,1)S(1)}, u32[]{:S(2)}, u32[]{:S(2)}) async-start(bf16[8,168,128]{2,1,0:T(8,128)(2,1)} %pack.1), calls=%async_computation | async-start | bytes 688128 | tf_op jit(solution)/shard_map/all_to_all | solution.py:381
  20.4 36.0 %all-to-all-start.1 = ((bf16[32,80,128]{2,1,0:T(8,128)(2,1)}), bf16[32,80,128]{2,1,0:T(8,128)(2,1)S(1)}, u32[]{:S(2)}, u32[]{:S(2)}) async-start(bf16[32,80,128]{2,1,0:T(8,128)(2,1)} %get-tuple-element.7), calls=%async_computation.1 | async-start | bytes 1310720 | tf_op jit(solution)/shard_map/all_to_all | solution.py:383
  60.9 17.7 %all-to-all-start.2 = ((bf16[32,64,128]{2,1,0:T(8,128)(2,1)}), bf16[32,64,128]{2,1,0:T(8,128)(2,1)S(1)}, u32[]{:S(2)}, u32[]{:S(2)}) async-start(bf16[32,64,128]{2,1,0:T(8,128)(2,1)} %bitcast.11), calls=%async_computation.2 | async-start | bytes 1048576 | tf_op jit(solution)/shard_map/all_to_all | solution.py:386

commit v11 on v10

--- a/solution.py
+++ b/solution.py
@@ -178,27 +178,34 @@
             hot.append((jnp.broadcast_to(sx, (SHIFTS, SHIFTS)) == (lane_s[:, :SHIFTS] - 8).astype(f32)).astype(f32).astype(bf16))
         col_ref[...] = jnp.dot(jnp.concatenate(hot, axis=0), table, preferred_element_type=f32).astype(bf16)
 
-        for i in range(SEG):
-            c, s = turn(jnp.broadcast_to(sy[i : i + 1], (KY, COLS)) * kw)
-            wi = jnp.broadcast_to(w[i : i + 1], (KY, COLS))
-            c, s = c * wi, s * wi
-            left = jnp.concatenate([jnp.where(first, c, -s), jnp.where(first, s, c)], axis=0)
-            hi, lo = halves(left)
-            right = jnp.concatenate(
-                [col_ref[i * SHIFTS : (i + 1) * SHIFTS, q * COLS : (q + 1) * COLS] for q in range(4)], axis=0
+        for pair in range(0, SEG, 2):
+            lefts, rights = [], []
+            for i in (pair, pair + 1):
+                c, s = turn(jnp.broadcast_to(sy[i : i + 1], (KY, COLS)) * kw)
+                wi = jnp.broadcast_to(w[i : i + 1], (KY, COLS))
+                c, s = c * wi, s * wi
+                left = jnp.concatenate([jnp.where(first, c, -s), jnp.where(first, s, c)], axis=0)
+                lefts += halves(left)
+                rights.append(jnp.concatenate(
+                    [col_ref[i * SHIFTS : (i + 1) * SHIFTS, q * COLS : (q + 1) * COLS] for q in range(4)], axis=0
+                ))
+            product = jnp.dot(
+                jnp.concatenate(lefts, axis=0), jnp.concatenate(rights, axis=1), preferred_element_type=f32
             )
-            both = jnp.dot(jnp.concatenate([hi, lo], axis=0), right, preferred_element_type=f32)
-            q_re = both[0:KY] + both[D : D + KY]
-            q_im = both[KY:D] + both[D + KY : 2 * D]
-            arg = (200.0 * jnp.broadcast_to(defocus[i : i + 1], (KY, COLS))) * radius + 0.1
-            gain = -sine(arg) * jnp.broadcast_to(alive[i : i + 1], (KY, COLS))
-            img = recv_ref[a, i * D : (i + 1) * D].astype(f32)
-            xr, xi = img[0:KY] * gain, img[KY:D] * gain
-            at = (a * SEG + i) * D
-            gx_ref[at : at + KY] = xr
-            gx_ref[at + KY : at + D] = xi
-            y_ref[at : at + KY] = xr * q_re - xi * q_im
-            y_ref[at + KY : at + D] = xr * q_im + xi * q_re
+            for k in range(2):
+                i = pair + k
+                both = product[k * 2 * D : (k + 1) * 2 * D, k * COLS : (k + 1) * COLS]
+                q_re = both[0:KY] + both[D : D + KY]
+                q_im = both[KY:D] + both[D + KY : 2 * D]
+                arg = (200.0 * jnp.broadcast_to(defocus[i : i + 1], (KY, COLS))) * radius + 0.1
+                gain = -sine(arg) * jnp.broadcast_to(alive[i : i + 1], (KY, COLS))
+                img = recv_ref[a, i * D : (i + 1) * D].astype(f32)
+                xr, xi = img[0:KY] * gain, img[KY:D] * gain
+                at = (a * SEG + i) * D
+                gx_ref[at : at + KY] = xr
+                gx_ref[at + KY : at + D] = xi
+                y_ref[at : at + KY] = xr * q_re - xi * q_im
+                y_ref[at + KY : at + D] = xr * q_im + xi * q_re
 
     flat = wide_ref[...].T
     ids = jnp.broadcast_to(flat[99:100], (CLASSES, COLS))

time: 79.7 us -> 79.6 us (level)
  no operation moved by 1% of the time
where the time goes in v11:
time: 79.6 us; the launch traced here: 79.2 us
  starting transfers between devices  28.6 us (36%)
  Pallas kernels  23.7 us (30%)
  waiting for transfers between devices  21.5 us (27%)
  matrix products  2.83 us (4%)
  between operations  1.4 us (2%)
  other arithmetic  0.92 us (1%)
    all_to_all x1, starting transfers between devices, per_device(): panel = lax.all_to_all(sent, ('yh', 'zh', 'zl'), 0, 0, tiled=True)  15.4 us
    pallas_call x1, Pallas kernels, align(): pl.pallas_call(align_kernel, grid=(NA,), in_specs=[pl.BlockSpec(memory_sp...  13.4 us
    all_to_all x1, waiting for transfers between devices, per_device(): lax.all_to_all(partial.reshape(NA * NROW, SEG * 8, COLS), ('x', 'zl', *RO...  7.86 us
    all_to_all x1, waiting for transfers between devices, per_device(): panel = lax.all_to_all(sent, ('yh', 'zh', 'zl'), 0, 0, tiled=True)  7.11 us
    all_to_all x1, starting transfers between devices, per_device(): recv = lax.all_to_all(send, ('x', 'zl'), 0, 0, tiled=True)  6.67 us
    all_to_all x1, starting transfers between devices, per_device(): lax.all_to_all(partial.reshape(NA * NROW, SEG * 8, COLS), ('x', 'zl', *RO...  6.51 us
    all_to_all x1, waiting for transfers between devices, per_device(): recv = lax.all_to_all(send, ('x', 'zl'), 0, 0, tiled=True)  6.5 us
    pallas_call x1, Pallas kernels, score(): pl.pallas_call(score_kernel, in_specs=[vmem, vmem, pl.BlockSpec(memory_sp...  4.52 us
  transfers between devices with their start and end apart: 3, of which 3 were waited for; matrix products, arithmetic and copies ran while one was open for 4% of the time, Pallas kernels for 17%

profile of v11, /device:TPU:1, one launch (start us, length us, event | category | flops | bytes accessed | tf_op | source)
XLA Modules:
  0.0 79.2 jit_solution(13049852118588642474)
XLA Ops:
  1.3 1.8 %pack.1 = bf16[8,168,128]{2,1,0:T(8,128)(2,1)} custom-call(s32[1]{0:T(128)S(6)} %copy.9.refs_0_, f32[8]{0:T(128)} %refs_1_.1, s32[8]{0:T(128)} %refs_2_.1, bf16[8,2,64,128]{3,2,1,0:T(8,128)(2,1)} %refs_3_.1, bf16[1,2,64,128]{3,2,1,0:T(8,128)(2,1)} %refs_4_.1, s32[8,2,32]{2,1,0:T(2,128)} %bitcast.15, s32[8,32]{1,0:T(8,128)} %refs_6_.1), custom_call_target="tpu_custom_call" | custom-call | flops 100000 | bytes 700000 | tf_op jit(solution)/shard_map/pack/pallas_call | solution.py:126
  3.1 6.7 %all-to-all-start = ((bf16[8,168,128]{2,1,0:T(8,128)(2,1)}), bf16[8,168,128]{2,1,0:T(8,128)(2,1)S(1)}, u32[]{:S(2)}, u32[]{:S(2)}) async-start(bf16[8,168,128]{2,1,0:T(8,128)(2,1)} %pack.1), calls=%async_computation | async-start | bytes 688128 | tf_op jit(solution)/shard_map/all_to_all | solution.py:388
  9.8 0.1 pad_add_fusion.place_ref
  9.8 6.5 %all-to-all-done.recv_ref = bf16[8,168,128]{2,1,0:T(8,128)(2,1)S(1)} async-done(((bf16[8,168,128]{2,1,0:T(8,128)(2,1)}), bf16[8,168,128]{2,1,0:T(8,128)(2,1)S(1)}, u32[]{:S(2)}, u32[]{:S(2)}) %all-to-all-start) | async-done | bytes 344096 | tf_op jit(solution)/shard_map/all_to_all | solution.py:388
  16.3 4.0 %front.1 = (bf16[32,80,128]{2,1,0:T(8,128)(2,1)}, f32[64,128]{1,0:T(8,128)S(1)}, f32[1024,128]{1,0:T(8,128)S(1)}) custom-call(s32[2]{0:T(128)S(1)} %pad_add_fusion.place_ref, bf16[8,168,128]{2,1,0:T(8,128)(2,1)S(1)} %all-to-all-done.recv_ref), custom_call_target="tpu_custom_call" | custom-call | flops 100000000 | bytes 2000000 | tf_op jit(solution)/shard_map/front/pallas_call | solution.py:234
  20.3 15.4 %all-to-all-start.1 = ((bf16[32,80,128]{2,1,0:T(8,128)(2,1)}), bf16[32,80,128]{2,1,0:T(8,128)(2,1)S(1)}, u32[]{:S(2)}, u32[]{:S(2)}) async-start(bf16[32,80,128]{2,1,0:T(8,128)(2,1)} %get-tuple-element.7), calls=%async_computation.1 | async-start | bytes 1310720 | tf_op jit(solution)/shard_map/all_to_all | solution.py:390
  35.8 13.4 %align.1 = (bf16[512,2048]{1,0:T(8,128)(2,1)S(1)}, bf16[1536,2048]{1,0:T(8,128)(2,1)}) custom-call(s32[2]{0:T(128)S(1)} %pad_add_fusion.place_ref, f32[1024,128]{1,0:T(8,128)S(1)} %get-tuple-element.8.gx_ref, f32[64,128]{1,0:T(8,128)S(1)} %get-tuple-element.9.meta_ref), custom_call_target="tpu_custom_call" | custom-call | flops 600000000 | bytes 9000000 | tf_op jit(solution)/shard_map/align/pallas_call | solution.py:288
  49.2 7.1 %all-to-all-done.1.panel_ref = bf16[32,80,128]{2,1,0:T(8,128)(2,1)S(1)} async-done(((bf16[32,80,128]{2,1,0:T(8,128)(2,1)}), bf16[32,80,128]{2,1,0:T(8,128)(2,1)S(1)}, u32[]{:S(2)}, u32[]{:S(2)}) %all-to-all-start.1) | async-done | bytes 655392 | tf_op jit(solution)/shard_map/all_to_all | solution.py:390
  56.3 4.5 %score.1 = bf16[8,4,8,8,128]{4,3,2,1,0:T(8,128)(2,1)} custom-call(bf16[32,80,128]{2,1,0:T(8,128)(2,1)S(1)} %all-to-all-done.1.panel_ref, bf16[512,2048]{1,0:T(8,128)(2,1)S(1)} %get-tuple-element.10.near_ref, bf16[1536,2048]{1,0:T(8,128)(2,1)} %get-tuple-element.11.far_ref), custom_call_target="tpu_custom_call" | custom-call | flops 1100000000 | bytes 10000000 | tf_op jit(solution)/shard_map/score/pallas_call | solution.py:352
  60.8 6.5 %all-to-all-start.2 = ((bf16[32,64,128]{2,1,0:T(8,128)(2,1)}), bf16[32,64,128]{2,1,0:T(8,128)(2,1)S(1)}, u32[]{:S(2)}, u32[]{:S(2)}) async-start(bf16[32,64,128]{2,1,0:T(8,128)(2,1)} %bitcast.11), calls=%async_computation.2 | async-start | bytes 1048576 | tf_op jit(solution)/shard_map/all_to_all | solution.py:393
  67.5 0.1 slice_reduce_fusion
  67.6 0.1 mul.101
  67.6 0.1 mul.98
  67.7 0.1 eq.23
  67.8 2.8 %fusion.1 = f32[16,128]{1,0:T(8,128)} fusion(f32[16,128]{1,0:T(8,128)S(1)} %convert_reduce_fusion.1, f32[128]{0:T(128)S(1)} %convert_multiply_fusion, f32[1024]{0:T(1024)S(1)} %mul.101, f32[1024]{0:T(1024)S(1)} %mul.98, f32[1024]{0:T(1024)S(1)} %eq.23), kind=kOutput, calls=%fused_computation.2 | convolution fusion | flops 25595904 | bytes 29184 | tf_op jit(solution)/shard_map/dot_general | solution.py:409
  70.6 7.9 %all-to-all-done.2 = bf16[32,64,128]{2,1,0:T(8,128)(2,1)S(1)} async-done(((bf16[32,64,128]{2,1,0:T(8,128)(2,1)}), bf16[32,64,128]{2,1,0:T(8,128)(2,1)S(1)}, u32[]{:S(2)}, u32[]{:S(2)}) %all-to-all-start.2) | async-done | bytes 524320 | tf_op jit(solution)/shard_map/all_to_all | solution.py:393
  78.5 0.7 convert_reduce_fusion
  (4 shorter events, 0.1 us)
Async XLA Ops:
  3.1 13.2 %all-to-all-start = ((bf16[8,168,128]{2,1,0:T(8,128)(2,1)}), bf16[8,168,128]{2,1,0:T(8,128)(2,1)S(1)}, u32[]{:S(2)}, u32[]{:S(2)}) async-start(bf16[8,168,128]{2,1,0:T(8,128)(2,1)} %pack.1), calls=%async_computation | async-start | bytes 688128 | tf_op jit(solution)/shard_map/all_to_all | solution.py:388
  20.3 36.0 %all-to-all-start.1 = ((bf16[32,80,128]{2,1,0:T(8,128)(2,1)}), bf16[32,80,128]{2,1,0:T(8,128)(2,1)S(1)}, u32[]{:S(2)}, u32[]{:S(2)}) async-start(bf16[32,80,128]{2,1,0:T(8,128)(2,1)} %get-tuple-element.7), calls=%async_computation.1 | async-start | bytes 1310720 | tf_op jit(solution)/shard_map/all_to_all | solution.py:390
  60.8 17.7 %all-to-all-start.2 = ((bf16[32,64,128]{2,1,0:T(8,128)(2,1)}), bf16[32,64,128]{2,1,0:T(8,128)(2,1)S(1)}, u32[]{:S(2)}, u32[]{:S(2)}) async-start(bf16[32,64,128]{2,1,0:T(8,128)(2,1)} %bitcast.11), calls=%async_computation.2 | async-start | bytes 1048576 | tf_op jit(solution)/shard_map/all_to_all | solution.py:393
